TPU v7x, 256 devices: a whole 4x4x8 slice. The times are simulated.
256 devices in a mesh: row: 32 (over x, z), col: 8 (over y, core).
Axes of the slice: x: 4, y: 4, z: 8, core: 2. Of those that a mesh axis runs over, the one named last changes fastest.
Arguments:
- incident: float32 [2, 36, 32768], P(None, None, 'row'), may hold values from -24 to 24
- diagonal: float32 [32768], P('row'), may hold values from 1 to 2
- near_blocks: bfloat16 [32, 8, 2, 1024, 1024], P('row', None, None, None, 'col'), may hold values from -0.046875 to 0.046875
- left_factors: bfloat16 [32, 32, 2, 64, 1024], P('row', 'col'), may hold values from -0.0390625 to 0.0390625
- right_factors: bfloat16 [32, 32, 2, 64, 1024], P('row', 'col'), may hold values from -0.1875 to 0.1875
- flags: int32 [32, 8], P('row'), may hold values from 0 to 1, as said below
- ranks: int32 [32, 32], P('row', 'col'), may hold values from 4 to 64
- harmonics: float32 [2, 36, 32768], P(None, None, 'row'), may hold values from -0.03125 to 0.03125
Outputs:
- solution: float32 [2, 36, 32768], P(None, None, 'row')
- coefficients: float32 [2, 36, 36], replicated
Inputs may be any that keep to these rules, and one draw needn't show every extreme that they name: `flags`: slot 8 / 2 (the pair of a cluster with itself) is always 1; the ones of a row form one run of slots around it.
All inputs are finite; a program needn't handle non-finite values.
Results may differ from a plain program's by a relative error of at most 0.0013.
Values may be sent and summed in bfloat16 or wider, within the bound.
A program may use at most 128 MiB of HBM per device.

v0:
```python
from functools import partial

import jax
import jax.numpy as jnp
from jax import lax
from jax.sharding import PartitionSpec as P

highest = lax.Precision.HIGHEST


def dense_term(vector, block):

    def product(left, right):
        return jnp.einsum("sf,ef->se", left, right, preferred_element_type=jnp.float32)

    real_out = product(vector[0], block[0]) - product(vector[1], block[1])
    imag_out = product(vector[0], block[1]) + product(vector[1], block[0])
    return jnp.stack([real_out, imag_out])


def lowrank_term(vector, left_block, right_block, rank):

    def inner(left, right):
        return jnp.einsum("sf,rf->sr", left, right, preferred_element_type=jnp.float32)

    def outer(left, right):
        return jnp.einsum("sr,re->se", left, right, preferred_element_type=jnp.float32)

    coeff_real = inner(vector[0], right_block[0]) - inner(vector[1], right_block[1])
    coeff_imag = inner(vector[0], right_block[1]) + inner(vector[1], right_block[0])
    keep = (jnp.arange(right_block.shape[1], dtype=jnp.int32) < rank)[None, None, :]
    coeffs = jnp.where(keep, jnp.stack([coeff_real, coeff_imag]), 0.0).astype(jnp.bfloat16)
    real_out = outer(coeffs[0], left_block[0]) - outer(coeffs[1], left_block[1])
    imag_out = outer(coeffs[0], left_block[1]) + outer(coeffs[1], left_block[0])
    return jnp.stack([real_out, imag_out])


def inner_products(first, second):
    return jnp.einsum("csn,ctn->st", first, second, precision=highest)


def combine_rows(matrix, vectors):
    return jnp.einsum("st,ctn->csn", matrix, vectors, precision=highest)


def matmul(left, right):
    return jnp.dot(left, right, precision=highest)


def lower_inverse(lower):
    identity = jnp.eye(lower.shape[0], dtype=lower.dtype)
    return lax.linalg.triangular_solve(lower, identity, left_side=True, lower=True)


def project(harmonics, vectors):

    def contract(left, right):
        return jnp.einsum("mn,sn->ms", left, right, precision=highest)

    real_out = contract(harmonics[0], vectors[0]) + contract(harmonics[1], vectors[1])
    imag_out = contract(harmonics[0], vectors[1]) - contract(harmonics[1], vectors[0])
    return jnp.stack([real_out, imag_out])


def body(incident, diagonal, near_blocks, left_factors, right_factors, flags, ranks, harmonics):
    blocks = left_factors.shape[1]
    slots = near_blocks.shape[1]
    width = near_blocks.shape[4]
    half_band = slots // 2
    elements = incident.shape[2]
    fields = incident.shape[1]
    clusters = lax.axis_size("row")
    row_index = lax.axis_index("row")
    column = lax.axis_index("col")
    empty = jnp.zeros((2, fields, elements), jnp.float32)

    def far_term(number, piece):
        cluster = column * blocks + number
        offset = (cluster - row_index + half_band) % clusters
        is_near = (offset < slots) & (flags[0, jnp.minimum(offset, slots - 1)] == 1)
        return lax.cond(
            is_near,
            lambda operand: empty,
            partial(
                lowrank_term,
                left_block=left_factors[0, number],
                right_block=right_factors[0, number],
                rank=ranks[0, number],
            ),
            piece,
        )

    def near_term(slot, piece):
        return lax.cond(
            flags[0, slot] == 1,
            partial(dense_term, block=near_blocks[0, slot]),
            lambda operand: empty,
            piece,
        )

    def apply_operator(vector):
        rounded = vector.astype(jnp.bfloat16)
        gathered = lax.all_gather(rounded, "row", axis=2, tiled=True)
        far_pieces = [
            lax.dynamic_slice_in_dim(gathered, (column * blocks + number) * elements, elements, 2)
            for number in range(blocks)
        ]
        near_pieces = [
            lax.dynamic_slice_in_dim(
                gathered,
                (row_index + slot - half_band) % clusters * elements + column * width,
                width,
                2,
            )
            for slot in range(slots)
        ]
        total = near_term(0, near_pieces[0])
        for slot in range(1, slots):
            total = total + near_term(slot, near_pieces[slot])
        for number in range(blocks):
            total = total + far_term(number, far_pieces[number])
        summed = lax.psum(total, "col")
        return summed + diagonal[None, None, :] * vector

    lower_first = jnp.linalg.cholesky(lax.psum(inner_products(incident, incident), "row"))
    basis_one = combine_rows(lower_inverse(lower_first), incident)
    image = apply_operator(basis_one)
    coupling_one = lax.psum(inner_products(image, basis_one), "row")
    rest = image - combine_rows(coupling_one, basis_one)
    gram_one = lax.psum(inner_products(rest, rest), "row")
    lower_second = jnp.linalg.cholesky(gram_one)
    basis_two = combine_rows(lower_inverse(lower_second), rest)
    image = apply_operator(basis_two)
    coupling_onetwo, coupling_two = lax.psum(
        (inner_products(image, basis_one), inner_products(image, basis_two)), "row"
    )
    rest = image - combine_rows(coupling_onetwo, basis_one) - combine_rows(coupling_two, basis_two)
    gram_two = lax.psum(inner_products(rest, rest), "row")
    upper_left = matmul(coupling_one, coupling_one.T) + gram_one
    upper_right = matmul(coupling_one, coupling_onetwo.T) + matmul(lower_second, coupling_two.T)
    lower_right = (
        matmul(coupling_onetwo, coupling_onetwo.T) + matmul(coupling_two, coupling_two.T) + gram_two
    )
    normal = jnp.concatenate(
        [
            jnp.concatenate([upper_left, upper_right], axis=1),
            jnp.concatenate([upper_right.T, lower_right], axis=1),
        ],
        axis=0,
    )
    target = jnp.concatenate(
        [matmul(lower_first, coupling_one.T), matmul(lower_first, coupling_onetwo.T)], axis=1
    )
    factor_inverse = lower_inverse(jnp.linalg.cholesky(normal))
    weights = matmul(factor_inverse.T, matmul(factor_inverse, target.T)).T
    first_weights = weights[:, :fields]
    second_weights = weights[:, fields:]
    solution = combine_rows(first_weights, basis_one) + combine_rows(second_weights, basis_two)
    coefficients = lax.psum(project(harmonics, solution), "row")
    return (solution, coefficients)


def solution(mesh):
    in_specs = (
        P(None, None, "row"),
        P("row"),
        P("row", None, None, None, "col"),
        P("row", "col", None, None, None),
        P("row", "col", None, None, None),
        P("row", None),
        P("row", "col"),
        P(None, None, "row"),
    )
    out_specs = (P(None, None, "row"), P())
    return jax.shard_map(body, mesh=mesh, in_specs=in_specs, out_specs=out_specs, check_vma=False)
```

profile of v0, /device:TPU:24, one launch (start us, length us, event | category | flops | bytes accessed | tf_op | source)
XLA Modules:
  0.0 1354.3 jit_solution(15684794761179191939)
XLA Ops:
  8.8 145.7 %psum.63 = f32[36,36]{0,1:T(8,128)S(1)} all-reduce(f32[36,36]{0,1:T(8,128)S(1)} %convolution_bitcast_fusion.12), channel_id=1, replica_groups=mesh['row'=32,'col'=8] {'row'}, use_global_device_ids=true, to_apply=%region_0.0 | all-reduce | flops 1296 | bytes 10368 | tf_op jit(solution)/shard_map/psum | solution.py:125
  179.7 63.7 %all-gather.3.cloned.1.call-done = bf16[2,36,32768]{2,1,0:T(8,128)(2,1)} async-done(((bf16[2,36,1024]{2,1,0:T(8,128)(2,1)}), bf16[2,36,32768]{2,1,0:T(8,128)(2,1)}) %all-gather.3.cloned.1.call-update) | async-done | bytes 4718608 | tf_op jit(solution)/shard_map/all_gather | solution.py:103
  243.4 10.3 conditional.35
  253.8 10.3 conditional.34
  264.1 10.5 conditional.33
  274.5 10.3 conditional.32
  284.9 6.4 conditional.31
  291.3 6.4 conditional.30
  297.7 4.9 conditional.29
  302.7 4.9 conditional.28
  307.5 4.8 conditional.27
  312.3 4.8 conditional.26
  317.2 4.8 conditional.24
  321.9 4.8 conditional.25
  329.9 58.6 %all-reduce.4.cloned.1.call-done = f32[2,36,1024]{2,1,0:T(8,128)} async-done(((f32[2,36,1024]{2,1,0:T(8,128)}), f32[2,36,1024]{2,1,0:T(8,128)}) %all-reduce.4.cloned.1.call-update) | async-done | bytes 294928 | tf_op jit(solution)/shard_map/psum | solution.py:122
  389.9 143.1 %psum.65 = f32[36,36]{1,0:T(8,128)S(1)} all-reduce(f32[36,36]{1,0:T(8,128)S(1)} %convolution_bitcast_fusion.10), channel_id=1, replica_groups=mesh['row'=32,'col'=8] {'row'}, use_global_device_ids=true, to_apply=%region_28.31 | all-reduce | flops 1296 | bytes 10368 | tf_op jit(solution)/shard_map/psum | solution.py:128
  535.5 137.9 %psum.66 = f32[36,36]{1,0:T(8,128)S(1)} all-reduce(f32[36,36]{1,0:T(8,128)S(1)} %convolution_bitcast_fusion.9), channel_id=1, replica_groups=mesh['row'=32,'col'=8] {'row'}, use_global_device_ids=true, to_apply=%region_29.32 | all-reduce | flops 1296 | bytes 10368 | tf_op jit(solution)/shard_map/psum | solution.py:130
  686.3 75.8 %all-gather.5.cloned.1.call-done = bf16[2,36,32768]{2,1,0:T(8,128)(2,1)} async-done(((bf16[2,36,1024]{2,1,0:T(8,128)(2,1)}), bf16[2,36,32768]{2,1,0:T(8,128)(2,1)}) %all-gather.5.cloned.1.call-update) | async-done | bytes 4718608 | tf_op jit(solution)/shard_map/all_gather | solution.py:103
  762.1 11.0 conditional.47
  773.1 10.9 conditional.46
  784.0 11.1 conditional.45
  795.1 7.3 conditional.44
  802.4 5.7 conditional.43
  808.2 5.7 conditional.42
  813.9 5.7 conditional.41
  829.1 4.9 conditional.38
  845.7 57.8 %all-reduce.6.cloned.1.call-done = f32[2,36,1024]{2,1,0:T(8,128)} async-done(((f32[2,36,1024]{2,1,0:T(8,128)}), f32[2,36,1024]{2,1,0:T(8,128)}) %all-reduce.6.cloned.1.call-update) | async-done | bytes 294928 | tf_op jit(solution)/shard_map/psum | solution.py:122
  906.3 143.1 %all-reduce = (f32[36,36]{1,0:T(8,128)S(1)}, f32[36,36]{1,0:T(8,128)S(1)}) all-reduce(f32[36,36]{1,0:T(8,128)S(1)} %convolution_bitcast_fusion.7, f32[36,36]{1,0:T(8,128)S(1)} %convolution_bitcast_fusion.6), channel_id=1, replica_groups=mesh['row'=32,'col'=8] {'row'}, use_global_device_ids=true, to_apply=%region_55.58 | all-reduce | flops 2592 | bytes 20736 | tf_op jit(solution)/shard_map/psum | solution.py:134
  1052.8 137.9 %psum.70 = f32[36,36]{0,1:T(8,128)S(1)} all-reduce(f32[36,36]{0,1:T(8,128)S(1)} %convolution_bitcast_fusion.5), channel_id=1, replica_groups=mesh['row'=32,'col'=8] {'row'}, use_global_device_ids=true, to_apply=%region_57.60 | all-reduce | flops 1296 | bytes 10368 | tf_op jit(solution)/shard_map/psum | solution.py:138
  1192.1 6.6 cholesky.42
  1200.1 5.5 custom-call.11
  1209.4 137.7 %psum.71 = f32[2,36,36]{1,2,0:T(8,128)S(1)} all-reduce(f32[2,36,36]{1,2,0:T(8,128)S(1)} %pad_maximum_fusion.24), channel_id=1, replica_groups=mesh['row'=32,'col'=8] {'row'}, use_global_device_ids=true, to_apply=%region_60.63 | all-reduce | flops 2592 | bytes 20736 | tf_op jit(solution)/shard_map/psum | solution.py:159
  (284 shorter events, 235.1 us)
Async XLA Ops:
  7.2 236.3 %all-gather.3.cloned.1.call-start = ((), (), s32[]{:S(2)}) async-start(), calls=%async_computation | async-start | bytes 5406720 | tf_op jit(solution)/shard_map/all_gather | solution.py:103
  157.9 4.1 copy-start.15
  164.4 224.1 %all-reduce.4.cloned.1.call-start = ((), (), s32[]{:S(2)}) async-start(), calls=%async_computation.1 | async-start | bytes 655360 | tf_op jit(solution)/shard_map/psum | solution.py:122
  173.9 4.4 copy-start.3
  179.7 118.1 %copy-start = (bf16[2,1024,128]{2,1,0:T(8,128)(2,1)}, bf16[2,1024,128]{2,1,0:T(8,128)(2,1)S(1)}, u32[]{:S(2)}) copy-start(bf16[2,1024,128]{2,1,0:T(8,128)(2,1)S(1)} %get-tuple-element.571) | copy-start | bytes 1572868
  302.7 4.9 copy-start.10
  312.3 14.4 %copy-start.6 = (f32[2,36,1024]{2,1,0:T(8,128)S(1)}, f32[2,36,1024]{2,1,0:T(8,128)}, u32[]{:S(2)}) copy-start(f32[2,36,1024]{2,1,0:T(8,128)} %get-tuple-element.623) | copy-start | bytes 884740
  317.2 71.3 %copy-start.19 = (f32[1024]{0:T(1024)S(1)}, f32[1024]{0:T(1024)}, u32[]{:S(2)}) copy-start(f32[1024]{0:T(1024)} %param.60) | copy-start | bytes 12292
  329.8 432.3 %all-gather.5.cloned.1.call-start = ((), (), s32[]{:S(2)}) async-start(), calls=%async_computation.2 | async-start | bytes 5406720 | tf_op jit(solution)/shard_map/all_gather | solution.py:103
  533.0 229.1 %copy-start.13 = (f32[36,36]{1,0:T(8,128)}, f32[36,36]{1,0:T(8,128)S(1)}, u32[]{:S(2)}) copy-start(f32[36,36]{1,0:T(8,128)S(1)} %psum.65) | copy-start | bytes 15556
  534.4 0.7 copy-start.2
  676.9 4.1 copy-start.17
  683.3 220.2 %all-reduce.6.cloned.1.call-start = ((), (), s32[]{:S(2)}) async-start(), calls=%async_computation.3 | async-start | bytes 655360 | tf_op jit(solution)/shard_map/psum | solution.py:122
  762.1 33.0 %copy-start.1 = (bf16[2,64,1024]{2,1,0:T(8,128)(2,1)S(1)}, bf16[2,64,1024]{2,1,0:T(8,128)(2,1)}, u32[]{:S(2)}) copy-start(bf16[2,64,1024]{2,1,0:T(8,128)(2,1)} %get-tuple-element.578) | copy-start | bytes 786436
  823.7 0.7 copy-start.11
  829.1 13.1 copy-start.7
  829.1 13.1 copy-start.8
  829.1 13.1 copy-start.9
  834.0 8.2 copy-start.12
  834.0 10.8 copy-start.14
  834.0 10.8 copy-start.16
  842.2 348.5 %copy-start.18 = (f32[36,36]{1,0:T(8,128)S(1)}, f32[36,36]{1,0:T(8,128)}, u32[]{:S(2)}) copy-start(f32[36,36]{1,0:T(8,128)} %copy-done.17) | copy-start | bytes 15556
  842.2 349.3 %copy-start.20 = (f32[36,36]{1,0:T(8,128)S(1)}, f32[36,36]{1,0:T(8,128)}, u32[]{:S(2)}) copy-start(f32[36,36]{1,0:T(8,128)} %convolution_add_fusion.36) | copy-start | bytes 15556
  844.8 363.4 %copy-start.5 = (f32[1,36,1024]{2,0,1:T(1,128)S(1)}, f32[1,36,1024]{2,0,1:T(1,128)}, u32[]{:S(2)}) copy-start(f32[1,36,1024]{2,0,1:T(1,128)} %get-tuple-element.587) | copy-start | bytes 442372
  844.8 364.0 %copy-start.4 = (f32[1,36,1024]{2,0,1:T(1,128)S(1)}, f32[1,36,1024]{2,0,1:T(1,128)}, u32[]{:S(2)}) copy-start(f32[1,36,1024]{2,0,1:T(1,128)} %get-tuple-element.586) | copy-start | bytes 442372
Sparse Core Ops, SparseCore 0:
  164.5 78.8 all-gather.2
  329.9 58.5 all-reduce.3
  683.4 78.6 all-gather.4
  844.9 58.5 all-reduce.5
where the time goes:
time: 1360 us; the launch traced here: 1350 us
  blocking collectives  845 us (62%)
  waiting for transfers between devices  256 us (19%)
  matrix products  162 us (12%)
  other arithmetic  54.3 us (4%)
  between operations  21.8 us (2%)
    psum x1, blocking collectives, body(): lax.psum(inner_products(incident, incident), 'row')  146 us
    psum x1, blocking collectives, body(): lax.psum((inner_products(image, basis_one), inner_products(image, basis_t...  143 us
    psum x1, blocking collectives, body(): coupling_one = lax.psum(inner_products(image, basis_one), 'row')  143 us
    all_gather x2, waiting for transfers between devices, apply_operator(): gathered = lax.all_gather(rounded, 'row', axis=2, tiled=True)  140 us
    psum x1, blocking collectives, body(): gram_two = lax.psum(inner_products(rest, rest), 'row')  138 us
    psum x1, blocking collectives, body(): gram_one = lax.psum(inner_products(rest, rest), 'row')  138 us
    psum x1, blocking collectives, body(): coefficients = lax.psum(project(harmonics, solution), 'row')  138 us
    psum x2, waiting for transfers between devices, apply_operator(): summed = lax.psum(total, 'col')  116 us
  transfers between devices with their start and end apart: 4, of which 4 were waited for; matrix products, arithmetic and copies ran while one was open for 1% of the time, Pallas kernels for 0%

commit v1 on v0

--- a/solution.py
+++ b/solution.py
@@ -3,9 +3,75 @@
 import jax
 import jax.numpy as jnp
 from jax import lax
+from jax.experimental import pallas as pl
+from jax.experimental.pallas import tpu as pltpu
 from jax.sharding import PartitionSpec as P
 
 highest = lax.Precision.HIGHEST
+MESH = pl.DeviceIdType.MESH
+
+
+def allreduce_kernel(n, x_ref, o_ref, buf, send_sems, recv_sems):
+    me = lax.axis_index("row")
+    col = lax.axis_index("col")
+    barrier = pltpu.get_barrier_semaphore()
+    for d in range(1, n):
+        pl.semaphore_signal(
+            barrier, inc=1, device_id=(lax.rem(me + d, n), col), device_id_type=MESH
+        )
+    pl.semaphore_wait(barrier, n - 1)
+    copies = []
+    for d in range(1, n):
+        copy = pltpu.make_async_remote_copy(
+            src_ref=x_ref,
+            dst_ref=buf.at[d],
+            send_sem=send_sems.at[d],
+            recv_sem=recv_sems.at[d],
+            device_id=(lax.rem(me + d, n), col),
+            device_id_type=MESH,
+        )
+        copy.start()
+        copies.append(copy)
+    buf[0] = x_ref[...]
+    for copy in copies:
+        copy.wait()
+    total = buf[me]
+    for source in range(1, n):
+        total = total + buf[lax.rem(me + n - source, n)]
+    o_ref[...] = total
+
+
+def row_allreduce(packed, collective_id):
+    n = lax.axis_size("row")
+    rows, lanes = packed.shape
+    return pl.pallas_call(
+        partial(allreduce_kernel, n),
+        out_shape=jax.ShapeDtypeStruct((rows, lanes), jnp.float32),
+        in_specs=[pl.BlockSpec(memory_space=pltpu.VMEM)],
+        out_specs=pl.BlockSpec(memory_space=pltpu.VMEM),
+        scratch_shapes=[
+            pltpu.VMEM((n, rows, lanes), jnp.float32),
+            pltpu.SemaphoreType.DMA((n,)),
+            pltpu.SemaphoreType.DMA((n,)),
+        ],
+        compiler_params=pltpu.CompilerParams(collective_id=collective_id, has_side_effects=True),
+    )(packed)
+
+
+def row_psum(ids, *arrays):
+    flat = [a.reshape(-1) for a in arrays]
+    sizes = [f.shape[0] for f in flat]
+    total = sum(sizes)
+    padded = -(-total // 1024) * 1024
+    packed = jnp.concatenate(flat + [jnp.zeros((padded - total,), jnp.float32)]).reshape(-1, 128)
+    summed = row_allreduce(packed, len(ids)).reshape(-1)
+    ids.append(None)
+    outs = []
+    start = 0
+    for a, size in zip(arrays, sizes):
+        outs.append(summed[start : start + size].reshape(a.shape))
+        start += size
+    return outs[0] if len(outs) == 1 else tuple(outs)
 
 
 def dense_term(vector, block):
@@ -73,6 +139,7 @@
     row_index = lax.axis_index("row")
     column = lax.axis_index("col")
     empty = jnp.zeros((2, fields, elements), jnp.float32)
+    ids = []
 
     def far_term(number, piece):
         cluster = column * blocks + number
@@ -122,20 +189,20 @@
         summed = lax.psum(total, "col")
         return summed + diagonal[None, None, :] * vector
 
-    lower_first = jnp.linalg.cholesky(lax.psum(inner_products(incident, incident), "row"))
+    lower_first = jnp.linalg.cholesky(row_psum(ids, inner_products(incident, incident)))
     basis_one = combine_rows(lower_inverse(lower_first), incident)
     image = apply_operator(basis_one)
-    coupling_one = lax.psum(inner_products(image, basis_one), "row")
+    coupling_one = row_psum(ids, inner_products(image, basis_one))
     rest = image - combine_rows(coupling_one, basis_one)
-    gram_one = lax.psum(inner_products(rest, rest), "row")
+    gram_one = row_psum(ids, inner_products(rest, rest))
     lower_second = jnp.linalg.cholesky(gram_one)
     basis_two = combine_rows(lower_inverse(lower_second), rest)
     image = apply_operator(basis_two)
-    coupling_onetwo, coupling_two = lax.psum(
-        (inner_products(image, basis_one), inner_products(image, basis_two)), "row"
+    coupling_onetwo, coupling_two = row_psum(
+        ids, inner_products(image, basis_one), inner_products(image, basis_two)
     )
     rest = image - combine_rows(coupling_onetwo, basis_one) - combine_rows(coupling_two, basis_two)
-    gram_two = lax.psum(inner_products(rest, rest), "row")
+    gram_two = row_psum(ids, inner_products(rest, rest))
     upper_left = matmul(coupling_one, coupling_one.T) + gram_one
     upper_right = matmul(coupling_one, coupling_onetwo.T) + matmul(lower_second, coupling_two.T)
     lower_right = (
@@ -156,7 +223,7 @@
     first_weights = weights[:, :fields]
     second_weights = weights[:, fields:]
     solution = combine_rows(first_weights, basis_one) + combine_rows(second_weights, basis_two)
-    coefficients = lax.psum(project(harmonics, solution), "row")
+    coefficients = row_psum(ids, project(harmonics, solution))
     return (solution, coefficients)
 
 

time: 1360 us -> 644 us (0.47)
  blocking collectives: 845 us -> 0 us
  Pallas kernels: 0 us -> 105 us
  waiting for transfers between devices: 256 us -> 270 us
    psum x6 -> x0, blocking collectives: 845 us -> none  [the longest x1 146 us: body(): lax.psum(inner_products(incident, incident), 'row')]
    pallas_call x0 -> x6, Pallas kernels: none -> 105 us  [row_allreduce(): pl.pallas_call(partial(allreduce_kernel, n), out_shape=jax.ShapeDtypeStru...]
  transfers between devices with their start and end apart: 4 -> 4, of which waited for: 4 -> 4; matrix products, arithmetic and copies ran while one was open for 1% -> 2% of each run, Pallas kernels for 0% -> 0%
where the time goes in v1:
time: 644 us; the launch traced here: 639 us
  waiting for transfers between devices  270 us (42%)
  matrix products  162 us (25%)
  Pallas kernels  105 us (16%)
  other arithmetic  54.5 us (8%)
  local copies, waits for them, and re-layouts  23.8 us (4%)
  between operations  22.2 us (3%)
    all_gather x2, waiting for transfers between devices, apply_operator(): gathered = lax.all_gather(rounded, 'row', axis=2, tiled=True)  151 us
    psum x2, waiting for transfers between devices, apply_operator(): summed = lax.psum(total, 'col')  119 us
    pallas_call x6, Pallas kernels, row_allreduce(): pl.pallas_call(partial(allreduce_kernel, n), out_shape=jax.ShapeDtypeStru...  105 us
    dot_general x64, matrix products, product(): jnp.einsum('sf,ef->se', left, right, preferred_element_type=jnp.float32)  71.2 us
    dot_general x32, matrix products, inner(): jnp.einsum('sf,rf->sr', left, right, preferred_element_type=jnp.float32)  40.1 us
    dot_general x32, matrix products, outer(): jnp.einsum('sr,re->se', left, right, preferred_element_type=jnp.float32)  30.2 us
  transfers between devices with their start and end apart: 4, of which 4 were waited for; matrix products, arithmetic and copies ran while one was open for 2% of the time, Pallas kernels for 0%

profile of v1, /device:TPU:24, one launch (start us, length us, event | category | flops | bytes accessed | tf_op | source)
XLA Modules:
  0.0 639.1 jit_solution(985040685682662673)
XLA Ops:
  9.5 19.1 %shard_map.95 = f32[16,128]{1,0:T(8,128)} custom-call(f32[16,128]{1,0:T(8,128)} %pad_bitcast_fusion.4.x_ref), custom_call_target="tpu_custom_call" | custom-call | tf_op jit(solution)/shard_map/pallas_call | solution.py:47
  54.6 69.4 %all-gather.3.cloned.1.call-done = bf16[2,36,32768]{2,1,0:T(8,128)(2,1)} async-done(((bf16[2,36,1024]{2,1,0:T(8,128)(2,1)}), bf16[2,36,32768]{2,1,0:T(8,128)(2,1)}) %all-gather.3.cloned.1.call-update) | async-done | bytes 4718608 | tf_op jit(solution)/shard_map/all_gather | solution.py:170
  124.0 10.4 %conditional.35 = (f32[2,36,1024]{2,1,0:T(8,128)}) conditional(s32[]{:T(128)} %convert_element_type.138, (s32[]{:T(128)}, bf16[2,36,32768]{2,1,0:T(8,128)(2,1)}, s32[]{:T(128)}, bf16[2,64,1024]{2,1,0:T(8,128)(2,1)}, bf16[2,64,1024]{2,1,0:T(8,128)(2,1)}) %tuple.224, () %tuple.225), branch_computations={%region_24.27_spmd, %region_25.28_spmd} | conditional | flops 37928512 | bytes 2991264 | solution.py:148
  134.3 10.5 %conditional.34 = (f32[2,36,1024]{2,1,0:T(8,128)}) conditional(s32[]{:T(128)} %convert_element_type.137, (s32[]{:T(128)}, bf16[2,36,32768]{2,1,0:T(8,128)(2,1)}, s32[]{:T(128)}, bf16[2,64,1024]{2,1,0:T(8,128)(2,1)}, bf16[2,64,1024]{2,1,0:T(8,128)(2,1)}) %tuple.222, () %tuple.223), branch_computations={%region_22.25_spmd, %region_23.26_spmd} | conditional | flops 37928512 | bytes 2991264 | solution.py:148
  144.8 10.4 %conditional.33 = (f32[2,36,1024]{2,1,0:T(8,128)}) conditional(s32[]{:T(128)} %convert_element_type.136, (s32[]{:T(128)}, bf16[2,36,32768]{2,1,0:T(8,128)(2,1)}, s32[]{:T(128)}, bf16[2,64,1024]{2,1,0:T(8,128)(2,1)}, bf16[2,64,1024]{2,1,0:T(8,128)(2,1)}) %tuple.220, () %tuple.221), branch_computations={%region_20.23_spmd, %region_21.24_spmd} | conditional | flops 37928512 | bytes 2991264 | solution.py:148
  155.2 10.4 %conditional.32 = (f32[2,36,1024]{2,1,0:T(8,128)}) conditional(s32[]{:T(128)} %convert_element_type.135, (s32[]{:T(128)}, bf16[2,36,32768]{2,1,0:T(8,128)(2,1)}, s32[]{:T(128)}, bf16[2,64,1024]{2,1,0:T(8,128)(2,1)}, bf16[2,64,1024]{2,1,0:T(8,128)(2,1)}) %tuple.218, () %tuple.219), branch_computations={%region_18.21_spmd, %region_19.22_spmd} | conditional | flops 37928512 | bytes 2991264 | solution.py:148
  165.6 6.4 %conditional.31 = (f32[2,36,1024]{2,1,0:T(8,128)}) conditional(s32[]{:T(128)} %bitcast.214, () %tuple.216, (bf16[2,36,32768]{2,1,0:T(8,128)(2,1)}, s32[]{:T(128)}, bf16[2,1024,128]{2,1,0:T(8,128)(2,1)}) %tuple.217), branch_computations={%region_16.19_spmd, %region_17.20_spmd} | conditional | flops 37896192 | bytes 2582556 | solution.py:161
  172.0 6.4 %conditional.30 = (f32[2,36,1024]{2,1,0:T(8,128)}) conditional(s32[]{:T(128)} %bitcast.212, () %tuple.214, (bf16[2,36,32768]{2,1,0:T(8,128)(2,1)}, s32[]{:T(128)}, bf16[2,1024,128]{2,1,0:T(8,128)(2,1)}) %tuple.215), branch_computations={%region_14.17_spmd, %region_15.18_spmd} | conditional | flops 37896192 | bytes 2582556 | solution.py:161
  178.5 4.9 conditional.29
  183.4 4.8 conditional.28
  188.2 4.8 conditional.27
  193.0 4.8 conditional.26
  197.8 4.8 conditional.24
  202.7 4.8 conditional.25
  210.8 59.8 %all-reduce.8.cloned.1.call-done = f32[2,36,1024]{2,1,0:T(8,128)} async-done(((f32[2,36,1024]{2,1,0:T(8,128)}), f32[2,36,1024]{2,1,0:T(8,128)}) %all-reduce.8.cloned.1.call-update) | async-done | bytes 294928 | tf_op jit(solution)/shard_map/psum | solution.py:189
  272.7 17.6 %shard_map.96 = f32[16,128]{1,0:T(8,128)} custom-call(f32[16,128]{1,0:T(8,128)} %pad_bitcast_fusion.3.x_ref), custom_call_target="tpu_custom_call" | custom-call | tf_op jit(solution)/shard_map/pallas_call | solution.py:47
  294.4 15.4 %shard_map.97 = f32[16,128]{1,0:T(8,128)} custom-call(f32[16,128]{1,0:T(8,128)} %pad_bitcast_fusion.2.x_ref), custom_call_target="tpu_custom_call" | custom-call | tf_op jit(solution)/shard_map/pallas_call | solution.py:47
  324.1 81.5 %all-gather.5.cloned.1.call-done = bf16[2,36,32768]{2,1,0:T(8,128)(2,1)} async-done(((bf16[2,36,1024]{2,1,0:T(8,128)(2,1)}), bf16[2,36,32768]{2,1,0:T(8,128)(2,1)}) %all-gather.5.cloned.1.call-update) | async-done | bytes 4718608 | tf_op jit(solution)/shard_map/all_gather | solution.py:170
  405.6 11.1 %conditional.47 = (f32[2,36,1024]{2,1,0:T(8,128)}) conditional(s32[]{:T(128)} %convert_element_type.138, (s32[]{:T(128)}, bf16[2,36,32768]{2,1,0:T(8,128)(2,1)}, s32[]{:T(128)}, bf16[2,64,1024]{2,1,0:T(8,128)(2,1)}, bf16[2,64,1024]{2,1,0:T(8,128)(2,1)}) %tuple.248, () %tuple.249), branch_computations={%region_49.52_spmd, %region_50.53_spmd} | conditional | flops 37928512 | bytes 3002528 | solution.py:148
  416.6 11.1 %conditional.46 = (f32[2,36,1024]{2,1,0:T(8,128)}) conditional(s32[]{:T(128)} %convert_element_type.137, (s32[]{:T(128)}, bf16[2,36,32768]{2,1,0:T(8,128)(2,1)}, s32[]{:T(128)}, bf16[2,64,1024]{2,1,0:T(8,128)(2,1)}, bf16[2,64,1024]{2,1,0:T(8,128)(2,1)}) %tuple.246, () %tuple.247), branch_computations={%region_47.50_spmd, %region_48.51_spmd} | conditional | flops 37928512 | bytes 3002528 | solution.py:148
  427.7 11.0 %conditional.45 = (f32[2,36,1024]{2,1,0:T(8,128)}) conditional(s32[]{:T(128)} %convert_element_type.136, (s32[]{:T(128)}, bf16[2,36,32768]{2,1,0:T(8,128)(2,1)}, s32[]{:T(128)}, bf16[2,64,1024]{2,1,0:T(8,128)(2,1)}, bf16[2,64,1024]{2,1,0:T(8,128)(2,1)}) %tuple.244, () %tuple.245), branch_computations={%region_45.48_spmd, %region_46.49_spmd} | conditional | flops 37928512 | bytes 3002528 | solution.py:148
  438.7 7.4 %conditional.44 = (f32[2,36,1024]{2,1,0:T(8,128)}) conditional(s32[]{:T(128)} %convert_element_type.135, (s32[]{:T(128)}, bf16[2,36,32768]{2,1,0:T(8,128)(2,1)}, s32[]{:T(128)}, bf16[2,64,1024]{2,1,0:T(8,128)(2,1)}, bf16[2,64,1024]{2,1,0:T(8,128)(2,1)S(1)}) %tuple.345, () %tuple.243), branch_computations={%region_43.46_spmd, %region_44.47_spmd} | conditional | flops 37928512 | bytes 3002528 | solution.py:148
  446.2 5.7 conditional.43
  451.9 5.7 conditional.42
  457.6 5.7 conditional.41
  472.9 4.9 conditional.38
  489.6 59.2 %all-reduce.10.cloned.1.call-done = f32[2,36,1024]{2,1,0:T(8,128)} async-done(((f32[2,36,1024]{2,1,0:T(8,128)}), f32[2,36,1024]{2,1,0:T(8,128)}) %all-reduce.10.cloned.1.call-update) | async-done | bytes 294928 | tf_op jit(solution)/shard_map/psum | solution.py:189
  552.4 20.5 %shard_map.98 = f32[24,128]{1,0:T(8,128)} custom-call(f32[24,128]{1,0:T(8,128)} %bitcast.903), custom_call_target="tpu_custom_call" | custom-call | tf_op jit(solution)/shard_map/pallas_call | solution.py:47
  578.2 15.7 %shard_map.99 = f32[16,128]{1,0:T(8,128)} custom-call(f32[16,128]{1,0:T(8,128)} %pad_bitcast_fusion.1.x_ref), custom_call_target="tpu_custom_call" | custom-call | tf_op jit(solution)/shard_map/pallas_call | solution.py:47
  596.1 6.6 %cholesky.42 = f32[72,72]{1,0:T(8,128)S(1)} custom-call(f32[72,72]{1,0:T(8,128)S(1)} %fusion.503), custom_call_target="Cholesky" | custom-call | tf_op jit(solution)/shard_map/jit(cholesky)/cholesky | solution.py:221
  604.0 5.5 custom-call.11
  614.2 17.0 %shard_map.100 = f32[24,128]{1,0:T(8,128)} custom-call(f32[24,128]{1,0:T(8,128)} %pad_bitcast_fusion.x_ref), custom_call_target="tpu_custom_call" | custom-call | tf_op jit(solution)/shard_map/pallas_call | solution.py:47
  (311 shorter events, 246.0 us)
Async XLA Ops:
  7.2 116.8 %all-gather.3.cloned.1.call-start = ((), (), s32[]{:S(2)}) async-start(), calls=%async_computation | async-start | bytes 5406720 | tf_op jit(solution)/shard_map/all_gather | solution.py:170
  32.8 4.0 copy-start.15
  39.1 231.4 %all-reduce.8.cloned.1.call-start = ((), (), s32[]{:S(2)}) async-start(), calls=%async_computation.1 | async-start | bytes 655360 | tf_op jit(solution)/shard_map/psum | solution.py:189
  48.9 4.4 copy-start.3
  54.6 123.9 %copy-start = (bf16[2,1024,128]{2,1,0:T(8,128)(2,1)}, bf16[2,1024,128]{2,1,0:T(8,128)(2,1)S(1)}, u32[]{:S(2)}) copy-start(bf16[2,1024,128]{2,1,0:T(8,128)(2,1)S(1)} %get-tuple-element.569) | copy-start | bytes 1572868
  183.4 4.8 copy-start.10
  193.0 14.5 %copy-start.6 = (f32[2,36,1024]{2,1,0:T(8,128)S(1)}, f32[2,36,1024]{2,1,0:T(8,128)}, u32[]{:S(2)}) copy-start(f32[2,36,1024]{2,1,0:T(8,128)} %get-tuple-element.623) | copy-start | bytes 884740
  197.8 72.7 %copy-start.19 = (f32[1024]{0:T(1024)S(1)}, f32[1024]{0:T(1024)}, u32[]{:S(2)}) copy-start(f32[1024]{0:T(1024)} %param.60) | copy-start | bytes 12292
  210.5 195.0 %all-gather.5.cloned.1.call-start = ((), (), s32[]{:S(2)}) async-start(), calls=%async_computation.2 | async-start | bytes 5406720 | tf_op jit(solution)/shard_map/all_gather | solution.py:170
  292.5 0.7 copy-start.2
  314.1 4.0 copy-start.17
  320.4 228.4 %all-reduce.10.cloned.1.call-start = ((), (), s32[]{:S(2)}) async-start(), calls=%async_computation.3 | async-start | bytes 655360 | tf_op jit(solution)/shard_map/psum | solution.py:189
  323.3 82.3 %copy-start.13 = (f32[36,36]{1,0:T(8,128)}, f32[36,36]{1,0:T(8,128)S(1)}, u32[]{:S(2)}) copy-start(f32[36,36]{1,0:T(8,128)S(1)} %reshape.182) | copy-start | bytes 15556
  405.6 33.1 %copy-start.1 = (bf16[2,64,1024]{2,1,0:T(8,128)(2,1)S(1)}, bf16[2,64,1024]{2,1,0:T(8,128)(2,1)}, u32[]{:S(2)}) copy-start(bf16[2,64,1024]{2,1,0:T(8,128)(2,1)} %get-tuple-element.576) | copy-start | bytes 786436
  467.4 0.7 copy-start.11
  472.9 13.3 %copy-start.7 = (f32[2,36,1024]{2,1,0:T(8,128)S(1)}, f32[2,36,1024]{2,1,0:T(8,128)}, u32[]{:S(2)}) copy-start(f32[2,36,1024]{2,1,0:T(8,128)} %get-tuple-element.635) | copy-start | bytes 884740
  472.9 13.3 %copy-start.8 = (f32[2,36,1024]{2,1,0:T(8,128)S(1)}, f32[2,36,1024]{2,1,0:T(8,128)}, u32[]{:S(2)}) copy-start(f32[2,36,1024]{2,1,0:T(8,128)} %get-tuple-element.634) | copy-start | bytes 884740
  472.9 13.3 %copy-start.9 = (f32[2,36,1024]{2,1,0:T(8,128)S(1)}, f32[2,36,1024]{2,1,0:T(8,128)}, u32[]{:S(2)}) copy-start(f32[2,36,1024]{2,1,0:T(8,128)} %get-tuple-element.633) | copy-start | bytes 884740
  477.8 8.4 %copy-start.12 = (f32[2,36,1024]{2,1,0:T(8,128)S(1)}, f32[2,36,1024]{2,1,0:T(8,128)}, u32[]{:S(2)}) copy-start(f32[2,36,1024]{2,1,0:T(8,128)} %copy-done.11) | copy-start | bytes 884740
  477.8 11.0 %copy-start.14 = (f32[36,36]{1,0:T(8,128)S(1)}, f32[36,36]{1,0:T(8,128)}, u32[]{:S(2)}) copy-start(f32[36,36]{1,0:T(8,128)} %copy-done.13) | copy-start | bytes 15556
  477.8 11.0 %copy-start.16 = (f32[36,36]{1,0:T(8,128)S(1)}, f32[36,36]{1,0:T(8,128)}, u32[]{:S(2)}) copy-start(f32[36,36]{1,0:T(8,128)} %copy-done.15) | copy-start | bytes 15556
  486.1 108.6 %copy-start.18 = (f32[36,36]{1,0:T(8,128)S(1)}, f32[36,36]{1,0:T(8,128)}, u32[]{:S(2)}) copy-start(f32[36,36]{1,0:T(8,128)} %copy-done.17) | copy-start | bytes 15556
  486.1 109.3 %copy-start.20 = (f32[36,36]{1,0:T(8,128)S(1)}, f32[36,36]{1,0:T(8,128)}, u32[]{:S(2)}) copy-start(f32[36,36]{1,0:T(8,128)} %convolution_add_fusion.36) | copy-start | bytes 15556
  488.7 123.4 %copy-start.5 = (f32[1,36,1024]{2,0,1:T(1,128)S(1)}, f32[1,36,1024]{2,0,1:T(1,128)}, u32[]{:S(2)}) copy-start(f32[1,36,1024]{2,0,1:T(1,128)} %get-tuple-element.585) | copy-start | bytes 442372
  488.7 124.0 %copy-start.4 = (f32[1,36,1024]{2,0,1:T(1,128)S(1)}, f32[1,36,1024]{2,0,1:T(1,128)}, u32[]{:S(2)}) copy-start(f32[1,36,1024]{2,0,1:T(1,128)} %get-tuple-element.584) | copy-start | bytes 442372
Sparse Core Ops, SparseCore 0:
  39.3 84.6 all-gather.2
  210.7 59.8 all-reduce.7
  320.5 85.0 all-gather.4
  488.9 59.8 all-reduce.9

commit v2 on v1

--- a/solution.py
+++ b/solution.py
@@ -15,30 +15,41 @@
     me = lax.axis_index("row")
     col = lax.axis_index("col")
     barrier = pltpu.get_barrier_semaphore()
-    for d in range(1, n):
-        pl.semaphore_signal(
-            barrier, inc=1, device_id=(lax.rem(me + d, n), col), device_id_type=MESH
-        )
-    pl.semaphore_wait(barrier, n - 1)
-    copies = []
-    for d in range(1, n):
-        copy = pltpu.make_async_remote_copy(
+
+    def peer(d):
+        return (lax.rem(me + d, n), col)
+
+    def copy(d):
+        return pltpu.make_async_remote_copy(
             src_ref=x_ref,
             dst_ref=buf.at[d],
             send_sem=send_sems.at[d],
             recv_sem=recv_sems.at[d],
-            device_id=(lax.rem(me + d, n), col),
+            device_id=peer(d),
             device_id_type=MESH,
         )
-        copy.start()
-        copies.append(copy)
+
+    def greet(d, carry):
+        pl.semaphore_signal(barrier, inc=1, device_id=peer(d), device_id_type=MESH)
+        return carry
+
+    def start(d, carry):
+        copy(d).start()
+        return carry
+
+    def finish(d, carry):
+        copy(d).wait()
+        return carry
+
+    def add(source, total):
+        return total + buf[lax.rem(me + n - source, n)]
+
+    lax.fori_loop(1, n, greet, 0)
+    pl.semaphore_wait(barrier, n - 1)
+    lax.fori_loop(1, n, start, 0)
     buf[0] = x_ref[...]
-    for copy in copies:
-        copy.wait()
-    total = buf[me]
-    for source in range(1, n):
-        total = total + buf[lax.rem(me + n - source, n)]
-    o_ref[...] = total
+    lax.fori_loop(1, n, finish, 0)
+    o_ref[...] = lax.fori_loop(1, n, add, buf[me])
 
 
 def row_allreduce(packed, collective_id):
@@ -74,31 +85,10 @@
     return outs[0] if len(outs) == 1 else tuple(outs)
 
 
-def dense_term(vector, block):
-
-    def product(left, right):
-        return jnp.einsum("sf,ef->se", left, right, preferred_element_type=jnp.float32)
-
-    real_out = product(vector[0], block[0]) - product(vector[1], block[1])
-    imag_out = product(vector[0], block[1]) + product(vector[1], block[0])
-    return jnp.stack([real_out, imag_out])
-
-
-def lowrank_term(vector, left_block, right_block, rank):
-
-    def inner(left, right):
-        return jnp.einsum("sf,rf->sr", left, right, preferred_element_type=jnp.float32)
-
-    def outer(left, right):
-        return jnp.einsum("sr,re->se", left, right, preferred_element_type=jnp.float32)
-
-    coeff_real = inner(vector[0], right_block[0]) - inner(vector[1], right_block[1])
-    coeff_imag = inner(vector[0], right_block[1]) + inner(vector[1], right_block[0])
-    keep = (jnp.arange(right_block.shape[1], dtype=jnp.int32) < rank)[None, None, :]
-    coeffs = jnp.where(keep, jnp.stack([coeff_real, coeff_imag]), 0.0).astype(jnp.bfloat16)
-    real_out = outer(coeffs[0], left_block[0]) - outer(coeffs[1], left_block[1])
-    imag_out = outer(coeffs[0], left_block[1]) + outer(coeffs[1], left_block[0])
-    return jnp.stack([real_out, imag_out])
+def complex_lhs(values, part_axis):
+    real = jnp.take(values, 0, axis=part_axis)
+    imag = jnp.take(values, 1, axis=part_axis)
+    return jnp.stack([jnp.stack([real, -imag]), jnp.stack([imag, real])])
 
 
 def inner_products(first, second):
@@ -138,54 +128,59 @@
     clusters = lax.axis_size("row")
     row_index = lax.axis_index("row")
     column = lax.axis_index("col")
-    empty = jnp.zeros((2, fields, elements), jnp.float32)
     ids = []
 
-    def far_term(number, piece):
-        cluster = column * blocks + number
+    def operator_terms(near_pieces, far_pieces):
+        near_on = flags[0] == 1
+        near_vector = jnp.where(near_on[:, None, None, None], near_pieces, 0).astype(jnp.bfloat16)
+        near_out = jnp.einsum(
+            "caksf,kaef->cse",
+            complex_lhs(near_vector, 1),
+            near_blocks[0],
+            preferred_element_type=jnp.float32,
+        )
+        cluster = column * blocks + jnp.arange(blocks, dtype=jnp.int32)
         offset = (cluster - row_index + half_band) % clusters
         is_near = (offset < slots) & (flags[0, jnp.minimum(offset, slots - 1)] == 1)
-        return lax.cond(
-            is_near,
-            lambda operand: empty,
-            partial(
-                lowrank_term,
-                left_block=left_factors[0, number],
-                right_block=right_factors[0, number],
-                rank=ranks[0, number],
-            ),
-            piece,
-        )
-
-    def near_term(slot, piece):
-        return lax.cond(
-            flags[0, slot] == 1,
-            partial(dense_term, block=near_blocks[0, slot]),
-            lambda operand: empty,
-            piece,
-        )
+        keep = (~is_near)[:, None] & (
+            jnp.arange(right_factors.shape[3], dtype=jnp.int32)[None, :] < ranks[0][:, None]
+        )
+        coeffs = jnp.einsum(
+            "cansf,narf->cnsr",
+            complex_lhs(far_pieces, 1),
+            right_factors[0],
+            preferred_element_type=jnp.float32,
+        )
+        coeffs = jnp.where(keep[None, :, None, :], coeffs, 0.0).astype(jnp.bfloat16)
+        far_out = jnp.einsum(
+            "cansr,nare->cse",
+            complex_lhs(coeffs, 0),
+            left_factors[0],
+            preferred_element_type=jnp.float32,
+        )
+        return near_out + far_out
 
     def apply_operator(vector):
         rounded = vector.astype(jnp.bfloat16)
         gathered = lax.all_gather(rounded, "row", axis=2, tiled=True)
-        far_pieces = [
-            lax.dynamic_slice_in_dim(gathered, (column * blocks + number) * elements, elements, 2)
-            for number in range(blocks)
-        ]
-        near_pieces = [
-            lax.dynamic_slice_in_dim(
-                gathered,
-                (row_index + slot - half_band) % clusters * elements + column * width,
-                width,
-                2,
-            )
-            for slot in range(slots)
-        ]
-        total = near_term(0, near_pieces[0])
-        for slot in range(1, slots):
-            total = total + near_term(slot, near_pieces[slot])
-        for number in range(blocks):
-            total = total + far_term(number, far_pieces[number])
+        far_pieces = jnp.stack(
+            [
+                lax.dynamic_slice_in_dim(gathered, (column * blocks + number) * elements, elements, 2)
+                for number in range(blocks)
+            ]
+        )
+        near_pieces = jnp.stack(
+            [
+                lax.dynamic_slice_in_dim(
+                    gathered,
+                    (row_index + slot - half_band) % clusters * elements + column * width,
+                    width,
+                    2,
+                )
+                for slot in range(slots)
+            ]
+        )
+        total = operator_terms(near_pieces, far_pieces)
         summed = lax.psum(total, "col")
         return summed + diagonal[None, None, :] * vector
 

time: 644 us -> 495 us (0.77)
  matrix products: 162 us -> 25.3 us
  other arithmetic: 54.5 us -> 30.6 us
  waiting for transfers between devices: 270 us -> 285 us
  between operations: 22.2 us -> 14.6 us
  local copies, waits for them, and re-layouts: 23.8 us -> 30.7 us
    dot_general x128 -> x6, matrix products: 142 us -> 6.02 us  [the longest x2 4.24 us: operator_terms(): jnp.einsum('caksf,kaef->cse', complex_lhs(near_vector, 1), near_blocks[0]...]
    another operation x24 -> x14, other arithmetic: 15.4 us -> 0.66 us  [the longest x12 0.48 us: complex_lhs(): return jnp.stack([jnp.stack([real, -imag]), jnp.stack([imag, real])])]
    all_gather x2, waiting for transfers between devices: 151 us -> 165 us  [apply_operator(): gathered = lax.all_gather(rounded, 'row', axis=2, tiled=True)]
    unnamed x44 -> x30, local copies, waits for them, and re-layouts: 3.12 us -> 13.9 us
  transfers between devices with their start and end apart: 4 -> 4, of which waited for: 4 -> 4; matrix products, arithmetic and copies ran while one was open for 2% -> 1% of each run, Pallas kernels for 0% -> 0%
where the time goes in v2:
time: 495 us; the launch traced here: 493 us
  waiting for transfers between devices  285 us (58%)
  Pallas kernels  106 us (21%)
  local copies, waits for them, and re-layouts  30.7 us (6%)
  other arithmetic  30.6 us (6%)
  matrix products  25.3 us (5%)
  between operations  14.6 us (3%)
    all_gather x2, waiting for transfers between devices, apply_operator(): gathered = lax.all_gather(rounded, 'row', axis=2, tiled=True)  165 us
    psum x2, waiting for transfers between devices, apply_operator(): summed = lax.psum(total, 'col')  120 us
    pallas_call x6, Pallas kernels, row_allreduce(): pl.pallas_call(partial(allreduce_kernel, n), out_shape=jax.ShapeDtypeStru...  106 us
    unnamed x30, local copies, waits for them, and re-layouts  13.9 us
    another operation x6, other arithmetic, lower_inverse(): lax.linalg.triangular_solve(lower, identity, left_side=True, lower=True)  12.9 us
  transfers between devices with their start and end apart: 4, of which 4 were waited for; matrix products, arithmetic and copies ran while one was open for 1% of the time, Pallas kernels for 0%

profile of v2, /device:TPU:24, one launch (start us, length us, event | category | flops | bytes accessed | tf_op | source)
XLA Modules:
  0.0 493.0 jit_solution(575208657516743727)
XLA Ops:
  7.2 1.7 convolution_bitcast_fusion.14
  9.6 19.2 %shard_map.95 = f32[16,128]{1,0:T(8,128)} custom-call(f32[16,128]{1,0:T(8,128)} %pad_bitcast_fusion.4.x_ref), custom_call_target="tpu_custom_call" | custom-call | tf_op jit(solution)/shard_map/pallas_call | solution.py:58
  29.7 3.3 cholesky.81
  34.4 2.8 custom-call.15
  37.4 2.1 fusion.137
  39.8 1.4 gather_fusion
  42.6 81.8 %all-gather.3.cloned.1.call-done = bf16[2,36,32768]{2,1,0:T(8,128)(2,1)} async-done(((bf16[2,36,1024]{2,1,0:T(8,128)(2,1)}), bf16[2,36,32768]{2,1,0:T(8,128)(2,1)}) %all-gather.3.cloned.1.call-update) | async-done | bytes 4718608 | tf_op jit(solution)/shard_map/all_gather | solution.py:165
  130.3 1.2 dynamic-slice_bitcast_fusion.7
  132.9 1.0 copy-done.3
  133.9 2.1 fusion.27
  136.1 60.2 %all-reduce.9.cloned.1.call-done = f32[2,36,1024]{2,1,0:T(8,128)} async-done(((f32[2,36,1024]{2,1,0:T(8,128)}), f32[2,36,1024]{2,1,0:T(8,128)}) %all-reduce.9.cloned.1.call-update) | async-done | bytes 294928 | tf_op jit(solution)/shard_map/psum | solution.py:184
  196.3 1.4 convolution_bitcast_fusion.12
  198.4 17.8 %shard_map.96 = f32[16,128]{1,0:T(8,128)} custom-call(f32[16,128]{1,0:T(8,128)} %pad_bitcast_fusion.3.x_ref), custom_call_target="tpu_custom_call" | custom-call | tf_op jit(solution)/shard_map/pallas_call | solution.py:58
  217.0 1.4 fusion.23
  219.5 15.6 %shard_map.97 = f32[16,128]{1,0:T(8,128)} custom-call(f32[16,128]{1,0:T(8,128)} %pad_bitcast_fusion.2.x_ref), custom_call_target="tpu_custom_call" | custom-call | tf_op jit(solution)/shard_map/pallas_call | solution.py:58
  236.1 3.3 cholesky.92
  240.6 2.8 custom-call.16
  243.6 1.1 fusion.138
  246.3 83.7 %all-gather.5.cloned.1.call-done = bf16[2,36,32768]{2,1,0:T(8,128)(2,1)} async-done(((bf16[2,36,1024]{2,1,0:T(8,128)(2,1)}), bf16[2,36,32768]{2,1,0:T(8,128)(2,1)}) %all-gather.5.cloned.1.call-update) | async-done | bytes 4718608 | tf_op jit(solution)/shard_map/all_gather | solution.py:165
  336.0 1.2 dynamic-slice_bitcast_fusion.3
  338.5 1.0 copy-done.4
  339.6 2.1 fusion.24
  342.5 59.4 %all-reduce.11.cloned.1.call-done = f32[2,36,1024]{2,1,0:T(8,128)} async-done(((f32[2,36,1024]{2,1,0:T(8,128)}), f32[2,36,1024]{2,1,0:T(8,128)}) %all-reduce.11.cloned.1.call-update) | async-done | bytes 294928 | tf_op jit(solution)/shard_map/psum | solution.py:184
  402.0 1.4 convolution_bitcast_fusion.8
  403.4 1.4 convolution_bitcast_fusion.9
  405.6 20.6 %shard_map.98 = f32[24,128]{1,0:T(8,128)} custom-call(f32[24,128]{1,0:T(8,128)} %bitcast.400), custom_call_target="tpu_custom_call" | custom-call | tf_op jit(solution)/shard_map/pallas_call | solution.py:58
  429.6 1.4 fusion.22
  432.6 15.9 %shard_map.99 = f32[16,128]{1,0:T(8,128)} custom-call(f32[16,128]{1,0:T(8,128)} %pad_bitcast_fusion.1.x_ref), custom_call_target="tpu_custom_call" | custom-call | tf_op jit(solution)/shard_map/pallas_call | solution.py:58
  449.8 6.6 %cholesky.42 = f32[72,72]{1,0:T(8,128)S(1)} custom-call(f32[72,72]{1,0:T(8,128)S(1)} %fusion.89), custom_call_target="Cholesky" | custom-call | tf_op jit(solution)/shard_map/jit(cholesky)/cholesky | solution.py:216
  457.7 5.5 %custom-call.11 = f32[1,72,72]{1,2,0:T(8,128)S(1)} custom-call(f32[1,72,72]{2,1,0:T(8,128)S(1)} %fusion.86), custom_call_target="InvertDiagBlocksLowerTriangular" | custom-call | tf_op jit(solution)/shard_map/triangular_solve | solution.py:108
  465.4 0.9 copy.55
  467.8 17.2 %shard_map.100 = f32[24,128]{1,0:T(8,128)} custom-call(f32[24,128]{1,0:T(8,128)} %pad_bitcast_fusion.x_ref), custom_call_target="tpu_custom_call" | custom-call | tf_op jit(solution)/shard_map/pallas_call | solution.py:58
  (136 shorter events, 40.0 us)
Async XLA Ops:
  7.2 125.4 %copy-start = (bf16[1,4,2,64,1024]{4,3,2,1,0:T(8,128)(2,1)S(1)}, bf16[1,4,2,64,1024]{4,3,2,1,0:T(8,128)(2,1)}, u32[]{:S(2)}) copy-start(bf16[1,4,2,64,1024]{4,3,2,1,0:T(8,128)(2,1)} %param.26) | copy-start | bytes 3145732
  7.2 117.2 %all-gather.3.cloned.1.call-start = ((), (), s32[]{:S(2)}) async-start(), calls=%async_computation | async-start | bytes 5406720 | tf_op jit(solution)/shard_map/all_gather | solution.py:165
  39.5 156.8 %all-reduce.9.cloned.1.call-start = ((), (), s32[]{:S(2)}) async-start(), calls=%async_computation.1 | async-start | bytes 655360 | tf_op jit(solution)/shard_map/psum | solution.py:184
  39.8 92.1 %copy-start.5 = (bf16[1,4,2,64,1024]{4,3,2,1,0:T(8,128)(2,1)S(1)}, bf16[1,4,2,64,1024]{4,3,2,1,0:T(8,128)(2,1)}, u32[]{:S(2)}) copy-start(bf16[1,4,2,64,1024]{4,3,2,1,0:T(8,128)(2,1)} %param.27) | copy-start | bytes 3145732
  131.7 2.2 copy-start.3
  132.5 63.8 %copy-start.2 = (f32[1024]{0:T(1024)S(1)}, f32[1024]{0:T(1024)}, u32[]{:S(2)}) copy-start(f32[1024]{0:T(1024)} %param.24) | copy-start | bytes 12292
  133.9 111.0 %copy-start.1 = (f32[2,36,1024]{2,0,1:T(2,128)S(1)}, f32[2,36,1024]{2,0,1:T(2,128)}, u32[]{:S(2)}) copy-start(f32[2,36,1024]{2,0,1:T(2,128)} %param.30) | copy-start | bytes 884740
  136.1 193.9 %all-gather.5.cloned.1.call-start = ((), (), s32[]{:S(2)}) async-start(), calls=%async_computation.2 | async-start | bytes 5406720 | tf_op jit(solution)/shard_map/all_gather | solution.py:165
  244.7 157.2 %all-reduce.11.cloned.1.call-start = ((), (), s32[]{:S(2)}) async-start(), calls=%async_computation.3 | async-start | bytes 655360 | tf_op jit(solution)/shard_map/psum | solution.py:184
  245.2 92.3 %copy-start.6 = (bf16[1,4,2,64,1024]{4,3,2,1,0:T(8,128)(2,1)S(1)}, bf16[1,4,2,64,1024]{4,3,2,1,0:T(8,128)(2,1)}, u32[]{:S(2)}) copy-start(bf16[1,4,2,64,1024]{4,3,2,1,0:T(8,128)(2,1)} %param.27) | copy-start | bytes 3145732
  337.4 2.2 copy-start.4
Sparse Core Ops, SparseCore 0:
  39.7 84.6 all-gather.2
  136.2 60.0 all-reduce.8
  244.9 85.0 all-gather.4
  341.8 60.0 all-reduce.10

commit v3 on v2

--- a/solution.py
+++ b/solution.py
@@ -69,6 +69,120 @@
     )(packed)
 
 
+def gather_kernel(rows, cols, blocks, half, v_ref, near_ref, far_ref, slices, far_buf,
+                  first_send, first_recv, second_send, second_recv, local_sems):
+    me = lax.axis_index("row")
+    col = lax.axis_index("col")
+    width = slices.shape[-1]
+    barrier = pltpu.get_barrier_semaphore()
+
+    def row_peer(d):
+        return (lax.rem(me + d, rows), col)
+
+    def col_peer(e):
+        return (me, lax.rem(col + e, cols))
+
+    def window(c):
+        return pl.ds(pl.multiple_of(c * width, width), width)
+
+    own = v_ref.at[:, :, window(col)]
+
+    def first(d):
+        return pltpu.make_async_remote_copy(
+            src_ref=own,
+            dst_ref=slices.at[d],
+            send_sem=first_send.at[d],
+            recv_sem=first_recv.at[d],
+            device_id=row_peer(d),
+            device_id_type=MESH,
+        )
+
+    def second(t):
+        e = 1 + t // blocks
+        n = t % blocks
+        target = lax.rem(col + e, cols)
+        slot = lax.rem(me + rows - blocks * target - n, rows)
+        return pltpu.make_async_remote_copy(
+            src_ref=slices.at[slot],
+            dst_ref=far_buf.at[n, :, :, window(col)],
+            send_sem=second_send.at[t],
+            recv_sem=second_recv.at[t],
+            device_id=col_peer(e),
+            device_id_type=MESH,
+        )
+
+    def greet_row(d, carry):
+        pl.semaphore_signal(barrier, inc=1, device_id=row_peer(d), device_id_type=MESH)
+        return carry
+
+    def greet_col(e, carry):
+        pl.semaphore_signal(barrier, inc=1, device_id=col_peer(e), device_id_type=MESH)
+        return carry
+
+    def start_first(d, carry):
+        first(d).start()
+        return carry
+
+    def finish_first(d, carry):
+        first(d).wait()
+        return carry
+
+    def start_second(t, carry):
+        second(t).start()
+        return carry
+
+    def finish_second(t, carry):
+        second(t).wait()
+        return carry
+
+    lax.fori_loop(1, rows, greet_row, 0)
+    lax.fori_loop(1, cols, greet_col, 0)
+    pl.semaphore_wait(barrier, rows - 1 + cols - 1)
+    lax.fori_loop(1, rows, start_first, 0)
+    local = pltpu.make_async_copy(own, slices.at[0], local_sems.at[blocks])
+    local.start()
+    lax.fori_loop(1, rows, finish_first, 0)
+    local.wait()
+    lax.fori_loop(0, (cols - 1) * blocks, start_second, 0)
+    mine = []
+    for n in range(blocks):
+        slot = lax.rem(me + rows - blocks * col - n, rows)
+        copy = pltpu.make_async_copy(slices.at[slot], far_buf.at[n, :, :, window(col)], local_sems.at[n])
+        copy.start()
+        mine.append(copy)
+    for k in range(2 * half):
+        near_ref[k] = slices[(half - k) % rows]
+    lax.fori_loop(0, (cols - 1) * blocks, finish_second, 0)
+    for copy in mine:
+        copy.wait()
+    far_ref[...] = far_buf[...]
+
+
+def gather_pieces(vector, blocks, half, width, collective_id):
+    rows = lax.axis_size("row")
+    cols = lax.axis_size("col")
+    parts, fields, elements = vector.shape
+    return pl.pallas_call(
+        partial(gather_kernel, rows, cols, blocks, half),
+        out_shape=(
+            jax.ShapeDtypeStruct((2 * half, parts, fields, width), vector.dtype),
+            jax.ShapeDtypeStruct((blocks, parts, fields, elements), vector.dtype),
+        ),
+        in_specs=[pl.BlockSpec(memory_space=pltpu.VMEM)],
+        out_specs=(pl.BlockSpec(memory_space=pltpu.VMEM), pl.BlockSpec(memory_space=pltpu.VMEM)),
+        scratch_shapes=[
+            pltpu.VMEM((rows, parts, fields, width), vector.dtype),
+            pltpu.VMEM((blocks, parts, fields, elements), vector.dtype),
+            pltpu.SemaphoreType.DMA((rows,)),
+            pltpu.SemaphoreType.DMA((rows,)),
+            pltpu.SemaphoreType.DMA(((cols - 1) * blocks,)),
+            pltpu.SemaphoreType.DMA(((cols - 1) * blocks,)),
+            pltpu.SemaphoreType.DMA((blocks + 1,)),
+        ],
+        compiler_params=pltpu.CompilerParams(collective_id=collective_id, has_side_effects=True),
+    )(vector)
+
+
 def row_psum(ids, *arrays):
     flat = [a.reshape(-1) for a in arrays]
     sizes = [f.shape[0] for f in flat]
@@ -162,24 +276,8 @@
 
     def apply_operator(vector):
         rounded = vector.astype(jnp.bfloat16)
-        gathered = lax.all_gather(rounded, "row", axis=2, tiled=True)
-        far_pieces = jnp.stack(
-            [
-                lax.dynamic_slice_in_dim(gathered, (column * blocks + number) * elements, elements, 2)
-                for number in range(blocks)
-            ]
-        )
-        near_pieces = jnp.stack(
-            [
-                lax.dynamic_slice_in_dim(
-                    gathered,
-                    (row_index + slot - half_band) % clusters * elements + column * width,
-                    width,
-                    2,
-                )
-                for slot in range(slots)
-            ]
-        )
+        near_pieces, far_pieces = gather_pieces(rounded, blocks, half_band, width, 16 + len(ids))
+        ids.append(None)
         total = operator_terms(near_pieces, far_pieces)
         summed = lax.psum(total, "col")
         return summed + diagonal[None, None, :] * vector

time: 495 us -> 385 us (0.78)
  waiting for transfers between devices: 285 us -> 122 us
  Pallas kernels: 106 us -> 169 us
  local copies, waits for them, and re-layouts: 30.7 us -> 17.6 us
    all_gather x2 -> x0, waiting for transfers between devices: 165 us -> none  [apply_operator(): gathered = lax.all_gather(rounded, 'row', axis=2, tiled=True)]
    pallas_call x0 -> x2, Pallas kernels: none -> 62.2 us  [gather_pieces(): pl.pallas_call(partial(gather_kernel, rows, cols, blocks, half), out_shap...]
    unnamed x30 -> x20, local copies, waits for them, and re-layouts: 13.9 us -> 1.63 us
  transfers between devices with their start and end apart: 4 -> 2, of which waited for: 4 -> 2; matrix products, arithmetic and copies ran while one was open for 1% -> 0% of each run, Pallas kernels for 0% -> 0%
where the time goes in v3:
time: 385 us; the launch traced here: 384 us
  Pallas kernels  169 us (44%)
  waiting for transfers between devices  122 us (32%)
  other arithmetic  31.9 us (8%)
  matrix products  29.1 us (8%)
  local copies, waits for them, and re-layouts  17.6 us (5%)
  between operations  14.7 us (4%)
    psum x2, waiting for transfers between devices, apply_operator(): summed = lax.psum(total, 'col')  122 us
    pallas_call x6, Pallas kernels, row_allreduce(): pl.pallas_call(partial(allreduce_kernel, n), out_shape=jax.ShapeDtypeStru...  107 us
    pallas_call x2, Pallas kernels, gather_pieces(): pl.pallas_call(partial(gather_kernel, rows, cols, blocks, half), out_shap...  62.2 us
    another operation x6, other arithmetic, lower_inverse(): lax.linalg.triangular_solve(lower, identity, left_side=True, lower=True)  13 us
  transfers between devices with their start and end apart: 2, of which 2 were waited for; matrix products, arithmetic and copies ran while one was open for 0% of the time, Pallas kernels for 0%

profile of v3, /device:TPU:24, one launch (start us, length us, event | category | flops | bytes accessed | tf_op | source)
XLA Modules:
  0.0 384.3 jit_solution(6994748768881296385)
XLA Ops:
  7.2 1.7 convolution_bitcast_fusion.14
  9.6 19.2 %shard_map.95 = f32[16,128]{1,0:T(8,128)} custom-call(f32[16,128]{1,0:T(8,128)} %pad_bitcast_fusion.4.x_ref), custom_call_target="tpu_custom_call" | custom-call | tf_op jit(solution)/shard_map/pallas_call | solution.py:58
  29.7 3.3 cholesky.81
  34.4 2.8 custom-call.15
  37.4 2.1 fusion.131
  39.5 30.3 %shard_map.96 = (bf16[8,2,36,128]{3,2,1,0:T(8,128)(2,1)}, bf16[4,2,36,1024]{3,2,1,0:T(8,128)(2,1)}) custom-call(bf16[2,36,1024]{2,1,0:T(8,128)(2,1)} %get-tuple-element.112.v_ref), custom_call_target="tpu_custom_call" | custom-call | tf_op jit(solution)/shard_map/pallas_call | solution.py:165
  71.9 1.0 slice_bitcast_fusion.3
  73.0 1.3 gather_fusion
  75.2 1.9 fusion.44
  77.7 2.1 fusion.23
  80.4 61.5 %all-reduce.9.cloned.1.call-done = f32[2,36,1024]{2,1,0:T(8,128)} async-done(((f32[2,36,1024]{2,1,0:T(8,128)}), f32[2,36,1024]{2,1,0:T(8,128)}) %all-reduce.9.cloned.1.call-update) | async-done | bytes 294928 | tf_op jit(solution)/shard_map/psum | solution.py:282
  141.9 1.5 convolution_bitcast_fusion.12
  144.1 17.8 %shard_map.97 = f32[16,128]{1,0:T(8,128)} custom-call(f32[16,128]{1,0:T(8,128)} %pad_bitcast_fusion.3.x_ref), custom_call_target="tpu_custom_call" | custom-call | tf_op jit(solution)/shard_map/pallas_call | solution.py:58
  162.7 1.4 fusion.19
  165.2 15.6 %shard_map.98 = f32[16,128]{1,0:T(8,128)} custom-call(f32[16,128]{1,0:T(8,128)} %pad_bitcast_fusion.2.x_ref), custom_call_target="tpu_custom_call" | custom-call | tf_op jit(solution)/shard_map/pallas_call | solution.py:58
  181.8 3.3 cholesky.92
  186.5 2.8 custom-call.16
  189.6 1.1 fusion.132
  190.6 31.9 %shard_map.99 = (bf16[8,2,36,128]{3,2,1,0:T(8,128)(2,1)}, bf16[4,2,36,1024]{3,2,1,0:T(8,128)(2,1)}) custom-call(bf16[2,36,1024]{2,1,0:T(8,128)(2,1)} %get-tuple-element.114.v_ref), custom_call_target="tpu_custom_call" | custom-call | tf_op jit(solution)/shard_map/pallas_call | solution.py:165
  222.5 1.0 fusion.65
  223.6 1.0 slice_bitcast_fusion
  224.6 1.0 slice_bitcast_fusion.2
  227.1 4.3 %fusion.20 = f32[2,36,1024]{2,1,0:T(8,128)} fusion(f32[2,36,1024]{2,1,0:T(8,128)S(1)} %convolution_bitcast_fusion, bf16[1,2,8,36,128]{4,3,2,1,0:T(8,128)(2,1)S(1)} %get-tuple-element.99, bf16[1,2,8,36,128]{4,3,2,1,0:T(8,128)(2,1)S(1)} %get-tuple-element.98, bf16[1,8,2,1024,128]{4,3,2,1,0:T(8,128)(2,1)} %param.25), kind=kOutput, calls=%fused_computation.27 | convolution fusion | flops 302211072 | bytes 5079040 | tf_op jit(solution)/shard_map/caksf,kaef->cse/dot_general | solution.py:250
  232.4 60.2 %all-reduce.11.cloned.1.call-done = f32[2,36,1024]{2,1,0:T(8,128)} async-done(((f32[2,36,1024]{2,1,0:T(8,128)}), f32[2,36,1024]{2,1,0:T(8,128)}) %all-reduce.11.cloned.1.call-update) | async-done | bytes 294928 | tf_op jit(solution)/shard_map/psum | solution.py:282
  292.6 1.4 convolution_bitcast_fusion.9
  294.1 1.4 convolution_bitcast_fusion.8
  296.3 20.7 %shard_map.100 = f32[24,128]{1,0:T(8,128)} custom-call(f32[24,128]{1,0:T(8,128)} %bitcast.348), custom_call_target="tpu_custom_call" | custom-call | tf_op jit(solution)/shard_map/pallas_call | solution.py:58
  319.4 1.4 fusion.18
  322.3 16.1 %shard_map.101 = f32[16,128]{1,0:T(8,128)} custom-call(f32[16,128]{1,0:T(8,128)} %pad_bitcast_fusion.1.x_ref), custom_call_target="tpu_custom_call" | custom-call | tf_op jit(solution)/shard_map/pallas_call | solution.py:58
  340.7 6.6 %cholesky.42 = f32[72,72]{1,0:T(8,128)S(1)} custom-call(f32[72,72]{1,0:T(8,128)S(1)} %fusion.85), custom_call_target="Cholesky" | custom-call | tf_op jit(solution)/shard_map/jit(cholesky)/cholesky | solution.py:314
  348.7 5.5 %custom-call.11 = f32[1,72,72]{1,2,0:T(8,128)S(1)} custom-call(f32[1,72,72]{2,1,0:T(8,128)S(1)} %fusion.82), custom_call_target="InvertDiagBlocksLowerTriangular" | custom-call | tf_op jit(solution)/shard_map/triangular_solve | solution.py:222
  358.8 17.2 %shard_map.102 = f32[24,128]{1,0:T(8,128)} custom-call(f32[24,128]{1,0:T(8,128)} %pad_bitcast_fusion.x_ref), custom_call_target="tpu_custom_call" | custom-call | tf_op jit(solution)/shard_map/pallas_call | solution.py:58
  (118 shorter events, 29.2 us)
Async XLA Ops:
  7.2 70.1 %copy-start = (bf16[1,4,2,64,1024]{4,3,2,1,0:T(8,128)(2,1)S(1)}, bf16[1,4,2,64,1024]{4,3,2,1,0:T(8,128)(2,1)}, u32[]{:S(2)}) copy-start(bf16[1,4,2,64,1024]{4,3,2,1,0:T(8,128)(2,1)} %param.26) | copy-start | bytes 3145732
  7.2 134.7 %all-reduce.9.cloned.1.call-start = ((), (), s32[]{:S(2)}) async-start(), calls=%async_computation | async-start | bytes 655360 | tf_op jit(solution)/shard_map/psum | solution.py:282
  71.9 5.2 %copy-start.1 = (s32[1,8]{1,0:T(1,128)S(1)}, s32[1,8]{1,0:T(1,128)}, u32[]{:S(2)}) copy-start(s32[1,8]{1,0:T(1,128)} %param.28) | copy-start | bytes 100
  71.9 5.2 %copy-start.3 = (bf16[8,2,36,128]{3,2,1,0:T(8,128)(2,1)S(1)}, bf16[8,2,36,128]{3,2,1,0:T(8,128)(2,1)}, u32[]{:S(2)}) copy-start(bf16[8,2,36,128]{3,2,1,0:T(8,128)(2,1)} %get-tuple-element.12) | copy-start | bytes 442372
  75.1 2.6 copy-start.7
  77.3 2.8 copy-start.2
  77.3 64.6 %copy-start.5 = (f32[1024]{0:T(1024)S(1)}, f32[1024]{0:T(1024)}, u32[]{:S(2)}) copy-start(f32[1024]{0:T(1024)} %param.24) | copy-start | bytes 12292
  79.9 212.7 %all-reduce.11.cloned.1.call-start = ((), (), s32[]{:S(2)}) async-start(), calls=%async_computation.1 | async-start | bytes 655360 | tf_op jit(solution)/shard_map/psum | solution.py:282
  141.9 83.8 %copy-start.8 = (bf16[1,4,2,64,1024]{4,3,2,1,0:T(8,128)(2,1)S(1)}, bf16[1,4,2,64,1024]{4,3,2,1,0:T(8,128)(2,1)}, u32[]{:S(2)}) copy-start(bf16[1,4,2,64,1024]{4,3,2,1,0:T(8,128)(2,1)} %param.27) | copy-start | bytes 3145732
  223.5 2.8 copy-start.4
  224.6 1.9 copy-start.6
Sparse Core Ops, SparseCore 0:
  80.0 61.8 all-reduce.8
  231.5 61.0 all-reduce.10

commit v4 on v3

--- a/solution.py
+++ b/solution.py
@@ -183,6 +183,101 @@
     )(vector)
 
 
+def reduce_kernel(cols, x_ref, o_ref, parts_buf, full, first_send, first_recv, second_send, second_recv):
+    me = lax.axis_index("row")
+    col = lax.axis_index("col")
+    width = parts_buf.shape[-1]
+    barrier = pltpu.get_barrier_semaphore()
+
+    def col_peer(e):
+        return (me, lax.rem(col + e, cols))
+
+    def window(c):
+        return pl.ds(pl.multiple_of(c * width, width), width)
+
+    def first(e):
+        return pltpu.make_async_remote_copy(
+            src_ref=x_ref.at[:, :, window(lax.rem(col + e, cols))],
+            dst_ref=parts_buf.at[e],
+            send_sem=first_send.at[e],
+            recv_sem=first_recv.at[e],
+            device_id=col_peer(e),
+            device_id_type=MESH,
+        )
+
+    def second(e):
+        return pltpu.make_async_remote_copy(
+            src_ref=full.at[:, :, window(col)],
+            dst_ref=full.at[:, :, window(col)],
+            send_sem=second_send.at[e],
+            recv_sem=second_recv.at[e],
+            device_id=col_peer(e),
+            device_id_type=MESH,
+        )
+
+    def greet(e, carry):
+        pl.semaphore_signal(barrier, inc=1, device_id=col_peer(e), device_id_type=MESH)
+        return carry
+
+    def start_first(e, carry):
+        first(e).start()
+        return carry
+
+    def finish_first(e, carry):
+        first(e).wait()
+        return carry
+
+    def start_second(e, carry):
+        second(e).start()
+        return carry
+
+    def finish_second(e, carry):
+        second(e).wait_send()
+        pltpu.make_async_remote_copy(
+            src_ref=full.at[:, :, window(col)],
+            dst_ref=full.at[:, :, window(lax.rem(col + cols - e, cols))],
+            send_sem=second_send.at[e],
+            recv_sem=second_recv.at[e],
+            device_id=col_peer(e),
+            device_id_type=MESH,
+        ).wait_recv()
+        return carry
+
+    def add(source, total):
+        return total + parts_buf[lax.rem(col + cols - source, cols)]
+
+    lax.fori_loop(1, cols, greet, 0)
+    pl.semaphore_wait(barrier, cols - 1)
+    lax.fori_loop(1, cols, start_first, 0)
+    parts_buf[0] = x_ref[:, :, window(col)]
+    lax.fori_loop(1, cols, finish_first, 0)
+    full[:, :, window(col)] = lax.fori_loop(1, cols, add, parts_buf[col])
+    lax.fori_loop(1, cols, start_second, 0)
+    lax.fori_loop(1, cols, finish_second, 0)
+    o_ref[...] = full[...]
+
+
+def col_reduce(partial_sum, collective_id):
+    cols = lax.axis_size("col")
+    parts, fields, elements = partial_sum.shape
+    width = elements // cols
+    return pl.pallas_call(
+        partial(reduce_kernel, cols),
+        out_shape=jax.ShapeDtypeStruct(partial_sum.shape, jnp.float32),
+        in_specs=[pl.BlockSpec(memory_space=pltpu.VMEM)],
+        out_specs=pl.BlockSpec(memory_space=pltpu.VMEM),
+        scratch_shapes=[
+            pltpu.VMEM((cols, parts, fields, width), jnp.float32),
+            pltpu.VMEM((parts, fields, elements), jnp.float32),
+            pltpu.SemaphoreType.DMA((cols,)),
+            pltpu.SemaphoreType.DMA((cols,)),
+            pltpu.SemaphoreType.DMA((cols,)),
+            pltpu.SemaphoreType.DMA((cols,)),
+        ],
+        compiler_params=pltpu.CompilerParams(collective_id=collective_id, has_side_effects=True),
+    )(partial_sum)
+
+
 def row_psum(ids, *arrays):
     flat = [a.reshape(-1) for a in arrays]
     sizes = [f.shape[0] for f in flat]
@@ -279,7 +374,8 @@
         near_pieces, far_pieces = gather_pieces(rounded, blocks, half_band, width, 16 + len(ids))
         ids.append(None)
         total = operator_terms(near_pieces, far_pieces)
-        summed = lax.psum(total, "col")
+        summed = col_reduce(total, 32 + len(ids))
+        ids.append(None)
         return summed + diagonal[None, None, :] * vector
 
     lower_first = jnp.linalg.cholesky(row_psum(ids, inner_products(incident, incident)))

time: 385 us -> 277 us (0.72)
  waiting for transfers between devices: 122 us -> 0 us
  Pallas kernels: 169 us -> 197 us
  between operations: 14.7 us -> 1.34 us
    psum x2 -> x0, waiting for transfers between devices: 122 us -> none  [apply_operator(): summed = lax.psum(total, 'col')]
    pallas_call x0 -> x2, Pallas kernels: none -> 31.6 us  [col_reduce(): pl.pallas_call(partial(reduce_kernel, cols), out_shape=jax.ShapeDtypeStru...]
  transfers between devices with their start and end apart: 2 -> 0, of which waited for: 2 -> 0; matrix products, arithmetic and copies ran while one was open for 0% -> 0% of each run, Pallas kernels for 0% -> 0%
where the time goes in v4:
time: 277 us; the launch traced here: 275 us
  Pallas kernels  197 us (71%)
  other arithmetic  31.8 us (11%)
  matrix products  25.5 us (9%)
  local copies, waits for them, and re-layouts  19.6 us (7%)
    pallas_call x6, Pallas kernels, row_allreduce(): pl.pallas_call(partial(allreduce_kernel, n), out_shape=jax.ShapeDtypeStru...  103 us
    pallas_call x2, Pallas kernels, gather_pieces(): pl.pallas_call(partial(gather_kernel, rows, cols, blocks, half), out_shap...  61.8 us
    pallas_call x2, Pallas kernels, col_reduce(): pl.pallas_call(partial(reduce_kernel, cols), out_shape=jax.ShapeDtypeStru...  31.6 us
    another operation x6, other arithmetic, lower_inverse(): lax.linalg.triangular_solve(lower, identity, left_side=True, lower=True)  12.9 us
    dot_general x7, matrix products, combine_rows(): return jnp.einsum('st,ctn->csn', matrix, vectors, precision=highest)  7.32 us
    another operation x3, other arithmetic, body(): factor_inverse = lower_inverse(jnp.linalg.cholesky(normal))  7.26 us
    dot_general x6, matrix products, inner_products(): return jnp.einsum('csn,ctn->st', first, second, precision=highest)  6.69 us

profile of v4, /device:TPU:24, one launch (start us, length us, event | category | flops | bytes accessed | tf_op | source)
XLA Modules:
  0.0 275.2 jit_solution(16726809022106079017)
XLA Ops:
  0.7 1.7 convolution_bitcast_fusion.14
  3.1 19.2 %shard_map.95 = f32[16,128]{1,0:T(8,128)} custom-call(f32[16,128]{1,0:T(8,128)} %pad_bitcast_fusion.4.x_ref), custom_call_target="tpu_custom_call" | custom-call | tf_op jit(solution)/shard_map/pallas_call | solution.py:58
  23.2 3.3 %cholesky.81 = f32[36,36]{1,0:T(8,128)S(1)} custom-call(f32[36,36]{1,0:T(8,128)S(1)} %fusion.96), custom_call_target="Cholesky" | custom-call | tf_op jit(solution)/shard_map/jit(cholesky)/cholesky | solution.py:381
  27.9 2.8 %custom-call.15 = f32[1,36,36]{1,2,0:T(8,128)S(1)} custom-call(f32[1,36,36]{2,1,0:T(8,128)S(1)} %select_bitcast_fusion.1), custom_call_target="InvertDiagBlocksLowerTriangular" | custom-call | tf_op jit(solution)/shard_map/triangular_solve/custom-call.2 | solution.py:317
  31.0 2.1 fusion.131
  33.1 1.3 gather_fusion
  35.2 30.3 %shard_map.96 = (bf16[8,2,36,128]{3,2,1,0:T(8,128)(2,1)}, bf16[4,2,36,1024]{3,2,1,0:T(8,128)(2,1)}) custom-call(bf16[2,36,1024]{2,1,0:T(8,128)(2,1)} %get-tuple-element.112.v_ref), custom_call_target="tpu_custom_call" | custom-call | tf_op jit(solution)/shard_map/pallas_call | solution.py:165
  65.5 1.0 fusion.66
  67.5 1.0 slice_bitcast_fusion.3
  69.9 1.0 copy-done.7
  70.9 2.1 fusion.23.x_ref
  73.0 15.3 %shard_map.97 = f32[2,36,1024]{2,1,0:T(8,128)} custom-call(f32[2,36,1024]{2,1,0:T(8,128)} %fusion.23.x_ref), custom_call_target="tpu_custom_call" | custom-call | tf_op jit(solution)/shard_map/pallas_call | solution.py:264
  88.3 1.4 convolution_bitcast_fusion.12
  90.4 16.8 %shard_map.98 = f32[16,128]{1,0:T(8,128)} custom-call(f32[16,128]{1,0:T(8,128)} %pad_bitcast_fusion.3.x_ref), custom_call_target="tpu_custom_call" | custom-call | tf_op jit(solution)/shard_map/pallas_call | solution.py:58
  108.0 1.4 fusion.19
  110.5 14.9 %shard_map.99 = f32[16,128]{1,0:T(8,128)} custom-call(f32[16,128]{1,0:T(8,128)} %pad_bitcast_fusion.2.x_ref), custom_call_target="tpu_custom_call" | custom-call | tf_op jit(solution)/shard_map/pallas_call | solution.py:58
  126.4 3.3 %cholesky.92 = f32[36,36]{1,0:T(8,128)S(1)} custom-call(f32[36,36]{1,0:T(8,128)S(1)} %copy.44), custom_call_target="Cholesky" | custom-call | tf_op jit(solution)/shard_map/jit(cholesky)/cholesky | solution.py:387
  130.9 2.8 %custom-call.16 = f32[1,36,36]{1,2,0:T(8,128)S(1)} custom-call(f32[1,36,36]{2,1,0:T(8,128)S(1)} %select_bitcast_fusion), custom_call_target="InvertDiagBlocksLowerTriangular" | custom-call | tf_op jit(solution)/shard_map/triangular_solve/custom-call.2 | solution.py:317
  133.9 1.1 fusion.132
  135.0 31.5 %shard_map.100 = (bf16[8,2,36,128]{3,2,1,0:T(8,128)(2,1)}, bf16[4,2,36,1024]{3,2,1,0:T(8,128)(2,1)}) custom-call(bf16[2,36,1024]{2,1,0:T(8,128)(2,1)} %get-tuple-element.114.v_ref), custom_call_target="tpu_custom_call" | custom-call | tf_op jit(solution)/shard_map/pallas_call | solution.py:165
  166.5 1.0 fusion.65
  170.8 1.0 copy-done.8
  171.9 2.1 fusion.20.x_ref
  174.0 16.4 %shard_map.101 = f32[2,36,1024]{2,1,0:T(8,128)} custom-call(f32[2,36,1024]{2,1,0:T(8,128)} %fusion.20.x_ref), custom_call_target="tpu_custom_call" | custom-call | tf_op jit(solution)/shard_map/pallas_call | solution.py:264
  190.4 1.4 convolution_bitcast_fusion.9
  191.9 1.4 convolution_bitcast_fusion.8
  194.1 19.5 %shard_map.102 = f32[24,128]{1,0:T(8,128)} custom-call(f32[24,128]{1,0:T(8,128)} %bitcast.348), custom_call_target="tpu_custom_call" | custom-call | tf_op jit(solution)/shard_map/pallas_call | solution.py:58
  214.5 1.4 fusion.18
  217.6 15.9 %shard_map.103 = f32[16,128]{1,0:T(8,128)} custom-call(f32[16,128]{1,0:T(8,128)} %pad_bitcast_fusion.1.x_ref), custom_call_target="tpu_custom_call" | custom-call | tf_op jit(solution)/shard_map/pallas_call | solution.py:58
  236.6 6.6 %cholesky.42 = f32[72,72]{1,0:T(8,128)S(1)} custom-call(f32[72,72]{1,0:T(8,128)S(1)} %fusion.85), custom_call_target="Cholesky" | custom-call | tf_op jit(solution)/shard_map/jit(cholesky)/cholesky | solution.py:410
  244.5 5.5 %custom-call.11 = f32[1,72,72]{1,2,0:T(8,128)S(1)} custom-call(f32[1,72,72]{2,1,0:T(8,128)S(1)} %fusion.82), custom_call_target="InvertDiagBlocksLowerTriangular" | custom-call | tf_op jit(solution)/shard_map/triangular_solve | solution.py:317
  256.6 17.1 %shard_map.104 = f32[24,128]{1,0:T(8,128)} custom-call(f32[24,128]{1,0:T(8,128)} %pad_bitcast_fusion.x_ref), custom_call_target="tpu_custom_call" | custom-call | tf_op jit(solution)/shard_map/pallas_call | solution.py:58
  (116 shorter events, 30.2 us)
Async XLA Ops:
  0.6 68.7 %copy-start = (bf16[1,4,2,64,1024]{4,3,2,1,0:T(8,128)(2,1)S(1)}, bf16[1,4,2,64,1024]{4,3,2,1,0:T(8,128)(2,1)}, u32[]{:S(2)}) copy-start(bf16[1,4,2,64,1024]{4,3,2,1,0:T(8,128)(2,1)} %param.26) | copy-start | bytes 3145732
  0.6 68.0 %copy-start.9 = (bf16[1,4,2,64,1024]{4,3,2,1,0:T(8,128)(2,1)S(1)}, bf16[1,4,2,64,1024]{4,3,2,1,0:T(8,128)(2,1)}, u32[]{:S(2)}) copy-start(bf16[1,4,2,64,1024]{4,3,2,1,0:T(8,128)(2,1)} %param.27) | copy-start | bytes 3145732
  68.5 1.2 copy-start.1
  68.5 1.2 copy-start.4
  68.7 2.2 copy-start.7
  69.6 18.6 %copy-start.5 = (f32[1024]{0:T(1024)S(1)}, f32[1024]{0:T(1024)}, u32[]{:S(2)}) copy-start(f32[1024]{0:T(1024)} %param.24) | copy-start | bytes 12292
  169.5 1.1 copy-start.3
  169.7 2.2 copy-start.8
  174.0 61.0 %copy-start.6 = (f32[16,128]{1,0:T(8,128)S(1)}, f32[16,128]{1,0:T(8,128)}, u32[]{:S(2)}) copy-start(f32[16,128]{1,0:T(8,128)} %shard_map.98) | copy-start | bytes 24580
  191.8 62.6 %copy-start.2 = (f32[2,36,1024]{2,0,1:T(2,128)S(1)}, f32[2,36,1024]{2,0,1:T(2,128)}, u32[]{:S(2)}) copy-start(f32[2,36,1024]{2,0,1:T(2,128)} %param.30) | copy-start | bytes 884740

commit v5 on v4

--- a/solution.py
+++ b/solution.py
@@ -381,17 +381,39 @@
     lower_first = jnp.linalg.cholesky(row_psum(ids, inner_products(incident, incident)))
     basis_one = combine_rows(lower_inverse(lower_first), incident)
     image = apply_operator(basis_one)
-    coupling_one = row_psum(ids, inner_products(image, basis_one))
+    coupling_one, harmonics_one, self_one = row_psum(
+        ids,
+        inner_products(image, basis_one),
+        project(harmonics, basis_one),
+        inner_products(basis_one, basis_one),
+    )
     rest = image - combine_rows(coupling_one, basis_one)
     gram_one = row_psum(ids, inner_products(rest, rest))
     lower_second = jnp.linalg.cholesky(gram_one)
     basis_two = combine_rows(lower_inverse(lower_second), rest)
     image = apply_operator(basis_two)
-    coupling_onetwo, coupling_two = row_psum(
-        ids, inner_products(image, basis_one), inner_products(image, basis_two)
-    )
-    rest = image - combine_rows(coupling_onetwo, basis_one) - combine_rows(coupling_two, basis_two)
-    gram_two = row_psum(ids, inner_products(rest, rest))
+    coupling_onetwo, coupling_two, image_gram, cross, self_two, harmonics_two = row_psum(
+        ids,
+        inner_products(image, basis_one),
+        inner_products(image, basis_two),
+        inner_products(image, image),
+        inner_products(basis_one, basis_two),
+        inner_products(basis_two, basis_two),
+        project(harmonics, basis_two),
+    )
+    coupling = jnp.concatenate([coupling_onetwo, coupling_two], axis=1)
+    basis_gram = jnp.concatenate(
+        [
+            jnp.concatenate([self_one, cross], axis=1),
+            jnp.concatenate([cross.T, self_two], axis=1),
+        ],
+        axis=0,
+    )
+    gram_two = (
+        image_gram
+        - 2.0 * matmul(coupling, coupling.T)
+        + matmul(coupling, matmul(basis_gram, coupling.T))
+    )
     upper_left = matmul(coupling_one, coupling_one.T) + gram_one
     upper_right = matmul(coupling_one, coupling_onetwo.T) + matmul(lower_second, coupling_two.T)
     lower_right = (
@@ -412,7 +434,9 @@
     first_weights = weights[:, :fields]
     second_weights = weights[:, fields:]
     solution = combine_rows(first_weights, basis_one) + combine_rows(second_weights, basis_two)
-    coefficients = row_psum(ids, project(harmonics, solution))
+    coefficients = jnp.einsum(
+        "cmt,st->cms", harmonics_one, first_weights, precision=highest
+    ) + jnp.einsum("cmt,st->cms", harmonics_two, second_weights, precision=highest)
     return (solution, coefficients)
 
 

time: 277 us -> 274 us (0.989)
  Pallas kernels: 197 us -> 191 us
  matrix products: 25.5 us -> 28.9 us
  local copies, waits for them, and re-layouts: 19.6 us -> 16.8 us
    pallas_call x6 -> x4, Pallas kernels: 103 us -> 98 us  [row_allreduce(): pl.pallas_call(partial(allreduce_kernel, n), out_shape=jax.ShapeDtypeStru...]
    dot_general x7 -> x5, matrix products: 7.32 us -> 4.54 us  [combine_rows(): return jnp.einsum('st,ctn->csn', matrix, vectors, precision=highest)]
    dot_general x6 -> x9, matrix products: 6.69 us -> 9 us  [inner_products(): return jnp.einsum('csn,ctn->st', first, second, precision=highest)]
where the time goes in v5:
time: 274 us; the launch traced here: 271 us
  Pallas kernels  191 us (70%)
  other arithmetic  32.3 us (12%)
  matrix products  28.9 us (11%)
  local copies, waits for them, and re-layouts  16.8 us (6%)
    pallas_call x4, Pallas kernels, row_allreduce(): pl.pallas_call(partial(allreduce_kernel, n), out_shape=jax.ShapeDtypeStru...  98 us
    pallas_call x2, Pallas kernels, gather_pieces(): pl.pallas_call(partial(gather_kernel, rows, cols, blocks, half), out_shap...  62.4 us
    pallas_call x2, Pallas kernels, col_reduce(): pl.pallas_call(partial(reduce_kernel, cols), out_shape=jax.ShapeDtypeStru...  30.6 us
    another operation x6, other arithmetic, lower_inverse(): lax.linalg.triangular_solve(lower, identity, left_side=True, lower=True)  13.1 us
    dot_general x9, matrix products, inner_products(): return jnp.einsum('csn,ctn->st', first, second, precision=highest)  9 us
    another operation x3, other arithmetic, body(): factor_inverse = lower_inverse(jnp.linalg.cholesky(normal))  7.26 us

profile of v5, /device:TPU:24, one launch (start us, length us, event | category | flops | bytes accessed | tf_op | source)
XLA Modules:
  0.0 270.5 jit_solution(3182504549641127318)
XLA Ops:
  0.7 1.7 convolution_bitcast_fusion.15
  3.0 19.2 %shard_map.95 = f32[16,128]{1,0:T(8,128)} custom-call(f32[16,128]{1,0:T(8,128)} %pad_bitcast_fusion.1.x_ref), custom_call_target="tpu_custom_call" | custom-call | tf_op jit(solution)/shard_map/pallas_call | solution.py:58
  23.2 3.3 %cholesky.81 = f32[36,36]{1,0:T(8,128)S(1)} custom-call(f32[36,36]{1,0:T(8,128)S(1)} %fusion.106), custom_call_target="Cholesky" | custom-call | tf_op jit(solution)/shard_map/jit(cholesky)/cholesky | solution.py:381
  27.9 2.8 %custom-call.15 = f32[1,36,36]{1,2,0:T(8,128)S(1)} custom-call(f32[1,36,36]{2,1,0:T(8,128)S(1)} %select_bitcast_fusion.1), custom_call_target="InvertDiagBlocksLowerTriangular" | custom-call | tf_op jit(solution)/shard_map/triangular_solve/custom-call.2 | solution.py:317
  30.9 2.1 fusion.152
  33.1 30.4 %shard_map.96 = (bf16[8,2,36,128]{3,2,1,0:T(8,128)(2,1)}, bf16[4,2,36,1024]{3,2,1,0:T(8,128)(2,1)}) custom-call(bf16[2,36,1024]{2,1,0:T(8,128)(2,1)} %get-tuple-element.118.v_ref), custom_call_target="tpu_custom_call" | custom-call | tf_op jit(solution)/shard_map/pallas_call | solution.py:165
  63.4 1.0 fusion.67
  64.4 1.0 slice_bitcast_fusion.1
  65.4 1.0 slice_bitcast_fusion.3
  67.4 2.0 fusion.42
  70.0 2.1 fusion.21.x_ref
  72.2 15.3 %shard_map.97 = f32[2,36,1024]{2,1,0:T(8,128)} custom-call(f32[2,36,1024]{2,1,0:T(8,128)} %fusion.21.x_ref), custom_call_target="tpu_custom_call" | custom-call | tf_op jit(solution)/shard_map/pallas_call | solution.py:264
  87.4 1.4 convolution_bitcast_fusion.13
  91.8 27.9 %shard_map.98 = f32[48,128]{1,0:T(8,128)} custom-call(f32[48,128]{1,0:T(8,128)} %bitcast.357), custom_call_target="tpu_custom_call" | custom-call | tf_op jit(solution)/shard_map/pallas_call | solution.py:58
  122.2 14.6 %shard_map.99 = f32[16,128]{1,0:T(8,128)} custom-call(f32[16,128]{1,0:T(8,128)} %pad_bitcast_fusion.x_ref), custom_call_target="tpu_custom_call" | custom-call | tf_op jit(solution)/shard_map/pallas_call | solution.py:58
  137.7 3.3 %cholesky.92 = f32[36,36]{1,0:T(8,128)S(1)} custom-call(f32[36,36]{1,0:T(8,128)S(1)} %copy.51), custom_call_target="Cholesky" | custom-call | tf_op jit(solution)/shard_map/jit(cholesky)/cholesky | solution.py:392
  142.5 2.8 %custom-call.16 = f32[1,36,36]{1,2,0:T(8,128)S(1)} custom-call(f32[1,36,36]{2,1,0:T(8,128)S(1)} %select_bitcast_fusion), custom_call_target="InvertDiagBlocksLowerTriangular" | custom-call | tf_op jit(solution)/shard_map/triangular_solve/custom-call.2 | solution.py:317
  145.5 1.1 fusion.153
  147.9 32.0 %shard_map.100 = (bf16[8,2,36,128]{3,2,1,0:T(8,128)(2,1)}, bf16[4,2,36,1024]{3,2,1,0:T(8,128)(2,1)}) custom-call(bf16[2,36,1024]{2,1,0:T(8,128)(2,1)} %get-tuple-element.120.v_ref), custom_call_target="tpu_custom_call" | custom-call | tf_op jit(solution)/shard_map/pallas_call | solution.py:165
  179.9 1.0 broadcast_select_fusion
  181.0 1.0 fusion.66
  182.0 1.0 slice_bitcast_fusion
  183.0 1.0 slice_bitcast_fusion.2
  185.2 1.0 copy-done.8
  186.2 2.1 fusion.18.x_ref
  188.4 15.3 %shard_map.101 = f32[2,36,1024]{2,1,0:T(8,128)} custom-call(f32[2,36,1024]{2,1,0:T(8,128)} %fusion.18.x_ref), custom_call_target="tpu_custom_call" | custom-call | tf_op jit(solution)/shard_map/pallas_call | solution.py:264
  203.7 1.5 convolution_bitcast_fusion.7
  205.3 1.4 convolution_bitcast_fusion.8
  206.8 1.4 convolution_bitcast_fusion.9
  210.0 36.4 %shard_map.102 = f32[72,128]{1,0:T(8,128)} custom-call(f32[72,128]{1,0:T(8,128)} %bitcast.354), custom_call_target="tpu_custom_call" | custom-call | tf_op jit(solution)/shard_map/pallas_call | solution.py:58
  250.6 6.6 %cholesky.42 = f32[72,72]{1,0:T(8,128)S(1)} custom-call(f32[72,72]{1,0:T(8,128)S(1)} %fusion.96), custom_call_target="Cholesky" | custom-call | tf_op jit(solution)/shard_map/jit(cholesky)/cholesky | solution.py:432
  258.5 5.5 %custom-call.11 = f32[1,72,72]{1,2,0:T(8,128)S(1)} custom-call(f32[1,72,72]{2,1,0:T(8,128)S(1)} %fusion.85), custom_call_target="InvertDiagBlocksLowerTriangular" | custom-call | tf_op jit(solution)/shard_map/triangular_solve | solution.py:317
  (133 shorter events, 29.0 us)
Async XLA Ops:
  0.6 68.8 %copy-start = (bf16[1,4,2,64,1024]{4,3,2,1,0:T(8,128)(2,1)S(1)}, bf16[1,4,2,64,1024]{4,3,2,1,0:T(8,128)(2,1)}, u32[]{:S(2)}) copy-start(bf16[1,4,2,64,1024]{4,3,2,1,0:T(8,128)(2,1)} %param.26) | copy-start | bytes 3145732
  0.6 66.0 %copy-start.1 = (s32[1,8]{1,0:T(1,128)S(1)}, s32[1,8]{1,0:T(1,128)}, u32[]{:S(2)}) copy-start(s32[1,8]{1,0:T(1,128)} %param.28) | copy-start | bytes 100
  0.7 66.6 %copy-start.10 = (s32[1,4]{1,0:T(1,128)S(1)}, s32[1,4]{1,0:T(1,128)}, u32[]{:S(2)}) copy-start(s32[1,4]{1,0:T(1,128)} %param.29) | copy-start | bytes 52
  66.6 3.2 %copy-start.4 = (bf16[8,2,36,128]{3,2,1,0:T(8,128)(2,1)S(1)}, bf16[8,2,36,128]{3,2,1,0:T(8,128)(2,1)}, u32[]{:S(2)}) copy-start(bf16[8,2,36,128]{3,2,1,0:T(8,128)(2,1)} %get-tuple-element.12) | copy-start | bytes 442372
  67.3 2.7 %copy-start.7 = (bf16[1,8,2,1024,128]{4,3,2,1,0:T(8,128)(2,1)S(1)}, bf16[1,8,2,1024,128]{4,3,2,1,0:T(8,128)(2,1)}, u32[]{:S(2)}) copy-start(bf16[1,8,2,1024,128]{4,3,2,1,0:T(8,128)(2,1)} %param.25) | copy-start | bytes 12582916
  69.8 17.6 %copy-start.6 = (f32[1024]{0:T(1024)S(1)}, f32[1024]{0:T(1024)}, u32[]{:S(2)}) copy-start(f32[1024]{0:T(1024)} %param.24) | copy-start | bytes 12292
  69.9 19.1 %copy-start.3 = (f32[2,36,1024]{2,0,1:T(2,128)S(1)}, f32[2,36,1024]{2,0,1:T(2,128)}, u32[]{:S(2)}) copy-start(f32[2,36,1024]{2,0,1:T(2,128)} %param.30) | copy-start | bytes 884740
  87.4 33.2 %copy-start.2 = (f32[2,36,1024]{2,1,0:T(8,128)S(1)}, f32[2,36,1024]{2,1,0:T(8,128)}, u32[]{:S(2)}) copy-start(f32[2,36,1024]{2,1,0:T(8,128)} %shard_map.97) | copy-start | bytes 884740
  142.5 41.7 %copy-start.9 = (bf16[1,4,2,64,1024]{4,3,2,1,0:T(8,128)(2,1)S(1)}, bf16[1,4,2,64,1024]{4,3,2,1,0:T(8,128)(2,1)}, u32[]{:S(2)}) copy-start(bf16[1,4,2,64,1024]{4,3,2,1,0:T(8,128)(2,1)} %param.27) | copy-start | bytes 3145732
  184.0 2.2 copy-start.8
  188.4 78.2 %copy-start.5 = (f32[48,128]{1,0:T(8,128)S(1)}, f32[48,128]{1,0:T(8,128)}, u32[]{:S(2)}) copy-start(f32[48,128]{1,0:T(8,128)} %shard_map.98) | copy-start | bytes 73732

commit v6 on v5

--- a/solution.py
+++ b/solution.py
@@ -11,59 +11,99 @@
 MESH = pl.DeviceIdType.MESH
 
 
-def allreduce_kernel(n, x_ref, o_ref, buf, send_sems, recv_sems):
+def allreduce_kernel(inner, outer, x_ref, o_ref, buf, partial_buf,
+                     first_send, first_recv, second_send, second_recv):
     me = lax.axis_index("row")
     col = lax.axis_index("col")
+    high = me // inner
+    low = me % inner
     barrier = pltpu.get_barrier_semaphore()
 
-    def peer(d):
-        return (lax.rem(me + d, n), col)
-
-    def copy(d):
+    def inner_peer(d):
+        return (high * inner + lax.rem(low + d, inner), col)
+
+    def outer_peer(d):
+        return (lax.rem(high + d, outer) * inner + low, col)
+
+    def first(d):
         return pltpu.make_async_remote_copy(
             src_ref=x_ref,
             dst_ref=buf.at[d],
-            send_sem=send_sems.at[d],
-            recv_sem=recv_sems.at[d],
-            device_id=peer(d),
-            device_id_type=MESH,
-        )
-
-    def greet(d, carry):
-        pl.semaphore_signal(barrier, inc=1, device_id=peer(d), device_id_type=MESH)
-        return carry
-
-    def start(d, carry):
-        copy(d).start()
-        return carry
-
-    def finish(d, carry):
-        copy(d).wait()
-        return carry
-
-    def add(source, total):
-        return total + buf[lax.rem(me + n - source, n)]
-
-    lax.fori_loop(1, n, greet, 0)
-    pl.semaphore_wait(barrier, n - 1)
-    lax.fori_loop(1, n, start, 0)
+            send_sem=first_send.at[d],
+            recv_sem=first_recv.at[d],
+            device_id=inner_peer(d),
+            device_id_type=MESH,
+        )
+
+    def second(d):
+        return pltpu.make_async_remote_copy(
+            src_ref=partial_buf.at[0],
+            dst_ref=partial_buf.at[d],
+            send_sem=second_send.at[d],
+            recv_sem=second_recv.at[d],
+            device_id=outer_peer(d),
+            device_id_type=MESH,
+        )
+
+    def greet_inner(d, carry):
+        pl.semaphore_signal(barrier, inc=1, device_id=inner_peer(d), device_id_type=MESH)
+        return carry
+
+    def greet_outer(d, carry):
+        pl.semaphore_signal(barrier, inc=1, device_id=outer_peer(d), device_id_type=MESH)
+        return carry
+
+    def start_first(d, carry):
+        first(d).start()
+        return carry
+
+    def finish_first(d, carry):
+        first(d).wait()
+        return carry
+
+    def start_second(d, carry):
+        second(d).start()
+        return carry
+
+    def finish_second(d, carry):
+        second(d).wait()
+        return carry
+
+    def add_inner(source, total):
+        return total + buf[lax.rem(low + inner - source, inner)]
+
+    def add_outer(source, total):
+        return total + partial_buf[lax.rem(high + outer - source, outer)]
+
+    lax.fori_loop(1, inner, greet_inner, 0)
+    lax.fori_loop(1, outer, greet_outer, 0)
+    pl.semaphore_wait(barrier, inner - 1 + outer - 1)
+    lax.fori_loop(1, inner, start_first, 0)
     buf[0] = x_ref[...]
-    lax.fori_loop(1, n, finish, 0)
-    o_ref[...] = lax.fori_loop(1, n, add, buf[me])
+    lax.fori_loop(1, inner, finish_first, 0)
+    partial_buf[0] = lax.fori_loop(1, inner, add_inner, buf[low])
+    lax.fori_loop(1, outer, start_second, 0)
+    lax.fori_loop(1, outer, finish_second, 0)
+    o_ref[...] = lax.fori_loop(1, outer, add_outer, partial_buf[high])
 
 
 def row_allreduce(packed, collective_id):
     n = lax.axis_size("row")
+    inner = 8 if n % 8 == 0 else n
+    outer = n // inner
     rows, lanes = packed.shape
     return pl.pallas_call(
-        partial(allreduce_kernel, n),
+        partial(allreduce_kernel, inner, outer),
         out_shape=jax.ShapeDtypeStruct((rows, lanes), jnp.float32),
         in_specs=[pl.BlockSpec(memory_space=pltpu.VMEM)],
         out_specs=pl.BlockSpec(memory_space=pltpu.VMEM),
         scratch_shapes=[
-            pltpu.VMEM((n, rows, lanes), jnp.float32),
-            pltpu.SemaphoreType.DMA((n,)),
-            pltpu.SemaphoreType.DMA((n,)),
+            pltpu.VMEM((inner, rows, lanes), jnp.float32),
+            pltpu.VMEM((outer, rows, lanes), jnp.float32),
+            pltpu.SemaphoreType.DMA((inner,)),
+            pltpu.SemaphoreType.DMA((inner,)),
+            pltpu.SemaphoreType.DMA((outer,)),
+            pltpu.SemaphoreType.DMA((outer,)),
         ],
         compiler_params=pltpu.CompilerParams(collective_id=collective_id, has_side_effects=True),
     )(packed)

time: 274 us -> 240 us (0.88)
  Pallas kernels: 191 us -> 157 us
    pallas_call x4, Pallas kernels: 98 us -> 66.8 us  [row_allreduce(): pl.pallas_call(partial(allreduce_kernel, inner, outer), out_shape=jax.Sha...]
where the time goes in v6:
time: 240 us; the launch traced here: 237 us
  Pallas kernels  157 us (65%)
  other arithmetic  32.3 us (13%)
  matrix products  28.9 us (12%)
  local copies, waits for them, and re-layouts  16.8 us (7%)
    pallas_call x4, Pallas kernels, row_allreduce(): pl.pallas_call(partial(allreduce_kernel, inner, outer), out_shape=jax.Sha...  66.8 us
    pallas_call x2, Pallas kernels, gather_pieces(): pl.pallas_call(partial(gather_kernel, rows, cols, blocks, half), out_shap...  59.8 us
    pallas_call x2, Pallas kernels, col_reduce(): pl.pallas_call(partial(reduce_kernel, cols), out_shape=jax.ShapeDtypeStru...  30.5 us
    another operation x6, other arithmetic, lower_inverse(): lax.linalg.triangular_solve(lower, identity, left_side=True, lower=True)  13.1 us
    dot_general x9, matrix products, inner_products(): return jnp.einsum('csn,ctn->st', first, second, precision=highest)  9.01 us
    another operation x3, other arithmetic, body(): factor_inverse = lower_inverse(jnp.linalg.cholesky(normal))  7.26 us

profile of v6, /device:TPU:24, one launch (start us, length us, event | category | flops | bytes accessed | tf_op | source)
XLA Modules:
  0.0 236.8 jit_solution(13209612276443460476)
XLA Ops:
  0.7 1.7 convolution_bitcast_fusion.15
  3.0 17.3 %shard_map.95 = f32[16,128]{1,0:T(8,128)} custom-call(f32[16,128]{1,0:T(8,128)} %pad_bitcast_fusion.1.x_ref), custom_call_target="tpu_custom_call" | custom-call | tf_op jit(solution)/shard_map/pallas_call | solution.py:95
  21.3 3.3 %cholesky.81 = f32[36,36]{1,0:T(8,128)S(1)} custom-call(f32[36,36]{1,0:T(8,128)S(1)} %fusion.106), custom_call_target="Cholesky" | custom-call | tf_op jit(solution)/shard_map/jit(cholesky)/cholesky | solution.py:421
  26.0 2.8 %custom-call.15 = f32[1,36,36]{1,2,0:T(8,128)S(1)} custom-call(f32[1,36,36]{2,1,0:T(8,128)S(1)} %select_bitcast_fusion.1), custom_call_target="InvertDiagBlocksLowerTriangular" | custom-call | tf_op jit(solution)/shard_map/triangular_solve/custom-call.2 | solution.py:357
  29.0 2.1 fusion.152
  31.2 31.4 %shard_map.96 = (bf16[8,2,36,128]{3,2,1,0:T(8,128)(2,1)}, bf16[4,2,36,1024]{3,2,1,0:T(8,128)(2,1)}) custom-call(bf16[2,36,1024]{2,1,0:T(8,128)(2,1)} %get-tuple-element.118.v_ref), custom_call_target="tpu_custom_call" | custom-call | tf_op jit(solution)/shard_map/pallas_call | solution.py:205
  62.6 1.0 fusion.67
  63.6 1.0 slice_bitcast_fusion.1
  64.6 1.0 slice_bitcast_fusion.3
  66.5 2.0 fusion.42
  69.1 2.1 fusion.21.x_ref
  71.3 14.8 %shard_map.97 = f32[2,36,1024]{2,1,0:T(8,128)} custom-call(f32[2,36,1024]{2,1,0:T(8,128)} %fusion.21.x_ref), custom_call_target="tpu_custom_call" | custom-call | tf_op jit(solution)/shard_map/pallas_call | solution.py:304
  86.1 1.4 convolution_bitcast_fusion.13
  90.4 16.5 %shard_map.98 = f32[48,128]{1,0:T(8,128)} custom-call(f32[48,128]{1,0:T(8,128)} %bitcast.357), custom_call_target="tpu_custom_call" | custom-call | tf_op jit(solution)/shard_map/pallas_call | solution.py:95
  109.4 12.6 %shard_map.99 = f32[16,128]{1,0:T(8,128)} custom-call(f32[16,128]{1,0:T(8,128)} %pad_bitcast_fusion.x_ref), custom_call_target="tpu_custom_call" | custom-call | tf_op jit(solution)/shard_map/pallas_call | solution.py:95
  123.1 3.3 %cholesky.92 = f32[36,36]{1,0:T(8,128)S(1)} custom-call(f32[36,36]{1,0:T(8,128)S(1)} %copy.51), custom_call_target="Cholesky" | custom-call | tf_op jit(solution)/shard_map/jit(cholesky)/cholesky | solution.py:432
  127.8 2.8 %custom-call.16 = f32[1,36,36]{1,2,0:T(8,128)S(1)} custom-call(f32[1,36,36]{2,1,0:T(8,128)S(1)} %select_bitcast_fusion), custom_call_target="InvertDiagBlocksLowerTriangular" | custom-call | tf_op jit(solution)/shard_map/triangular_solve/custom-call.2 | solution.py:357
  130.8 1.1 fusion.153
  133.3 28.5 %shard_map.100 = (bf16[8,2,36,128]{3,2,1,0:T(8,128)(2,1)}, bf16[4,2,36,1024]{3,2,1,0:T(8,128)(2,1)}) custom-call(bf16[2,36,1024]{2,1,0:T(8,128)(2,1)} %get-tuple-element.120.v_ref), custom_call_target="tpu_custom_call" | custom-call | tf_op jit(solution)/shard_map/pallas_call | solution.py:205
  161.7 1.0 broadcast_select_fusion
  162.8 1.0 fusion.66
  163.8 1.0 slice_bitcast_fusion
  164.8 1.0 slice_bitcast_fusion.2
  167.0 1.0 copy-done.8
  168.0 2.1 fusion.18.x_ref
  170.1 15.8 %shard_map.101 = f32[2,36,1024]{2,1,0:T(8,128)} custom-call(f32[2,36,1024]{2,1,0:T(8,128)} %fusion.18.x_ref), custom_call_target="tpu_custom_call" | custom-call | tf_op jit(solution)/shard_map/pallas_call | solution.py:304
  185.9 1.5 convolution_bitcast_fusion.7
  187.5 1.4 convolution_bitcast_fusion.8
  189.0 1.4 convolution_bitcast_fusion.9
  192.3 20.4 %shard_map.102 = f32[72,128]{1,0:T(8,128)} custom-call(f32[72,128]{1,0:T(8,128)} %bitcast.354), custom_call_target="tpu_custom_call" | custom-call | tf_op jit(solution)/shard_map/pallas_call | solution.py:95
  216.8 6.6 %cholesky.42 = f32[72,72]{1,0:T(8,128)S(1)} custom-call(f32[72,72]{1,0:T(8,128)S(1)} %fusion.96), custom_call_target="Cholesky" | custom-call | tf_op jit(solution)/shard_map/jit(cholesky)/cholesky | solution.py:472
  224.7 5.5 %custom-call.11 = f32[1,72,72]{1,2,0:T(8,128)S(1)} custom-call(f32[1,72,72]{2,1,0:T(8,128)S(1)} %fusion.85), custom_call_target="InvertDiagBlocksLowerTriangular" | custom-call | tf_op jit(solution)/shard_map/triangular_solve | solution.py:357
  (133 shorter events, 29.0 us)
Async XLA Ops:
  0.6 67.9 %copy-start = (bf16[1,4,2,64,1024]{4,3,2,1,0:T(8,128)(2,1)S(1)}, bf16[1,4,2,64,1024]{4,3,2,1,0:T(8,128)(2,1)}, u32[]{:S(2)}) copy-start(bf16[1,4,2,64,1024]{4,3,2,1,0:T(8,128)(2,1)} %param.26) | copy-start | bytes 3145732
  0.6 65.1 %copy-start.1 = (s32[1,8]{1,0:T(1,128)S(1)}, s32[1,8]{1,0:T(1,128)}, u32[]{:S(2)}) copy-start(s32[1,8]{1,0:T(1,128)} %param.28) | copy-start | bytes 100
  0.7 65.8 %copy-start.10 = (s32[1,4]{1,0:T(1,128)S(1)}, s32[1,4]{1,0:T(1,128)}, u32[]{:S(2)}) copy-start(s32[1,4]{1,0:T(1,128)} %param.29) | copy-start | bytes 52
  65.7 3.2 %copy-start.4 = (bf16[8,2,36,128]{3,2,1,0:T(8,128)(2,1)S(1)}, bf16[8,2,36,128]{3,2,1,0:T(8,128)(2,1)}, u32[]{:S(2)}) copy-start(bf16[8,2,36,128]{3,2,1,0:T(8,128)(2,1)} %get-tuple-element.12) | copy-start | bytes 442372
  66.4 2.7 %copy-start.7 = (bf16[1,8,2,1024,128]{4,3,2,1,0:T(8,128)(2,1)S(1)}, bf16[1,8,2,1024,128]{4,3,2,1,0:T(8,128)(2,1)}, u32[]{:S(2)}) copy-start(bf16[1,8,2,1024,128]{4,3,2,1,0:T(8,128)(2,1)} %param.25) | copy-start | bytes 12582916
  68.9 17.1 %copy-start.6 = (f32[1024]{0:T(1024)S(1)}, f32[1024]{0:T(1024)}, u32[]{:S(2)}) copy-start(f32[1024]{0:T(1024)} %param.24) | copy-start | bytes 12292
  69.0 18.6 %copy-start.3 = (f32[2,36,1024]{2,0,1:T(2,128)S(1)}, f32[2,36,1024]{2,0,1:T(2,128)}, u32[]{:S(2)}) copy-start(f32[2,36,1024]{2,0,1:T(2,128)} %param.30) | copy-start | bytes 884740
  86.0 21.8 %copy-start.2 = (f32[2,36,1024]{2,1,0:T(8,128)S(1)}, f32[2,36,1024]{2,1,0:T(8,128)}, u32[]{:S(2)}) copy-start(f32[2,36,1024]{2,1,0:T(8,128)} %shard_map.97) | copy-start | bytes 884740
  127.8 38.2 %copy-start.9 = (bf16[1,4,2,64,1024]{4,3,2,1,0:T(8,128)(2,1)S(1)}, bf16[1,4,2,64,1024]{4,3,2,1,0:T(8,128)(2,1)}, u32[]{:S(2)}) copy-start(bf16[1,4,2,64,1024]{4,3,2,1,0:T(8,128)(2,1)} %param.27) | copy-start | bytes 3145732
  165.8 2.2 copy-start.8
  170.1 62.6 %copy-start.5 = (f32[48,128]{1,0:T(8,128)S(1)}, f32[48,128]{1,0:T(8,128)}, u32[]{:S(2)}) copy-start(f32[48,128]{1,0:T(8,128)} %shard_map.98) | copy-start | bytes 73732

commit v7 on v6

--- a/solution.py
+++ b/solution.py
@@ -163,33 +163,44 @@
         first(d).start()
         return carry
 
-    def finish_first(d, carry):
-        first(d).wait()
-        return carry
-
-    def start_second(t, carry):
-        second(t).start()
-        return carry
-
     def finish_second(t, carry):
         second(t).wait()
+        return carry
+
+    def arrived(slot):
+        pltpu.make_async_remote_copy(
+            src_ref=own,
+            dst_ref=slices.at[slot],
+            send_sem=first_send.at[slot],
+            recv_sem=first_recv.at[slot],
+            device_id=row_peer(slot),
+            device_id_type=MESH,
+        ).wait_recv()
+
+    def forward(t, carry):
+        target = lax.rem(col + 1 + t // blocks, cols)
+        arrived(lax.rem(me + rows - blocks * target - t % blocks, rows))
+        second(t).start()
+        return carry
+
+    def sent_first(d, carry):
+        first(d).wait_send()
         return carry
 
     lax.fori_loop(1, rows, greet_row, 0)
     lax.fori_loop(1, cols, greet_col, 0)
     pl.semaphore_wait(barrier, rows - 1 + cols - 1)
     lax.fori_loop(1, rows, start_first, 0)
-    local = pltpu.make_async_copy(own, slices.at[0], local_sems.at[blocks])
-    local.start()
-    lax.fori_loop(1, rows, finish_first, 0)
-    local.wait()
-    lax.fori_loop(0, (cols - 1) * blocks, start_second, 0)
+    pltpu.make_async_copy(own, slices.at[0], first_recv.at[0]).start()
+    lax.fori_loop(0, (cols - 1) * blocks, forward, 0)
     mine = []
     for n in range(blocks):
         slot = lax.rem(me + rows - blocks * col - n, rows)
+        arrived(slot)
         copy = pltpu.make_async_copy(slices.at[slot], far_buf.at[n, :, :, window(col)], local_sems.at[n])
         copy.start()
         mine.append(copy)
+    lax.fori_loop(1, rows, sent_first, 0)
     for k in range(2 * half):
         near_ref[k] = slices[(half - k) % rows]
     lax.fori_loop(0, (cols - 1) * blocks, finish_second, 0)

time: 240 us -> 239 us (level)
    pallas_call x2, Pallas kernels: 59.8 us -> 57.1 us  [gather_pieces(): pl.pallas_call(partial(gather_kernel, rows, cols, blocks, half), out_shap...]
where the time goes in v7:
time: 239 us; the launch traced here: 235 us
  Pallas kernels  156 us (65%)
  other arithmetic  32.3 us (14%)
  matrix products  29 us (12%)
  local copies, waits for them, and re-layouts  16.8 us (7%)
    pallas_call x4, Pallas kernels, row_allreduce(): pl.pallas_call(partial(allreduce_kernel, inner, outer), out_shape=jax.Sha...  68.3 us
    pallas_call x2, Pallas kernels, gather_pieces(): pl.pallas_call(partial(gather_kernel, rows, cols, blocks, half), out_shap...  57.1 us
    pallas_call x2, Pallas kernels, col_reduce(): pl.pallas_call(partial(reduce_kernel, cols), out_shape=jax.ShapeDtypeStru...  30.3 us
    another operation x6, other arithmetic, lower_inverse(): lax.linalg.triangular_solve(lower, identity, left_side=True, lower=True)  13.1 us
    dot_general x9, matrix products, inner_products(): return jnp.einsum('csn,ctn->st', first, second, precision=highest)  9.01 us
    another operation x3, other arithmetic, body(): factor_inverse = lower_inverse(jnp.linalg.cholesky(normal))  7.26 us

profile of v7, /device:TPU:24, one launch (start us, length us, event | category | flops | bytes accessed | tf_op | source)
XLA Modules:
  0.0 235.3 jit_solution(13076013205597172657)
XLA Ops:
  0.7 1.7 convolution_bitcast_fusion.15
  3.0 17.3 %shard_map.95 = f32[16,128]{1,0:T(8,128)} custom-call(f32[16,128]{1,0:T(8,128)} %pad_bitcast_fusion.1.x_ref), custom_call_target="tpu_custom_call" | custom-call | tf_op jit(solution)/shard_map/pallas_call | solution.py:95
  21.3 3.3 %cholesky.81 = f32[36,36]{1,0:T(8,128)S(1)} custom-call(f32[36,36]{1,0:T(8,128)S(1)} %fusion.106), custom_call_target="Cholesky" | custom-call | tf_op jit(solution)/shard_map/jit(cholesky)/cholesky | solution.py:432
  26.0 2.8 %custom-call.15 = f32[1,36,36]{1,2,0:T(8,128)S(1)} custom-call(f32[1,36,36]{2,1,0:T(8,128)S(1)} %select_bitcast_fusion.1), custom_call_target="InvertDiagBlocksLowerTriangular" | custom-call | tf_op jit(solution)/shard_map/triangular_solve/custom-call.2 | solution.py:368
  29.0 2.1 fusion.152
  31.2 29.4 %shard_map.96 = (bf16[8,2,36,128]{3,2,1,0:T(8,128)(2,1)}, bf16[4,2,36,1024]{3,2,1,0:T(8,128)(2,1)}) custom-call(bf16[2,36,1024]{2,1,0:T(8,128)(2,1)} %get-tuple-element.118.v_ref), custom_call_target="tpu_custom_call" | custom-call | tf_op jit(solution)/shard_map/pallas_call | solution.py:216
  60.6 1.0 fusion.67
  61.6 1.0 slice_bitcast_fusion.1
  62.6 1.0 slice_bitcast_fusion.3
  64.5 2.0 fusion.42
  67.2 2.1 fusion.21.x_ref
  69.3 15.2 %shard_map.97 = f32[2,36,1024]{2,1,0:T(8,128)} custom-call(f32[2,36,1024]{2,1,0:T(8,128)} %fusion.21.x_ref), custom_call_target="tpu_custom_call" | custom-call | tf_op jit(solution)/shard_map/pallas_call | solution.py:315
  84.5 1.4 convolution_bitcast_fusion.13
  88.9 17.2 %shard_map.98 = f32[48,128]{1,0:T(8,128)} custom-call(f32[48,128]{1,0:T(8,128)} %bitcast.357), custom_call_target="tpu_custom_call" | custom-call | tf_op jit(solution)/shard_map/pallas_call | solution.py:95
  108.6 12.9 %shard_map.99 = f32[16,128]{1,0:T(8,128)} custom-call(f32[16,128]{1,0:T(8,128)} %pad_bitcast_fusion.x_ref), custom_call_target="tpu_custom_call" | custom-call | tf_op jit(solution)/shard_map/pallas_call | solution.py:95
  122.4 3.3 %cholesky.92 = f32[36,36]{1,0:T(8,128)S(1)} custom-call(f32[36,36]{1,0:T(8,128)S(1)} %copy.51), custom_call_target="Cholesky" | custom-call | tf_op jit(solution)/shard_map/jit(cholesky)/cholesky | solution.py:443
  127.2 2.8 %custom-call.16 = f32[1,36,36]{1,2,0:T(8,128)S(1)} custom-call(f32[1,36,36]{2,1,0:T(8,128)S(1)} %select_bitcast_fusion), custom_call_target="InvertDiagBlocksLowerTriangular" | custom-call | tf_op jit(solution)/shard_map/triangular_solve/custom-call.2 | solution.py:368
  130.2 1.1 fusion.153
  132.6 27.8 %shard_map.100 = (bf16[8,2,36,128]{3,2,1,0:T(8,128)(2,1)}, bf16[4,2,36,1024]{3,2,1,0:T(8,128)(2,1)}) custom-call(bf16[2,36,1024]{2,1,0:T(8,128)(2,1)} %get-tuple-element.120.v_ref), custom_call_target="tpu_custom_call" | custom-call | tf_op jit(solution)/shard_map/pallas_call | solution.py:216
  160.4 1.0 broadcast_select_fusion
  161.5 1.0 fusion.66
  162.5 1.0 slice_bitcast_fusion
  163.5 1.0 slice_bitcast_fusion.2
  165.7 1.0 copy-done.8
  166.7 2.1 fusion.18.x_ref
  168.8 15.1 %shard_map.101 = f32[2,36,1024]{2,1,0:T(8,128)} custom-call(f32[2,36,1024]{2,1,0:T(8,128)} %fusion.18.x_ref), custom_call_target="tpu_custom_call" | custom-call | tf_op jit(solution)/shard_map/pallas_call | solution.py:315
  183.9 1.5 convolution_bitcast_fusion.7
  185.5 1.4 convolution_bitcast_fusion.8
  187.0 1.4 convolution_bitcast_fusion.9
  190.3 20.9 %shard_map.102 = f32[72,128]{1,0:T(8,128)} custom-call(f32[72,128]{1,0:T(8,128)} %bitcast.354), custom_call_target="tpu_custom_call" | custom-call | tf_op jit(solution)/shard_map/pallas_call | solution.py:95
  215.3 6.6 %cholesky.42 = f32[72,72]{1,0:T(8,128)S(1)} custom-call(f32[72,72]{1,0:T(8,128)S(1)} %fusion.96), custom_call_target="Cholesky" | custom-call | tf_op jit(solution)/shard_map/jit(cholesky)/cholesky | solution.py:483
  223.3 5.5 %custom-call.11 = f32[1,72,72]{1,2,0:T(8,128)S(1)} custom-call(f32[1,72,72]{2,1,0:T(8,128)S(1)} %fusion.85), custom_call_target="InvertDiagBlocksLowerTriangular" | custom-call | tf_op jit(solution)/shard_map/triangular_solve | solution.py:368
  (133 shorter events, 29.0 us)
Async XLA Ops:
  0.6 65.9 %copy-start = (bf16[1,4,2,64,1024]{4,3,2,1,0:T(8,128)(2,1)S(1)}, bf16[1,4,2,64,1024]{4,3,2,1,0:T(8,128)(2,1)}, u32[]{:S(2)}) copy-start(bf16[1,4,2,64,1024]{4,3,2,1,0:T(8,128)(2,1)} %param.26) | copy-start | bytes 3145732
  0.6 63.1 %copy-start.1 = (s32[1,8]{1,0:T(1,128)S(1)}, s32[1,8]{1,0:T(1,128)}, u32[]{:S(2)}) copy-start(s32[1,8]{1,0:T(1,128)} %param.28) | copy-start | bytes 100
  0.7 63.8 %copy-start.10 = (s32[1,4]{1,0:T(1,128)S(1)}, s32[1,4]{1,0:T(1,128)}, u32[]{:S(2)}) copy-start(s32[1,4]{1,0:T(1,128)} %param.29) | copy-start | bytes 52
  63.7 3.2 %copy-start.4 = (bf16[8,2,36,128]{3,2,1,0:T(8,128)(2,1)S(1)}, bf16[8,2,36,128]{3,2,1,0:T(8,128)(2,1)}, u32[]{:S(2)}) copy-start(bf16[8,2,36,128]{3,2,1,0:T(8,128)(2,1)} %get-tuple-element.12) | copy-start | bytes 442372
  64.4 2.7 %copy-start.7 = (bf16[1,8,2,1024,128]{4,3,2,1,0:T(8,128)(2,1)S(1)}, bf16[1,8,2,1024,128]{4,3,2,1,0:T(8,128)(2,1)}, u32[]{:S(2)}) copy-start(bf16[1,8,2,1024,128]{4,3,2,1,0:T(8,128)(2,1)} %param.25) | copy-start | bytes 12582916
  66.9 17.6 %copy-start.6 = (f32[1024]{0:T(1024)S(1)}, f32[1024]{0:T(1024)}, u32[]{:S(2)}) copy-start(f32[1024]{0:T(1024)} %param.24) | copy-start | bytes 12292
  67.1 19.0 %copy-start.3 = (f32[2,36,1024]{2,0,1:T(2,128)S(1)}, f32[2,36,1024]{2,0,1:T(2,128)}, u32[]{:S(2)}) copy-start(f32[2,36,1024]{2,0,1:T(2,128)} %param.30) | copy-start | bytes 884740
  84.5 22.5 %copy-start.2 = (f32[2,36,1024]{2,1,0:T(8,128)S(1)}, f32[2,36,1024]{2,1,0:T(8,128)}, u32[]{:S(2)}) copy-start(f32[2,36,1024]{2,1,0:T(8,128)} %shard_map.97) | copy-start | bytes 884740
  127.2 37.5 %copy-start.9 = (bf16[1,4,2,64,1024]{4,3,2,1,0:T(8,128)(2,1)S(1)}, bf16[1,4,2,64,1024]{4,3,2,1,0:T(8,128)(2,1)}, u32[]{:S(2)}) copy-start(bf16[1,4,2,64,1024]{4,3,2,1,0:T(8,128)(2,1)} %param.27) | copy-start | bytes 3145732
  164.5 2.2 copy-start.8
  168.8 62.5 %copy-start.5 = (f32[48,128]{1,0:T(8,128)S(1)}, f32[48,128]{1,0:T(8,128)}, u32[]{:S(2)}) copy-start(f32[48,128]{1,0:T(8,128)} %shard_map.98) | copy-start | bytes 73732

commit v8 on v7

--- a/solution.py
+++ b/solution.py
@@ -125,7 +125,7 @@
     def window(c):
         return pl.ds(pl.multiple_of(c * width, width), width)
 
-    own = v_ref.at[:, :, window(col)]
+    own = v_ref.at[:, window(col)]
 
     def first(d):
         return pltpu.make_async_remote_copy(
@@ -144,7 +144,7 @@
         slot = lax.rem(me + rows - blocks * target - n, rows)
         return pltpu.make_async_remote_copy(
             src_ref=slices.at[slot],
-            dst_ref=far_buf.at[n, :, :, window(col)],
+            dst_ref=far_buf.at[n, :, window(col)],
             send_sem=second_send.at[t],
             recv_sem=second_recv.at[t],
             device_id=col_peer(e),
@@ -197,7 +197,7 @@
     for n in range(blocks):
         slot = lax.rem(me + rows - blocks * col - n, rows)
         arrived(slot)
-        copy = pltpu.make_async_copy(slices.at[slot], far_buf.at[n, :, :, window(col)], local_sems.at[n])
+        copy = pltpu.make_async_copy(slices.at[slot], far_buf.at[n, :, window(col)], local_sems.at[n])
         copy.start()
         mine.append(copy)
     lax.fori_loop(1, rows, sent_first, 0)
@@ -213,17 +213,18 @@
     rows = lax.axis_size("row")
     cols = lax.axis_size("col")
     parts, fields, elements = vector.shape
-    return pl.pallas_call(
+    flat = vector.reshape(parts * fields, elements)
+    near, far = pl.pallas_call(
         partial(gather_kernel, rows, cols, blocks, half),
         out_shape=(
-            jax.ShapeDtypeStruct((2 * half, parts, fields, width), vector.dtype),
-            jax.ShapeDtypeStruct((blocks, parts, fields, elements), vector.dtype),
+            jax.ShapeDtypeStruct((2 * half, parts * fields, width), vector.dtype),
+            jax.ShapeDtypeStruct((blocks, parts * fields, elements), vector.dtype),
         ),
         in_specs=[pl.BlockSpec(memory_space=pltpu.VMEM)],
         out_specs=(pl.BlockSpec(memory_space=pltpu.VMEM), pl.BlockSpec(memory_space=pltpu.VMEM)),
         scratch_shapes=[
-            pltpu.VMEM((rows, parts, fields, width), vector.dtype),
-            pltpu.VMEM((blocks, parts, fields, elements), vector.dtype),
+            pltpu.VMEM((rows, parts * fields, width), vector.dtype),
+            pltpu.VMEM((blocks, parts * fields, elements), vector.dtype),
             pltpu.SemaphoreType.DMA((rows,)),
             pltpu.SemaphoreType.DMA((rows,)),
             pltpu.SemaphoreType.DMA(((cols - 1) * blocks,)),
@@ -231,7 +232,11 @@
             pltpu.SemaphoreType.DMA((blocks + 1,)),
         ],
         compiler_params=pltpu.CompilerParams(collective_id=collective_id, has_side_effects=True),
-    )(vector)
+    )(flat)
+    return (
+        near.reshape(2 * half, parts, fields, width),
+        far.reshape(blocks, parts, fields, elements),
+    )
 
 
 def reduce_kernel(cols, x_ref, o_ref, parts_buf, full, first_send, first_recv, second_send, second_recv):

time: 239 us -> 231 us (0.967)
  Pallas kernels: 156 us -> 151 us
  other arithmetic: 32.3 us -> 29.1 us
    pallas_call x0 -> x4, local copies, waits for them, and re-layouts: none -> 4 us  [gather_pieces(): pl.pallas_call(partial(gather_kernel, rows, cols, blocks, half), out_shap...]
    another operation x8 -> x5, local copies, waits for them, and re-layouts: 4.05 us -> 0.24 us  [complex_lhs(): return jnp.stack([jnp.stack([real, -imag]), jnp.stack([imag, real])])]
    pallas_call x2, Pallas kernels: 57.1 us -> 53.4 us  [gather_pieces(): pl.pallas_call(partial(gather_kernel, rows, cols, blocks, half), out_shap...]
where the time goes in v8:
time: 231 us; the launch traced here: 228 us
  Pallas kernels  151 us (65%)
  other arithmetic  29.1 us (13%)
  matrix products  27.1 us (12%)
  local copies, waits for them, and re-layouts  19 us (8%)
    pallas_call x4, Pallas kernels, row_allreduce(): pl.pallas_call(partial(allreduce_kernel, inner, outer), out_shape=jax.Sha...  68.1 us
    pallas_call x2, Pallas kernels, gather_pieces(): pl.pallas_call(partial(gather_kernel, rows, cols, blocks, half), out_shap...  53.4 us
    pallas_call x2, Pallas kernels, col_reduce(): pl.pallas_call(partial(reduce_kernel, cols), out_shape=jax.ShapeDtypeStru...  29.9 us
    another operation x6, other arithmetic, lower_inverse(): lax.linalg.triangular_solve(lower, identity, left_side=True, lower=True)  12.8 us
    dot_general x9, matrix products, inner_products(): return jnp.einsum('csn,ctn->st', first, second, precision=highest)  9.02 us
    another operation x3, other arithmetic, body(): factor_inverse = lower_inverse(jnp.linalg.cholesky(normal))  7.26 us

profile of v8, /device:TPU:24, one launch (start us, length us, event | category | flops | bytes accessed | tf_op | source)
XLA Modules:
  0.0 228.3 jit_solution(2648796809561644292)
XLA Ops:
  0.7 1.7 convolution_bitcast_fusion.15
  3.0 17.3 %shard_map.95 = f32[16,128]{1,0:T(8,128)} custom-call(f32[16,128]{1,0:T(8,128)} %pad_bitcast_fusion.1.x_ref), custom_call_target="tpu_custom_call" | custom-call | tf_op jit(solution)/shard_map/pallas_call | solution.py:95
  20.4 0.8 reshape.247
  21.3 3.3 %cholesky.81 = f32[36,36]{1,0:T(8,128)S(1)} custom-call(f32[36,36]{1,0:T(8,128)S(1)} %fusion.110), custom_call_target="Cholesky" | custom-call | tf_op jit(solution)/shard_map/jit(cholesky)/cholesky | solution.py:437
  25.8 2.8 %custom-call.15 = f32[1,36,36]{1,2,0:T(8,128)S(1)} custom-call(f32[1,36,36]{2,1,0:T(8,128)S(1)} %select_bitcast_fusion.1), custom_call_target="InvertDiagBlocksLowerTriangular" | custom-call | tf_op jit(solution)/shard_map/triangular_solve/custom-call.2 | solution.py:373
  28.8 1.5 fusion.160
  31.0 27.5 %shard_map.96 = (bf16[8,72,128]{2,1,0:T(8,128)(2,1)}, bf16[4,72,1024]{2,1,0:T(8,128)(2,1)}) custom-call(bf16[72,1024]{1,0:T(8,128)(2,1)} %reshape.248.v_ref), custom_call_target="tpu_custom_call" | custom-call | tf_op jit(solution)/shard_map/pallas_call | solution.py:217
  58.5 1.5 copy.48
  61.4 1.9 fusion.49
  64.1 2.1 fusion.25.x_ref
  66.2 14.9 %shard_map.97 = f32[2,36,1024]{2,1,0:T(8,128)} custom-call(f32[2,36,1024]{2,1,0:T(8,128)} %fusion.25.x_ref), custom_call_target="tpu_custom_call" | custom-call | tf_op jit(solution)/shard_map/pallas_call | solution.py:320
  81.1 1.4 convolution_bitcast_fusion.13
  85.5 17.4 %shard_map.98 = f32[48,128]{1,0:T(8,128)} custom-call(f32[48,128]{1,0:T(8,128)} %bitcast.373), custom_call_target="tpu_custom_call" | custom-call | tf_op jit(solution)/shard_map/pallas_call | solution.py:95
  102.9 0.8 fusion.159
  105.4 12.6 %shard_map.99 = f32[16,128]{1,0:T(8,128)} custom-call(f32[16,128]{1,0:T(8,128)} %pad_bitcast_fusion.x_ref), custom_call_target="tpu_custom_call" | custom-call | tf_op jit(solution)/shard_map/pallas_call | solution.py:95
  118.0 0.8 reshape.260
  119.0 3.3 %cholesky.92 = f32[36,36]{1,0:T(8,128)S(1)} custom-call(f32[36,36]{1,0:T(8,128)S(1)} %copy.59), custom_call_target="Cholesky" | custom-call | tf_op jit(solution)/shard_map/jit(cholesky)/cholesky | solution.py:448
  123.5 2.8 %custom-call.16 = f32[1,36,36]{1,2,0:T(8,128)S(1)} custom-call(f32[1,36,36]{2,1,0:T(8,128)S(1)} %select_bitcast_fusion), custom_call_target="InvertDiagBlocksLowerTriangular" | custom-call | tf_op jit(solution)/shard_map/triangular_solve/custom-call.2 | solution.py:373
  129.0 25.9 %shard_map.100 = (bf16[8,72,128]{2,1,0:T(8,128)(2,1)}, bf16[4,72,1024]{2,1,0:T(8,128)(2,1)}) custom-call(bf16[72,1024]{1,0:T(8,128)(2,1)} %reshape.261.v_ref), custom_call_target="tpu_custom_call" | custom-call | tf_op jit(solution)/shard_map/pallas_call | solution.py:217
  155.0 0.9 copy.60
  156.1 1.5 copy.63
  159.2 1.1 copy-done.8
  160.3 2.1 fusion.22.x_ref
  162.4 15.0 %shard_map.101 = f32[2,36,1024]{2,1,0:T(8,128)} custom-call(f32[2,36,1024]{2,1,0:T(8,128)} %fusion.22.x_ref), custom_call_target="tpu_custom_call" | custom-call | tf_op jit(solution)/shard_map/pallas_call | solution.py:320
  177.5 1.5 convolution_bitcast_fusion.7
  179.1 1.4 convolution_bitcast_fusion.8
  180.6 1.4 convolution_bitcast_fusion.9
  183.8 20.7 %shard_map.102 = f32[72,128]{1,0:T(8,128)} custom-call(f32[72,128]{1,0:T(8,128)} %bitcast.370), custom_call_target="tpu_custom_call" | custom-call | tf_op jit(solution)/shard_map/pallas_call | solution.py:95
  204.6 0.9 slice.99
  208.6 6.6 %cholesky.42 = f32[72,72]{1,0:T(8,128)S(1)} custom-call(f32[72,72]{1,0:T(8,128)S(1)} %fusion.100), custom_call_target="Cholesky" | custom-call | tf_op jit(solution)/shard_map/jit(cholesky)/cholesky | solution.py:488
  216.5 5.5 %custom-call.11 = f32[1,72,72]{1,2,0:T(8,128)S(1)} custom-call(f32[1,72,72]{2,1,0:T(8,128)S(1)} %fusion.89), custom_call_target="InvertDiagBlocksLowerTriangular" | custom-call | tf_op jit(solution)/shard_map/triangular_solve | solution.py:373
  227.3 0.9 copy.79
  (140 shorter events, 26.8 us)
Async XLA Ops:
  0.6 62.8 %copy-start = (bf16[1,4,2,64,1024]{4,3,2,1,0:T(8,128)(2,1)S(1)}, bf16[1,4,2,64,1024]{4,3,2,1,0:T(8,128)(2,1)}, u32[]{:S(2)}) copy-start(bf16[1,4,2,64,1024]{4,3,2,1,0:T(8,128)(2,1)} %param.26) | copy-start | bytes 3145732
  0.6 60.1 %copy-start.1 = (s32[1,8]{1,0:T(1,128)S(1)}, s32[1,8]{1,0:T(1,128)}, u32[]{:S(2)}) copy-start(s32[1,8]{1,0:T(1,128)} %param.28) | copy-start | bytes 100
  28.8 32.6 %copy-start.10 = (s32[1,4]{1,0:T(1,128)S(1)}, s32[1,4]{1,0:T(1,128)}, u32[]{:S(2)}) copy-start(s32[1,4]{1,0:T(1,128)} %param.29) | copy-start | bytes 52
  60.5 3.3 %copy-start.4 = (bf16[8,72,128]{2,1,0:T(8,128)(2,1)S(1)}, bf16[8,72,128]{2,1,0:T(8,128)(2,1)}, u32[]{:S(2)}) copy-start(bf16[8,72,128]{2,1,0:T(8,128)(2,1)} %get-tuple-element.12) | copy-start | bytes 442372
  61.3 2.7 %copy-start.7 = (bf16[1,8,2,1024,128]{4,3,2,1,0:T(8,128)(2,1)S(1)}, bf16[1,8,2,1024,128]{4,3,2,1,0:T(8,128)(2,1)}, u32[]{:S(2)}) copy-start(bf16[1,8,2,1024,128]{4,3,2,1,0:T(8,128)(2,1)} %param.25) | copy-start | bytes 12582916
  63.8 17.3 %copy-start.6 = (f32[1024]{0:T(1024)S(1)}, f32[1024]{0:T(1024)}, u32[]{:S(2)}) copy-start(f32[1024]{0:T(1024)} %param.24) | copy-start | bytes 12292
  63.9 18.7 %copy-start.3 = (f32[2,36,1024]{2,0,1:T(2,128)S(1)}, f32[2,36,1024]{2,0,1:T(2,128)}, u32[]{:S(2)}) copy-start(f32[2,36,1024]{2,0,1:T(2,128)} %param.30) | copy-start | bytes 884740
  81.1 22.7 %copy-start.2 = (f32[2,36,1024]{2,1,0:T(8,128)S(1)}, f32[2,36,1024]{2,1,0:T(8,128)}, u32[]{:S(2)}) copy-start(f32[2,36,1024]{2,1,0:T(8,128)} %shard_map.97) | copy-start | bytes 884740
  129.0 29.2 %copy-start.9 = (bf16[1,4,2,64,1024]{4,3,2,1,0:T(8,128)(2,1)S(1)}, bf16[1,4,2,64,1024]{4,3,2,1,0:T(8,128)(2,1)}, u32[]{:S(2)}) copy-start(bf16[1,4,2,64,1024]{4,3,2,1,0:T(8,128)(2,1)} %param.27) | copy-start | bytes 3145732
  158.1 2.2 copy-start.8
  162.4 61.8 %copy-start.5 = (f32[48,128]{1,0:T(8,128)S(1)}, f32[48,128]{1,0:T(8,128)}, u32[]{:S(2)}) copy-start(f32[48,128]{1,0:T(8,128)} %shard_map.98) | copy-start | bytes 73732

commit v9 on v8

--- a/solution.py
+++ b/solution.py
@@ -253,7 +253,7 @@
 
     def first(e):
         return pltpu.make_async_remote_copy(
-            src_ref=x_ref.at[:, :, window(lax.rem(col + e, cols))],
+            src_ref=x_ref.at[:, window(lax.rem(col + e, cols))],
             dst_ref=parts_buf.at[e],
             send_sem=first_send.at[e],
             recv_sem=first_recv.at[e],
@@ -263,8 +263,8 @@
 
     def second(e):
         return pltpu.make_async_remote_copy(
-            src_ref=full.at[:, :, window(col)],
-            dst_ref=full.at[:, :, window(col)],
+            src_ref=full.at[:, window(col)],
+            dst_ref=full.at[:, window(col)],
             send_sem=second_send.at[e],
             recv_sem=second_recv.at[e],
             device_id=col_peer(e),
@@ -290,8 +290,8 @@
     def finish_second(e, carry):
         second(e).wait_send()
         pltpu.make_async_remote_copy(
-            src_ref=full.at[:, :, window(col)],
-            dst_ref=full.at[:, :, window(lax.rem(col + cols - e, cols))],
+            src_ref=full.at[:, window(col)],
+            dst_ref=full.at[:, window(lax.rem(col + cols - e, cols))],
             send_sem=second_send.at[e],
             recv_sem=second_recv.at[e],
             device_id=col_peer(e),
@@ -305,9 +305,9 @@
     lax.fori_loop(1, cols, greet, 0)
     pl.semaphore_wait(barrier, cols - 1)
     lax.fori_loop(1, cols, start_first, 0)
-    parts_buf[0] = x_ref[:, :, window(col)]
+    parts_buf[0] = x_ref[:, window(col)]
     lax.fori_loop(1, cols, finish_first, 0)
-    full[:, :, window(col)] = lax.fori_loop(1, cols, add, parts_buf[col])
+    full[:, window(col)] = lax.fori_loop(1, cols, add, parts_buf[col])
     lax.fori_loop(1, cols, start_second, 0)
     lax.fori_loop(1, cols, finish_second, 0)
     o_ref[...] = full[...]
@@ -317,21 +317,23 @@
     cols = lax.axis_size("col")
     parts, fields, elements = partial_sum.shape
     width = elements // cols
-    return pl.pallas_call(
+    flat = partial_sum.reshape(parts * fields, elements)
+    summed = pl.pallas_call(
         partial(reduce_kernel, cols),
-        out_shape=jax.ShapeDtypeStruct(partial_sum.shape, jnp.float32),
+        out_shape=jax.ShapeDtypeStruct(flat.shape, jnp.float32),
         in_specs=[pl.BlockSpec(memory_space=pltpu.VMEM)],
         out_specs=pl.BlockSpec(memory_space=pltpu.VMEM),
         scratch_shapes=[
-            pltpu.VMEM((cols, parts, fields, width), jnp.float32),
-            pltpu.VMEM((parts, fields, elements), jnp.float32),
+            pltpu.VMEM((cols, parts * fields, width), jnp.float32),
+            pltpu.VMEM((parts * fields, elements), jnp.float32),
             pltpu.SemaphoreType.DMA((cols,)),
             pltpu.SemaphoreType.DMA((cols,)),
             pltpu.SemaphoreType.DMA((cols,)),
             pltpu.SemaphoreType.DMA((cols,)),
         ],
         compiler_params=pltpu.CompilerParams(collective_id=collective_id, has_side_effects=True),
-    )(partial_sum)
+    )(flat)
+    return summed.reshape(partial_sum.shape)
 
 
 def row_psum(ids, *arrays):

time: 231 us -> 230 us (level)
  matrix products: 27.1 us -> 21.8 us
  local copies, waits for them, and re-layouts: 19 us -> 22.5 us
    dot_general x9, matrix products: 9.02 us -> 4.91 us  [inner_products(): return jnp.einsum('csn,ctn->st', first, second, precision=highest)]
    reshape x0 -> x4, local copies, waits for them, and re-layouts: none -> 3.48 us  [the longest x2 1.99 us: col_reduce(): return summed.reshape(partial_sum.shape)]
where the time goes in v9:
time: 230 us; the launch traced here: 227 us
  Pallas kernels  152 us (66%)
  other arithmetic  29.3 us (13%)
  local copies, waits for them, and re-layouts  22.5 us (10%)
  matrix products  21.8 us (9%)
    pallas_call x4, Pallas kernels, row_allreduce(): pl.pallas_call(partial(allreduce_kernel, inner, outer), out_shape=jax.Sha...  68.8 us
    pallas_call x2, Pallas kernels, gather_pieces(): pl.pallas_call(partial(gather_kernel, rows, cols, blocks, half), out_shap...  53.5 us
    pallas_call x2, Pallas kernels, col_reduce(): pl.pallas_call(partial(reduce_kernel, cols), out_shape=jax.ShapeDtypeStru...  29.5 us
    another operation x6, other arithmetic, lower_inverse(): lax.linalg.triangular_solve(lower, identity, left_side=True, lower=True)  12.9 us
    another operation x3, other arithmetic, body(): factor_inverse = lower_inverse(jnp.linalg.cholesky(normal))  7.26 us
    dot_general x9, matrix products, inner_products(): return jnp.einsum('csn,ctn->st', first, second, precision=highest)  4.91 us

profile of v9, /device:TPU:24, one launch (start us, length us, event | category | flops | bytes accessed | tf_op | source)
XLA Modules:
  0.0 226.9 jit_solution(4625725723549677044)
XLA Ops:
  0.7 1.7 convolution_bitcast_fusion.15
  3.0 17.3 %shard_map.95 = f32[16,128]{1,0:T(8,128)} custom-call(f32[16,128]{1,0:T(8,128)} %pad_bitcast_fusion.1.x_ref), custom_call_target="tpu_custom_call" | custom-call | tf_op jit(solution)/shard_map/pallas_call | solution.py:95
  20.4 0.8 reshape.259
  21.3 3.3 %cholesky.81 = f32[36,36]{1,0:T(8,128)S(1)} custom-call(f32[36,36]{1,0:T(8,128)S(1)} %fusion.110), custom_call_target="Cholesky" | custom-call | tf_op jit(solution)/shard_map/jit(cholesky)/cholesky | solution.py:439
  26.0 2.8 %custom-call.15 = f32[1,36,36]{1,2,0:T(8,128)S(1)} custom-call(f32[1,36,36]{2,1,0:T(8,128)S(1)} %select_bitcast_fusion.1), custom_call_target="InvertDiagBlocksLowerTriangular" | custom-call | tf_op jit(solution)/shard_map/triangular_solve/custom-call.2 | solution.py:375
  29.0 1.5 fusion.160
  31.2 27.5 %shard_map.96 = (bf16[8,72,128]{2,1,0:T(8,128)(2,1)}, bf16[4,72,1024]{2,1,0:T(8,128)(2,1)}) custom-call(bf16[72,1024]{1,0:T(8,128)(2,1)} %reshape.260.v_ref), custom_call_target="tpu_custom_call" | custom-call | tf_op jit(solution)/shard_map/pallas_call | solution.py:217
  58.7 1.5 copy.48
  61.7 1.9 fusion.49
  64.3 1.4 fusion.25
  66.4 14.6 %shard_map.97 = f32[72,1024]{1,0:T(8,128)} custom-call(f32[72,1024]{1,0:T(8,128)} %reshape.263.x_ref), custom_call_target="tpu_custom_call" | custom-call | tf_op jit(solution)/shard_map/pallas_call | solution.py:321
  81.1 1.0 reshape.264
  85.4 17.4 %shard_map.98 = f32[48,128]{1,0:T(8,128)} custom-call(f32[48,128]{1,0:T(8,128)} %bitcast.373), custom_call_target="tpu_custom_call" | custom-call | tf_op jit(solution)/shard_map/pallas_call | solution.py:95
  102.8 0.8 fusion.159
  105.2 12.6 %shard_map.99 = f32[16,128]{1,0:T(8,128)} custom-call(f32[16,128]{1,0:T(8,128)} %pad_bitcast_fusion.x_ref), custom_call_target="tpu_custom_call" | custom-call | tf_op jit(solution)/shard_map/pallas_call | solution.py:95
  117.9 0.8 reshape.274
  118.8 3.3 %cholesky.92 = f32[36,36]{1,0:T(8,128)S(1)} custom-call(f32[36,36]{1,0:T(8,128)S(1)} %copy.59), custom_call_target="Cholesky" | custom-call | tf_op jit(solution)/shard_map/jit(cholesky)/cholesky | solution.py:450
  123.3 2.8 %custom-call.16 = f32[1,36,36]{1,2,0:T(8,128)S(1)} custom-call(f32[1,36,36]{2,1,0:T(8,128)S(1)} %select_bitcast_fusion), custom_call_target="InvertDiagBlocksLowerTriangular" | custom-call | tf_op jit(solution)/shard_map/triangular_solve/custom-call.2 | solution.py:375
  128.8 26.0 %shard_map.100 = (bf16[8,72,128]{2,1,0:T(8,128)(2,1)}, bf16[4,72,1024]{2,1,0:T(8,128)(2,1)}) custom-call(bf16[72,1024]{1,0:T(8,128)(2,1)} %reshape.275.v_ref), custom_call_target="tpu_custom_call" | custom-call | tf_op jit(solution)/shard_map/pallas_call | solution.py:217
  154.8 0.9 copy.60
  155.9 1.5 copy.63
  159.1 1.1 copy-done.7
  160.2 1.4 fusion.22
  162.3 14.9 %shard_map.101 = f32[72,1024]{1,0:T(8,128)} custom-call(f32[72,1024]{1,0:T(8,128)} %reshape.278.x_ref), custom_call_target="tpu_custom_call" | custom-call | tf_op jit(solution)/shard_map/pallas_call | solution.py:321
  177.2 1.0 reshape.279
  181.5 21.5 %shard_map.102 = f32[72,128]{1,0:T(8,128)} custom-call(f32[72,128]{1,0:T(8,128)} %bitcast.370), custom_call_target="tpu_custom_call" | custom-call | tf_op jit(solution)/shard_map/pallas_call | solution.py:95
  203.0 0.9 slice.99
  207.0 6.6 %cholesky.42 = f32[72,72]{1,0:T(8,128)S(1)} custom-call(f32[72,72]{1,0:T(8,128)S(1)} %fusion.100), custom_call_target="Cholesky" | custom-call | tf_op jit(solution)/shard_map/jit(cholesky)/cholesky | solution.py:490
  214.9 5.5 %custom-call.11 = f32[1,72,72]{1,2,0:T(8,128)S(1)} custom-call(f32[1,72,72]{2,1,0:T(8,128)S(1)} %fusion.89), custom_call_target="InvertDiagBlocksLowerTriangular" | custom-call | tf_op jit(solution)/shard_map/triangular_solve | solution.py:375
  220.7 0.8 fusion.114
  221.5 0.8 fusion.116
  226.0 0.9 copy.79
  (142 shorter events, 28.6 us)
Async XLA Ops:
  0.6 63.0 %copy-start = (bf16[1,4,2,64,1024]{4,3,2,1,0:T(8,128)(2,1)S(1)}, bf16[1,4,2,64,1024]{4,3,2,1,0:T(8,128)(2,1)}, u32[]{:S(2)}) copy-start(bf16[1,4,2,64,1024]{4,3,2,1,0:T(8,128)(2,1)} %param.26) | copy-start | bytes 3145732
  0.6 60.3 %copy-start.1 = (s32[1,8]{1,0:T(1,128)S(1)}, s32[1,8]{1,0:T(1,128)}, u32[]{:S(2)}) copy-start(s32[1,8]{1,0:T(1,128)} %param.28) | copy-start | bytes 100
  29.0 32.6 %copy-start.9 = (s32[1,4]{1,0:T(1,128)S(1)}, s32[1,4]{1,0:T(1,128)}, u32[]{:S(2)}) copy-start(s32[1,4]{1,0:T(1,128)} %param.29) | copy-start | bytes 52
  60.7 3.3 %copy-start.3 = (bf16[8,72,128]{2,1,0:T(8,128)(2,1)S(1)}, bf16[8,72,128]{2,1,0:T(8,128)(2,1)}, u32[]{:S(2)}) copy-start(bf16[8,72,128]{2,1,0:T(8,128)(2,1)} %get-tuple-element.12) | copy-start | bytes 442372
  61.6 2.7 %copy-start.6 = (bf16[1,8,2,1024,128]{4,3,2,1,0:T(8,128)(2,1)S(1)}, bf16[1,8,2,1024,128]{4,3,2,1,0:T(8,128)(2,1)}, u32[]{:S(2)}) copy-start(bf16[1,8,2,1024,128]{4,3,2,1,0:T(8,128)(2,1)} %param.25) | copy-start | bytes 12582916
  64.2 17.9 %copy-start.5 = (f32[1024]{0:T(1024)S(1)}, f32[1024]{0:T(1024)}, u32[]{:S(2)}) copy-start(f32[1024]{0:T(1024)} %param.24) | copy-start | bytes 12292
  64.3 18.3 %copy-start.2 = (f32[2,36,1024]{2,0,1:T(2,128)S(1)}, f32[2,36,1024]{2,0,1:T(2,128)}, u32[]{:S(2)}) copy-start(f32[2,36,1024]{2,0,1:T(2,128)} %param.30) | copy-start | bytes 884740
  128.8 29.3 %copy-start.8 = (bf16[1,4,2,64,1024]{4,3,2,1,0:T(8,128)(2,1)S(1)}, bf16[1,4,2,64,1024]{4,3,2,1,0:T(8,128)(2,1)}, u32[]{:S(2)}) copy-start(bf16[1,4,2,64,1024]{4,3,2,1,0:T(8,128)(2,1)} %param.27) | copy-start | bytes 3145732
  158.0 2.2 copy-start.7
  161.6 61.3 %copy-start.4 = (f32[48,128]{1,0:T(8,128)S(1)}, f32[48,128]{1,0:T(8,128)}, u32[]{:S(2)}) copy-start(f32[48,128]{1,0:T(8,128)} %shard_map.98) | copy-start | bytes 73732

commit v10 on v9

--- a/solution.py
+++ b/solution.py
@@ -109,7 +109,14 @@
     )(packed)
 
 
-def gather_kernel(rows, cols, blocks, half, v_ref, near_ref, far_ref, slices, far_buf,
+def gram(left, right):
+    return lax.dot_general(
+        left, right, (((1,), (1,)), ((), ())), precision=highest, preferred_element_type=jnp.float32
+    )
+
+
+def gather_kernel(rows, cols, blocks, half, v_ref, one_ref, cur_ref, harm_ref,
+                  near_ref, far_ref, cross_ref, self_ref, proj_ref, slices, far_buf,
                   first_send, first_recv, second_send, second_recv, local_sems):
     me = lax.axis_index("row")
     col = lax.axis_index("col")
@@ -192,6 +199,10 @@
     pl.semaphore_wait(barrier, rows - 1 + cols - 1)
     lax.fori_loop(1, rows, start_first, 0)
     pltpu.make_async_copy(own, slices.at[0], first_recv.at[0]).start()
+    cross_ref[...] = gram(one_ref[0], cur_ref[0]) + gram(one_ref[1], cur_ref[1])
+    self_ref[...] = gram(cur_ref[0], cur_ref[0]) + gram(cur_ref[1], cur_ref[1])
+    proj_ref[0] = gram(harm_ref[0], cur_ref[0]) + gram(harm_ref[1], cur_ref[1])
+    proj_ref[1] = gram(harm_ref[0], cur_ref[1]) - gram(harm_ref[1], cur_ref[0])
     lax.fori_loop(0, (cols - 1) * blocks, forward, 0)
     mine = []
     for n in range(blocks):
@@ -209,19 +220,22 @@
     far_ref[...] = far_buf[...]
 
 
-def gather_pieces(vector, blocks, half, width, collective_id):
+def gather_pieces(vector, basis_one, basis, harmonics, blocks, half, width, collective_id):
     rows = lax.axis_size("row")
     cols = lax.axis_size("col")
     parts, fields, elements = vector.shape
     flat = vector.reshape(parts * fields, elements)
-    near, far = pl.pallas_call(
+    near, far, cross, self_gram, proj = pl.pallas_call(
         partial(gather_kernel, rows, cols, blocks, half),
         out_shape=(
             jax.ShapeDtypeStruct((2 * half, parts * fields, width), vector.dtype),
             jax.ShapeDtypeStruct((blocks, parts * fields, elements), vector.dtype),
+            jax.ShapeDtypeStruct((fields, fields), jnp.float32),
+            jax.ShapeDtypeStruct((fields, fields), jnp.float32),
+            jax.ShapeDtypeStruct((2, harmonics.shape[1], fields), jnp.float32),
         ),
-        in_specs=[pl.BlockSpec(memory_space=pltpu.VMEM)],
-        out_specs=(pl.BlockSpec(memory_space=pltpu.VMEM), pl.BlockSpec(memory_space=pltpu.VMEM)),
+        in_specs=[pl.BlockSpec(memory_space=pltpu.VMEM)] * 4,
+        out_specs=tuple(pl.BlockSpec(memory_space=pltpu.VMEM) for _ in range(5)),
         scratch_shapes=[
             pltpu.VMEM((rows, parts * fields, width), vector.dtype),
             pltpu.VMEM((blocks, parts * fields, elements), vector.dtype),
@@ -232,10 +246,13 @@
             pltpu.SemaphoreType.DMA((blocks + 1,)),
         ],
         compiler_params=pltpu.CompilerParams(collective_id=collective_id, has_side_effects=True),
-    )(flat)
+    )(flat, basis_one, basis, harmonics)
     return (
         near.reshape(2 * half, parts, fields, width),
         far.reshape(blocks, parts, fields, elements),
+        cross,
+        self_gram,
+        proj,
     )
 
 
@@ -427,37 +444,36 @@
         )
         return near_out + far_out
 
-    def apply_operator(vector):
+    def apply_operator(vector, basis_one):
         rounded = vector.astype(jnp.bfloat16)
-        near_pieces, far_pieces = gather_pieces(rounded, blocks, half_band, width, 16 + len(ids))
+        near_pieces, far_pieces, cross, self_gram, proj = gather_pieces(
+            rounded, basis_one, vector, harmonics, blocks, half_band, width, 16 + len(ids)
+        )
         ids.append(None)
         total = operator_terms(near_pieces, far_pieces)
         summed = col_reduce(total, 32 + len(ids))
         ids.append(None)
-        return summed + diagonal[None, None, :] * vector
+        return summed + diagonal[None, None, :] * vector, cross, self_gram, proj
 
     lower_first = jnp.linalg.cholesky(row_psum(ids, inner_products(incident, incident)))
     basis_one = combine_rows(lower_inverse(lower_first), incident)
-    image = apply_operator(basis_one)
+    image, _, self_one, harmonics_one = apply_operator(basis_one, basis_one)
     coupling_one, harmonics_one, self_one = row_psum(
-        ids,
-        inner_products(image, basis_one),
-        project(harmonics, basis_one),
-        inner_products(basis_one, basis_one),
+        ids, inner_products(image, basis_one), harmonics_one, self_one
     )
     rest = image - combine_rows(coupling_one, basis_one)
     gram_one = row_psum(ids, inner_products(rest, rest))
     lower_second = jnp.linalg.cholesky(gram_one)
     basis_two = combine_rows(lower_inverse(lower_second), rest)
-    image = apply_operator(basis_two)
+    image, cross, self_two, harmonics_two = apply_operator(basis_two, basis_one)
     coupling_onetwo, coupling_two, image_gram, cross, self_two, harmonics_two = row_psum(
         ids,
         inner_products(image, basis_one),
         inner_products(image, basis_two),
         inner_products(image, image),
-        inner_products(basis_one, basis_two),
-        inner_products(basis_two, basis_two),
-        project(harmonics, basis_two),
+        cross,
+        self_two,
+        harmonics_two,
     )
     coupling = jnp.concatenate([coupling_onetwo, coupling_two], axis=1)
     basis_gram = jnp.concatenate(

time: 230 us -> 228 us (level)
    unnamed x25 -> x42, local copies, waits for them, and re-layouts: 2.98 us -> 4.72 us
    dot_general x9 -> x6, matrix products: 4.91 us -> 3.71 us  [inner_products(): return jnp.einsum('csn,ctn->st', first, second, precision=highest)]
where the time goes in v10:
time: 228 us; the launch traced here: 224 us
  Pallas kernels  151 us (66%)
  other arithmetic  29.4 us (13%)
  local copies, waits for them, and re-layouts  22.9 us (10%)
  matrix products  19.7 us (9%)
    pallas_call x4, Pallas kernels, row_allreduce(): pl.pallas_call(partial(allreduce_kernel, inner, outer), out_shape=jax.Sha...  67.5 us
    pallas_call x2, Pallas kernels, gather_pieces(): pl.pallas_call(partial(gather_kernel, rows, cols, blocks, half), out_shap...  54 us
    pallas_call x2, Pallas kernels, col_reduce(): pl.pallas_call(partial(reduce_kernel, cols), out_shape=jax.ShapeDtypeStru...  29.4 us
    another operation x6, other arithmetic, lower_inverse(): lax.linalg.triangular_solve(lower, identity, left_side=True, lower=True)  12.9 us
    another operation x3, other arithmetic, body(): factor_inverse = lower_inverse(jnp.linalg.cholesky(normal))  7.26 us
    unnamed x42, local copies, waits for them, and re-layouts  4.72 us
    dot_general x5, matrix products, combine_rows(): return jnp.einsum('st,ctn->csn', matrix, vectors, precision=highest)  4.66 us

profile of v10, /device:TPU:24, one launch (start us, length us, event | category | flops | bytes accessed | tf_op | source)
XLA Modules:
  0.0 224.4 jit_solution(13210907379805477656)
XLA Ops:
  0.6 1.7 convolution_bitcast_fusion.12
  3.0 17.3 %shard_map.95 = f32[16,128]{1,0:T(8,128)} custom-call(f32[16,128]{1,0:T(8,128)} %pad_bitcast_fusion.1.x_ref), custom_call_target="tpu_custom_call" | custom-call | tf_op jit(solution)/shard_map/pallas_call | solution.py:95
  20.4 0.8 reshape.259
  21.3 3.3 %cholesky.81 = f32[36,36]{1,0:T(8,128)S(1)} custom-call(f32[36,36]{1,0:T(8,128)S(1)} %fusion.102), custom_call_target="Cholesky" | custom-call | tf_op jit(solution)/shard_map/jit(cholesky)/cholesky | solution.py:458
  25.8 2.8 %custom-call.15 = f32[1,36,36]{1,2,0:T(8,128)S(1)} custom-call(f32[1,36,36]{2,1,0:T(8,128)S(1)} %select_bitcast_fusion.1), custom_call_target="InvertDiagBlocksLowerTriangular" | custom-call | tf_op jit(solution)/shard_map/triangular_solve/custom-call.2 | solution.py:392
  28.8 2.2 fusion.151
  31.7 1.8 copy.47.harm_ref
  33.5 27.9 %shard_map.96 = (bf16[8,72,128]{2,1,0:T(8,128)(2,1)}, bf16[4,72,1024]{2,1,0:T(8,128)(2,1)}, f32[36,36]{1,0:T(8,128)}, f32[36,36]{1,0:T(8,128)}, f32[2,36,36]{2,1,0:T(8,128)}) custom-call(bf16[72,1024]{1,0:T(8,128)(2,1)} %reshape.260.v_ref, f32[2,36,1024]{2,1,0:T(8,128)} %get-tuple-element.131.one_ref.cur_ref, ...), custom_call_target="tpu_custom_call" | custom-call | tf_op jit(solution)/shard_map/pallas_call | solution.py:228
  61.4 1.5 copy.51
  64.3 1.9 fusion.49
  67.0 1.4 fusion.25
  69.1 14.7 %shard_map.97 = f32[72,1024]{1,0:T(8,128)} custom-call(f32[72,1024]{1,0:T(8,128)} %reshape.263.x_ref), custom_call_target="tpu_custom_call" | custom-call | tf_op jit(solution)/shard_map/pallas_call | solution.py:338
  83.9 1.0 reshape.264
  86.3 17.4 %shard_map.98 = f32[48,128]{1,0:T(8,128)} custom-call(f32[48,128]{1,0:T(8,128)} %bitcast.317), custom_call_target="tpu_custom_call" | custom-call | tf_op jit(solution)/shard_map/pallas_call | solution.py:95
  103.7 0.8 fusion.150
  106.1 12.6 %shard_map.99 = f32[16,128]{1,0:T(8,128)} custom-call(f32[16,128]{1,0:T(8,128)} %pad_bitcast_fusion.x_ref), custom_call_target="tpu_custom_call" | custom-call | tf_op jit(solution)/shard_map/pallas_call | solution.py:95
  118.7 0.8 reshape.274
  119.7 3.3 %cholesky.92 = f32[36,36]{1,0:T(8,128)S(1)} custom-call(f32[36,36]{1,0:T(8,128)S(1)} %copy.59), custom_call_target="Cholesky" | custom-call | tf_op jit(solution)/shard_map/jit(cholesky)/cholesky | solution.py:466
  124.5 2.8 %custom-call.16 = f32[1,36,36]{1,2,0:T(8,128)S(1)} custom-call(f32[1,36,36]{2,1,0:T(8,128)S(1)} %select_bitcast_fusion), custom_call_target="InvertDiagBlocksLowerTriangular" | custom-call | tf_op jit(solution)/shard_map/triangular_solve/custom-call.2 | solution.py:392
  127.5 1.1 fusion.152
  129.3 26.1 %shard_map.100 = (bf16[8,72,128]{2,1,0:T(8,128)(2,1)}, bf16[4,72,1024]{2,1,0:T(8,128)(2,1)}, f32[36,36]{1,0:T(8,128)}, f32[36,36]{1,0:T(8,128)}, f32[2,36,36]{2,1,0:T(8,128)}) custom-call(bf16[72,1024]{1,0:T(8,128)(2,1)} %reshape.275.v_ref, f32[2,36,1024]{2,1,0:T(8,128)} %get-tuple-element.131.one_ref.cur_ref, f32[2,36,1024]{2,1,0:T(8,128)} %get-tuple-element.133.cur_ref, ...), custom_call_target="tpu_custom_call" | custom-call | tf_op jit(solution)/shard_map/pallas_call | solution.py:228
  155.4 1.5 copy.64
  158.8 1.0 copy-done.15
  159.8 1.4 fusion.22
  162.0 14.7 %shard_map.101 = f32[72,1024]{1,0:T(8,128)} custom-call(f32[72,1024]{1,0:T(8,128)} %reshape.278.x_ref), custom_call_target="tpu_custom_call" | custom-call | tf_op jit(solution)/shard_map/pallas_call | solution.py:338
  176.7 1.0 reshape.279
  180.3 20.2 %shard_map.102 = f32[72,128]{1,0:T(8,128)} custom-call(f32[72,128]{1,0:T(8,128)} %bitcast.314), custom_call_target="tpu_custom_call" | custom-call | tf_op jit(solution)/shard_map/pallas_call | solution.py:95
  200.6 0.9 slice.65
  203.3 0.8 convolution_add_fusion.4
  204.8 6.6 %cholesky.42 = f32[72,72]{1,0:T(8,128)S(1)} custom-call(f32[72,72]{1,0:T(8,128)S(1)} %fusion.92), custom_call_target="Cholesky" | custom-call | tf_op jit(solution)/shard_map/jit(cholesky)/cholesky | solution.py:506
  212.7 5.5 %custom-call.11 = f32[1,72,72]{1,2,0:T(8,128)S(1)} custom-call(f32[1,72,72]{2,1,0:T(8,128)S(1)} %fusion.81), custom_call_target="InvertDiagBlocksLowerTriangular" | custom-call | tf_op jit(solution)/shard_map/triangular_solve | solution.py:392
  221.4 0.9 copy.79
  (143 shorter events, 25.2 us)
Async XLA Ops:
  0.6 65.7 %copy-start = (bf16[1,4,2,64,1024]{4,3,2,1,0:T(8,128)(2,1)S(1)}, bf16[1,4,2,64,1024]{4,3,2,1,0:T(8,128)(2,1)}, u32[]{:S(2)}) copy-start(bf16[1,4,2,64,1024]{4,3,2,1,0:T(8,128)(2,1)} %param.26) | copy-start | bytes 3145732
  31.7 31.9 %copy-start.1 = (s32[1,8]{1,0:T(1,128)S(1)}, s32[1,8]{1,0:T(1,128)}, u32[]{:S(2)}) copy-start(s32[1,8]{1,0:T(1,128)} %param.28) | copy-start | bytes 100
  33.5 30.8 %copy-start.17 = (s32[1,4]{1,0:T(1,128)S(1)}, s32[1,4]{1,0:T(1,128)}, u32[]{:S(2)}) copy-start(s32[1,4]{1,0:T(1,128)} %param.29) | copy-start | bytes 52
  63.4 3.3 %copy-start.5 = (bf16[8,72,128]{2,1,0:T(8,128)(2,1)S(1)}, bf16[8,72,128]{2,1,0:T(8,128)(2,1)}, u32[]{:S(2)}) copy-start(bf16[8,72,128]{2,1,0:T(8,128)(2,1)} %get-tuple-element.19) | copy-start | bytes 442372
  64.2 2.7 %copy-start.14 = (bf16[1,8,2,1024,128]{4,3,2,1,0:T(8,128)(2,1)S(1)}, bf16[1,8,2,1024,128]{4,3,2,1,0:T(8,128)(2,1)}, u32[]{:S(2)}) copy-start(bf16[1,8,2,1024,128]{4,3,2,1,0:T(8,128)(2,1)} %param.25) | copy-start | bytes 12582916
  66.9 18.0 %copy-start.2 = (f32[2,36,1024]{2,1,0:T(8,128)S(1)}, f32[2,36,1024]{2,1,0:T(8,128)}, u32[]{:S(2)}) copy-start(f32[2,36,1024]{2,1,0:T(8,128)} %get-tuple-element.131.one_ref.cur_ref) | copy-start | bytes 884740
  66.9 18.0 %copy-start.8 = (f32[1024]{0:T(1024)S(1)}, f32[1024]{0:T(1024)}, u32[]{:S(2)}) copy-start(f32[1024]{0:T(1024)} %param.24) | copy-start | bytes 12292
  67.0 18.4 %copy-start.9 = (f32[2,36,36]{2,1,0:T(8,128)S(1)}, f32[2,36,36]{2,1,0:T(8,128)}, u32[]{:S(2)}) copy-start(f32[2,36,36]{2,1,0:T(8,128)} %get-tuple-element.21) | copy-start | bytes 31108
  67.0 18.5 %copy-start.11 = (f32[36,36]{1,0:T(8,128)S(1)}, f32[36,36]{1,0:T(8,128)}, u32[]{:S(2)}) copy-start(f32[36,36]{1,0:T(8,128)} %get-tuple-element.22) | copy-start | bytes 15556
  128.6 29.0 %copy-start.16 = (bf16[1,4,2,64,1024]{4,3,2,1,0:T(8,128)(2,1)S(1)}, bf16[1,4,2,64,1024]{4,3,2,1,0:T(8,128)(2,1)}, u32[]{:S(2)}) copy-start(bf16[1,4,2,64,1024]{4,3,2,1,0:T(8,128)(2,1)} %param.27) | copy-start | bytes 3145732
  157.5 1.1 copy-start.6
  157.6 2.2 copy-start.15
  158.7 18.9 %copy-start.3 = (f32[2,36,1024]{2,1,0:T(8,128)S(1)}, f32[2,36,1024]{2,1,0:T(8,128)}, u32[]{:S(2)}) copy-start(f32[2,36,1024]{2,1,0:T(8,128)} %get-tuple-element.131.one_ref.cur_ref) | copy-start | bytes 884740
  158.8 18.9 %copy-start.4 = (f32[2,36,1024]{2,1,0:T(8,128)S(1)}, f32[2,36,1024]{2,1,0:T(8,128)}, u32[]{:S(2)}) copy-start(f32[2,36,1024]{2,1,0:T(8,128)} %get-tuple-element.133.cur_ref) | copy-start | bytes 884740
  159.8 19.5 %copy-start.13 = (f32[36,36]{1,0:T(8,128)S(1)}, f32[36,36]{1,0:T(8,128)}, u32[]{:S(2)}) copy-start(f32[36,36]{1,0:T(8,128)} %get-tuple-element.25) | copy-start | bytes 15556
  159.8 19.6 %copy-start.12 = (f32[36,36]{1,0:T(8,128)S(1)}, f32[36,36]{1,0:T(8,128)}, u32[]{:S(2)}) copy-start(f32[36,36]{1,0:T(8,128)} %get-tuple-element.26) | copy-start | bytes 15556
  159.8 19.7 %copy-start.10 = (f32[2,36,36]{2,1,0:T(8,128)S(1)}, f32[2,36,36]{2,1,0:T(8,128)}, u32[]{:S(2)}) copy-start(f32[2,36,36]{2,1,0:T(8,128)} %get-tuple-element.27) | copy-start | bytes 31108
  176.7 45.6 %copy-start.7 = (f32[48,128]{1,0:T(8,128)S(1)}, f32[48,128]{1,0:T(8,128)}, u32[]{:S(2)}) copy-start(f32[48,128]{1,0:T(8,128)} %shard_map.98) | copy-start | bytes 73732

commit v11 on v10

--- a/solution.py
+++ b/solution.py
@@ -249,7 +249,7 @@
     )(flat, basis_one, basis, harmonics)
     return (
         near.reshape(2 * half, parts, fields, width),
-        far.reshape(blocks, parts, fields, elements),
+        far,
         cross,
         self_gram,
         proj,
@@ -332,25 +332,23 @@
 
 def col_reduce(partial_sum, collective_id):
     cols = lax.axis_size("col")
-    parts, fields, elements = partial_sum.shape
+    rows, elements = partial_sum.shape
     width = elements // cols
-    flat = partial_sum.reshape(parts * fields, elements)
-    summed = pl.pallas_call(
+    return pl.pallas_call(
         partial(reduce_kernel, cols),
-        out_shape=jax.ShapeDtypeStruct(flat.shape, jnp.float32),
+        out_shape=jax.ShapeDtypeStruct(partial_sum.shape, jnp.float32),
         in_specs=[pl.BlockSpec(memory_space=pltpu.VMEM)],
         out_specs=pl.BlockSpec(memory_space=pltpu.VMEM),
         scratch_shapes=[
-            pltpu.VMEM((cols, parts * fields, width), jnp.float32),
-            pltpu.VMEM((parts * fields, elements), jnp.float32),
+            pltpu.VMEM((cols, rows, width), jnp.float32),
+            pltpu.VMEM((rows, elements), jnp.float32),
             pltpu.SemaphoreType.DMA((cols,)),
             pltpu.SemaphoreType.DMA((cols,)),
             pltpu.SemaphoreType.DMA((cols,)),
             pltpu.SemaphoreType.DMA((cols,)),
         ],
         compiler_params=pltpu.CompilerParams(collective_id=collective_id, has_side_effects=True),
-    )(flat)
-    return summed.reshape(partial_sum.shape)
+    )(partial_sum)
 
 
 def row_psum(ids, *arrays):
@@ -417,9 +415,10 @@
     def operator_terms(near_pieces, far_pieces):
         near_on = flags[0] == 1
         near_vector = jnp.where(near_on[:, None, None, None], near_pieces, 0).astype(jnp.bfloat16)
+        near_lhs = complex_lhs(near_vector, 1).transpose(0, 3, 1, 2, 4)
         near_out = jnp.einsum(
-            "caksf,kaef->cse",
-            complex_lhs(near_vector, 1),
+            "xakf,kaef->xe",
+            near_lhs.reshape(2 * fields, 2, slots, width),
             near_blocks[0],
             preferred_element_type=jnp.float32,
         )
@@ -429,16 +428,20 @@
         keep = (~is_near)[:, None] & (
             jnp.arange(right_factors.shape[3], dtype=jnp.int32)[None, :] < ranks[0][:, None]
         )
-        coeffs = jnp.einsum(
-            "cansf,narf->cnsr",
-            complex_lhs(far_pieces, 1),
-            right_factors[0],
-            preferred_element_type=jnp.float32,
+        products = jnp.einsum(
+            "nxf,nbrf->nxbr", far_pieces, right_factors[0], preferred_element_type=jnp.float32
+        )
+        coeffs = jnp.stack(
+            [
+                products[:, :fields, 0] - products[:, fields:, 1],
+                products[:, :fields, 1] + products[:, fields:, 0],
+            ]
         )
         coeffs = jnp.where(keep[None, :, None, :], coeffs, 0.0).astype(jnp.bfloat16)
+        far_lhs = complex_lhs(coeffs, 0).transpose(0, 3, 1, 2, 4)
         far_out = jnp.einsum(
-            "cansr,nare->cse",
-            complex_lhs(coeffs, 0),
+            "xanr,nare->xe",
+            far_lhs.reshape(2 * fields, 2, blocks, far_lhs.shape[-1]),
             left_factors[0],
             preferred_element_type=jnp.float32,
         )
@@ -451,7 +454,7 @@
         )
         ids.append(None)
         total = operator_terms(near_pieces, far_pieces)
-        summed = col_reduce(total, 32 + len(ids))
+        summed = col_reduce(total, 32 + len(ids)).reshape(vector.shape)
         ids.append(None)
         return summed + diagonal[None, None, :] * vector, cross, self_gram, proj
 

time: 228 us -> 231 us (1.013)
  matrix products: 19.7 us -> 26.3 us
  local copies, waits for them, and re-layouts: 22.9 us -> 18.8 us
    dot_general x6, matrix products: 5.94 us -> 12.3 us  [the longest x2 8.64 us: operator_terms(): jnp.einsum('xakf,kaef->xe', near_lhs.reshape(2 * fields, 2, slots, width)...]
    unnamed x42 -> x32, local copies, waits for them, and re-layouts: 4.72 us -> 3.51 us
where the time goes in v11:
time: 231 us; the launch traced here: 228 us
  Pallas kernels  151 us (65%)
  other arithmetic  30.3 us (13%)
  matrix products  26.3 us (11%)
  local copies, waits for them, and re-layouts  18.8 us (8%)
    pallas_call x4, Pallas kernels, row_allreduce(): pl.pallas_call(partial(allreduce_kernel, inner, outer), out_shape=jax.Sha...  67.5 us
    pallas_call x2, Pallas kernels, gather_pieces(): pl.pallas_call(partial(gather_kernel, rows, cols, blocks, half), out_shap...  54 us
    pallas_call x2, Pallas kernels, col_reduce(): pl.pallas_call(partial(reduce_kernel, cols), out_shape=jax.ShapeDtypeStru...  29.5 us
    another operation x6, other arithmetic, lower_inverse(): lax.linalg.triangular_solve(lower, identity, left_side=True, lower=True)  12.9 us
    dot_general x2, matrix products, operator_terms(): jnp.einsum('xakf,kaef->xe', near_lhs.reshape(2 * fields, 2, slots, width)...  8.64 us
    another operation x3, other arithmetic, body(): factor_inverse = lower_inverse(jnp.linalg.cholesky(normal))  7.26 us
    dot_general x5, matrix products, combine_rows(): return jnp.einsum('st,ctn->csn', matrix, vectors, precision=highest)  4.63 us

profile of v11, /device:TPU:24, one launch (start us, length us, event | category | flops | bytes accessed | tf_op | source)
XLA Modules:
  0.0 227.9 jit_solution(7613702594996778369)
XLA Ops:
  0.7 1.7 convolution_bitcast_fusion.12
  3.1 17.3 %shard_map.95 = f32[16,128]{1,0:T(8,128)} custom-call(f32[16,128]{1,0:T(8,128)} %pad_bitcast_fusion.1.x_ref), custom_call_target="tpu_custom_call" | custom-call | tf_op jit(solution)/shard_map/pallas_call | solution.py:95
  20.4 0.8 reshape.329
  21.3 3.3 %cholesky.81 = f32[36,36]{1,0:T(8,128)S(1)} custom-call(f32[36,36]{1,0:T(8,128)S(1)} %fusion.66), custom_call_target="Cholesky" | custom-call | tf_op jit(solution)/shard_map/jit(cholesky)/cholesky | solution.py:461
  26.1 2.8 %custom-call.15 = f32[1,36,36]{1,2,0:T(8,128)S(1)} custom-call(f32[1,36,36]{2,1,0:T(8,128)S(1)} %select_bitcast_fusion.1), custom_call_target="InvertDiagBlocksLowerTriangular" | custom-call | tf_op jit(solution)/shard_map/triangular_solve/custom-call.2 | solution.py:390
  29.1 2.2 fusion.110
  32.0 1.8 copy.45.harm_ref
  33.7 27.9 %shard_map.96 = (bf16[8,72,128]{2,1,0:T(8,128)(2,1)}, bf16[4,72,1024]{2,1,0:T(8,128)(2,1)}, f32[36,36]{1,0:T(8,128)}, f32[36,36]{1,0:T(8,128)}, f32[2,36,36]{2,1,0:T(8,128)}) custom-call(bf16[72,1024]{1,0:T(8,128)(2,1)} %reshape.330.v_ref, f32[2,36,1024]{2,1,0:T(8,128)} %get-tuple-element.101.one_ref.cur_ref, ...), custom_call_target="tpu_custom_call" | custom-call | tf_op jit(solution)/shard_map/pallas_call | solution.py:228
  61.6 0.9 copy.46
  63.5 1.5 fusion.24
  66.8 4.3 %fusion.15.x_ref = f32[72,1024]{1,0:T(8,128)} fusion(f32[72,1024]{1,0:T(8,128)S(1)} %convolution_bitcast_fusion.4, bf16[72,2,8,128]{3,2,1,0:T(8,128)(2,1)S(1)} %bitcast.239, bf16[1,8,2,1024,128]{4,3,2,1,0:T(8,128)(2,1)} %param.21), kind=kOutput, calls=%fused_computation.16 | convolution fusion | flops 302063616 | bytes 5079040 | tf_op jit(solution)/shard_map/xakf,kaef->xe/dot_general | solution.py:419
  71.1 14.7 %shard_map.97 = f32[72,1024]{1,0:T(8,128)} custom-call(f32[72,1024]{1,0:T(8,128)} %fusion.15.x_ref), custom_call_target="tpu_custom_call" | custom-call | tf_op jit(solution)/shard_map/pallas_call | solution.py:337
  85.9 1.0 reshape.334
  88.3 17.4 %shard_map.98 = f32[48,128]{1,0:T(8,128)} custom-call(f32[48,128]{1,0:T(8,128)} %bitcast.247), custom_call_target="tpu_custom_call" | custom-call | tf_op jit(solution)/shard_map/pallas_call | solution.py:95
  108.1 12.6 %shard_map.99 = f32[16,128]{1,0:T(8,128)} custom-call(f32[16,128]{1,0:T(8,128)} %pad_bitcast_fusion.x_ref), custom_call_target="tpu_custom_call" | custom-call | tf_op jit(solution)/shard_map/pallas_call | solution.py:95
  120.7 0.8 reshape.344
  121.7 3.3 %cholesky.92 = f32[36,36]{1,0:T(8,128)S(1)} custom-call(f32[36,36]{1,0:T(8,128)S(1)} %copy.56), custom_call_target="Cholesky" | custom-call | tf_op jit(solution)/shard_map/jit(cholesky)/cholesky | solution.py:469
  126.3 2.8 %custom-call.16 = f32[1,36,36]{1,2,0:T(8,128)S(1)} custom-call(f32[1,36,36]{2,1,0:T(8,128)S(1)} %select_bitcast_fusion), custom_call_target="InvertDiagBlocksLowerTriangular" | custom-call | tf_op jit(solution)/shard_map/triangular_solve/custom-call.2 | solution.py:390
  129.3 1.1 fusion.111
  131.1 26.1 %shard_map.100 = (bf16[8,72,128]{2,1,0:T(8,128)(2,1)}, bf16[4,72,1024]{2,1,0:T(8,128)(2,1)}, f32[36,36]{1,0:T(8,128)}, f32[36,36]{1,0:T(8,128)}, f32[2,36,36]{2,1,0:T(8,128)}) custom-call(bf16[72,1024]{1,0:T(8,128)(2,1)} %reshape.345.v_ref, f32[2,36,1024]{2,1,0:T(8,128)} %get-tuple-element.101.one_ref.cur_ref, f32[2,36,1024]{2,1,0:T(8,128)} %get-tuple-element.103.cur_ref, ...), custom_call_target="tpu_custom_call" | custom-call | tf_op jit(solution)/shard_map/pallas_call | solution.py:228
  157.2 0.9 copy.58
  158.4 1.5 fusion.20
  160.9 4.3 %fusion.12.x_ref = f32[72,1024]{1,0:T(8,128)} fusion(f32[72,1024]{1,0:T(8,128)S(1)} %convolution_bitcast_fusion.3, bf16[72,2,8,128]{3,2,1,0:T(8,128)(2,1)S(1)} %bitcast.240, bf16[1,8,2,1024,128]{4,3,2,1,0:T(8,128)(2,1)} %param.21), kind=kOutput, calls=%fused_computation.15 | convolution fusion | flops 302063616 | bytes 5079040 | tf_op jit(solution)/shard_map/xakf,kaef->xe/dot_general | solution.py:419
  165.2 14.8 %shard_map.101 = f32[72,1024]{1,0:T(8,128)} custom-call(f32[72,1024]{1,0:T(8,128)} %fusion.12.x_ref), custom_call_target="tpu_custom_call" | custom-call | tf_op jit(solution)/shard_map/pallas_call | solution.py:337
  180.1 1.0 reshape.349
  183.7 20.2 %shard_map.102 = f32[72,128]{1,0:T(8,128)} custom-call(f32[72,128]{1,0:T(8,128)} %bitcast.244), custom_call_target="tpu_custom_call" | custom-call | tf_op jit(solution)/shard_map/pallas_call | solution.py:95
  203.9 0.9 slice.97
  207.9 6.6 %cholesky.42 = f32[72,72]{1,0:T(8,128)S(1)} custom-call(f32[72,72]{1,0:T(8,128)S(1)} %fusion.56), custom_call_target="Cholesky" | custom-call | tf_op jit(solution)/shard_map/jit(cholesky)/cholesky | solution.py:509
  215.8 5.5 %custom-call.11 = f32[1,72,72]{1,2,0:T(8,128)S(1)} custom-call(f32[1,72,72]{2,1,0:T(8,128)S(1)} %fusion.45), custom_call_target="InvertDiagBlocksLowerTriangular" | custom-call | tf_op jit(solution)/shard_map/triangular_solve | solution.py:390
  221.6 0.9 fusion.70
  222.5 0.9 fusion.72
  226.9 0.9 copy.77
  (135 shorter events, 23.8 us)
Async XLA Ops:
  0.6 65.8 %copy-start = (bf16[1,4,2,64,1024]{4,3,2,1,0:T(8,128)(2,1)S(1)}, bf16[1,4,2,64,1024]{4,3,2,1,0:T(8,128)(2,1)}, u32[]{:S(2)}) copy-start(bf16[1,4,2,64,1024]{4,3,2,1,0:T(8,128)(2,1)} %param.22) | copy-start | bytes 3145732
  0.6 62.8 %copy-start.5 = (bf16[1,4,2,64,1024]{4,3,2,1,0:T(8,128)(2,1)S(1)}, bf16[1,4,2,64,1024]{4,3,2,1,0:T(8,128)(2,1)}, u32[]{:S(2)}) copy-start(bf16[1,4,2,64,1024]{4,3,2,1,0:T(8,128)(2,1)} %param.23) | copy-start | bytes 3145732
  21.3 43.9 %copy-start.1 = (s32[1,8]{1,0:T(1,128)S(1)}, s32[1,8]{1,0:T(1,128)}, u32[]{:S(2)}) copy-start(s32[1,8]{1,0:T(1,128)} %param.24) | copy-start | bytes 100
  29.1 36.8 %copy-start.13 = (s32[1,4]{1,0:T(1,128)S(1)}, s32[1,4]{1,0:T(1,128)}, u32[]{:S(2)}) copy-start(s32[1,4]{1,0:T(1,128)} %param.25) | copy-start | bytes 52
  66.4 20.4 %copy-start.2 = (f32[2,36,1024]{2,1,0:T(8,128)S(1)}, f32[2,36,1024]{2,1,0:T(8,128)}, u32[]{:S(2)}) copy-start(f32[2,36,1024]{2,1,0:T(8,128)} %get-tuple-element.101.one_ref.cur_ref) | copy-start | bytes 884740
  66.5 20.4 %copy-start.7 = (f32[1024]{0:T(1024)S(1)}, f32[1024]{0:T(1024)}, u32[]{:S(2)}) copy-start(f32[1024]{0:T(1024)} %param.20) | copy-start | bytes 12292
  66.8 20.6 %copy-start.8 = (f32[2,36,36]{2,1,0:T(8,128)S(1)}, f32[2,36,36]{2,1,0:T(8,128)}, u32[]{:S(2)}) copy-start(f32[2,36,36]{2,1,0:T(8,128)} %get-tuple-element.19) | copy-start | bytes 31108
  66.8 20.7 %copy-start.10 = (f32[36,36]{1,0:T(8,128)S(1)}, f32[36,36]{1,0:T(8,128)}, u32[]{:S(2)}) copy-start(f32[36,36]{1,0:T(8,128)} %get-tuple-element.20) | copy-start | bytes 15556
  160.5 20.5 %copy-start.4 = (f32[2,36,1024]{2,1,0:T(8,128)S(1)}, f32[2,36,1024]{2,1,0:T(8,128)}, u32[]{:S(2)}) copy-start(f32[2,36,1024]{2,1,0:T(8,128)} %get-tuple-element.103.cur_ref) | copy-start | bytes 884740
  160.9 21.2 %copy-start.3 = (f32[2,36,1024]{2,1,0:T(8,128)S(1)}, f32[2,36,1024]{2,1,0:T(8,128)}, u32[]{:S(2)}) copy-start(f32[2,36,1024]{2,1,0:T(8,128)} %get-tuple-element.101.one_ref.cur_ref) | copy-start | bytes 884740
  160.9 21.8 %copy-start.9 = (f32[2,36,36]{2,1,0:T(8,128)S(1)}, f32[2,36,36]{2,1,0:T(8,128)}, u32[]{:S(2)}) copy-start(f32[2,36,36]{2,1,0:T(8,128)} %get-tuple-element.25) | copy-start | bytes 31108
  160.9 21.9 %copy-start.12 = (f32[36,36]{1,0:T(8,128)S(1)}, f32[36,36]{1,0:T(8,128)}, u32[]{:S(2)}) copy-start(f32[36,36]{1,0:T(8,128)} %get-tuple-element.23) | copy-start | bytes 15556
  160.9 22.0 %copy-start.11 = (f32[36,36]{1,0:T(8,128)S(1)}, f32[36,36]{1,0:T(8,128)}, u32[]{:S(2)}) copy-start(f32[36,36]{1,0:T(8,128)} %get-tuple-element.24) | copy-start | bytes 15556
  165.2 58.6 %copy-start.6 = (f32[48,128]{1,0:T(8,128)S(1)}, f32[48,128]{1,0:T(8,128)}, u32[]{:S(2)}) copy-start(f32[48,128]{1,0:T(8,128)} %shard_map.98) | copy-start | bytes 73732

commit v12 on v10

--- a/solution.py
+++ b/solution.py
@@ -249,7 +249,7 @@
     )(flat, basis_one, basis, harmonics)
     return (
         near.reshape(2 * half, parts, fields, width),
-        far.reshape(blocks, parts, fields, elements),
+        far,
         cross,
         self_gram,
         proj,
@@ -429,11 +429,14 @@
         keep = (~is_near)[:, None] & (
             jnp.arange(right_factors.shape[3], dtype=jnp.int32)[None, :] < ranks[0][:, None]
         )
-        coeffs = jnp.einsum(
-            "cansf,narf->cnsr",
-            complex_lhs(far_pieces, 1),
-            right_factors[0],
-            preferred_element_type=jnp.float32,
+        products = jnp.einsum(
+            "nxf,nbrf->nxbr", far_pieces, right_factors[0], preferred_element_type=jnp.float32
+        )
+        coeffs = jnp.stack(
+            [
+                products[:, :fields, 0] - products[:, fields:, 1],
+                products[:, :fields, 1] + products[:, fields:, 0],
+            ]
         )
         coeffs = jnp.where(keep[None, :, None, :], coeffs, 0.0).astype(jnp.bfloat16)
         far_out = jnp.einsum(

time: 228 us -> 228 us (level)
  local copies, waits for them, and re-layouts: 22.9 us -> 19 us
  matrix products: 19.7 us -> 23 us
    unnamed x42 -> x36, local copies, waits for them, and re-layouts: 4.72 us -> 3.53 us
where the time goes in v12:
time: 228 us; the launch traced here: 224 us
  Pallas kernels  151 us (66%)
  other arithmetic  29.5 us (13%)
  matrix products  23 us (10%)
  local copies, waits for them, and re-layouts  19 us (8%)
    pallas_call x4, Pallas kernels, row_allreduce(): pl.pallas_call(partial(allreduce_kernel, inner, outer), out_shape=jax.Sha...  67.5 us
    pallas_call x2, Pallas kernels, gather_pieces(): pl.pallas_call(partial(gather_kernel, rows, cols, blocks, half), out_shap...  54 us
    pallas_call x2, Pallas kernels, col_reduce(): pl.pallas_call(partial(reduce_kernel, cols), out_shape=jax.ShapeDtypeStru...  29.5 us
    another operation x6, other arithmetic, lower_inverse(): lax.linalg.triangular_solve(lower, identity, left_side=True, lower=True)  12.9 us
    another operation x3, other arithmetic, body(): factor_inverse = lower_inverse(jnp.linalg.cholesky(normal))  7.26 us
    dot_general x2, matrix products, operator_terms(): jnp.einsum('caksf,kaef->cse', complex_lhs(near_vector, 1), near_blocks[0]...  5 us
    dot_general x5, matrix products, combine_rows(): return jnp.einsum('st,ctn->csn', matrix, vectors, precision=highest)  4.64 us

profile of v12, /device:TPU:24, one launch (start us, length us, event | category | flops | bytes accessed | tf_op | source)
XLA Modules:
  0.0 224.0 jit_solution(5905323673086959754)
XLA Ops:
  0.7 1.7 convolution_bitcast_fusion.12
  3.0 17.3 %shard_map.95 = f32[16,128]{1,0:T(8,128)} custom-call(f32[16,128]{1,0:T(8,128)} %pad_bitcast_fusion.1.x_ref), custom_call_target="tpu_custom_call" | custom-call | tf_op jit(solution)/shard_map/pallas_call | solution.py:95
  20.4 0.8 reshape.323
  21.3 3.3 %cholesky.81 = f32[36,36]{1,0:T(8,128)S(1)} custom-call(f32[36,36]{1,0:T(8,128)S(1)} %fusion.74), custom_call_target="Cholesky" | custom-call | tf_op jit(solution)/shard_map/jit(cholesky)/cholesky | solution.py:461
  25.9 2.8 %custom-call.15 = f32[1,36,36]{1,2,0:T(8,128)S(1)} custom-call(f32[1,36,36]{2,1,0:T(8,128)S(1)} %select_bitcast_fusion.1), custom_call_target="InvertDiagBlocksLowerTriangular" | custom-call | tf_op jit(solution)/shard_map/triangular_solve/custom-call.2 | solution.py:392
  28.9 2.2 fusion.122
  31.8 1.8 copy.45.harm_ref
  33.6 27.9 %shard_map.96 = (bf16[8,72,128]{2,1,0:T(8,128)(2,1)}, bf16[4,72,1024]{2,1,0:T(8,128)(2,1)}, f32[36,36]{1,0:T(8,128)}, f32[36,36]{1,0:T(8,128)}, f32[2,36,36]{2,1,0:T(8,128)}) custom-call(bf16[72,1024]{1,0:T(8,128)(2,1)} %reshape.324.v_ref, f32[2,36,1024]{2,1,0:T(8,128)} %get-tuple-element.101.one_ref.cur_ref, ...), custom_call_target="tpu_custom_call" | custom-call | tf_op jit(solution)/shard_map/pallas_call | solution.py:228
  61.5 1.9 fusion.24
  64.8 3.6 %fusion.7 = f32[2,36,1024]{2,1,0:T(8,128)S(1)} fusion(bf16[1,2,8,36,128]{4,3,2,1,0:T(8,128)(2,1)S(1)} %get-tuple-element.93, bf16[1,2,8,36,128]{4,3,2,1,0:T(8,128)(2,1)S(1)} %get-tuple-element.92, bf16[1,8,2,1024,128]{4,3,2,1,0:T(8,128)(2,1)} %param.21), kind=kOutput, calls=%fused_computation.9 | convolution fusion | flops 302137344 | bytes 4784128 | tf_op jit(solution)/shard_map/caksf,kaef->cse/dot_general | solution.py:420
  69.5 14.7 %shard_map.97 = f32[72,1024]{1,0:T(8,128)} custom-call(f32[72,1024]{1,0:T(8,128)} %reshape.326.x_ref), custom_call_target="tpu_custom_call" | custom-call | tf_op jit(solution)/shard_map/pallas_call | solution.py:338
  84.2 1.0 reshape.327
  86.7 17.4 %shard_map.98 = f32[48,128]{1,0:T(8,128)} custom-call(f32[48,128]{1,0:T(8,128)} %bitcast.261), custom_call_target="tpu_custom_call" | custom-call | tf_op jit(solution)/shard_map/pallas_call | solution.py:95
  104.1 0.8 fusion.121
  106.5 12.6 %shard_map.99 = f32[16,128]{1,0:T(8,128)} custom-call(f32[16,128]{1,0:T(8,128)} %pad_bitcast_fusion.x_ref), custom_call_target="tpu_custom_call" | custom-call | tf_op jit(solution)/shard_map/pallas_call | solution.py:95
  119.1 0.8 reshape.337
  120.1 3.3 %cholesky.92 = f32[36,36]{1,0:T(8,128)S(1)} custom-call(f32[36,36]{1,0:T(8,128)S(1)} %copy.54), custom_call_target="Cholesky" | custom-call | tf_op jit(solution)/shard_map/jit(cholesky)/cholesky | solution.py:469
  124.7 2.8 %custom-call.16 = f32[1,36,36]{1,2,0:T(8,128)S(1)} custom-call(f32[1,36,36]{2,1,0:T(8,128)S(1)} %select_bitcast_fusion), custom_call_target="InvertDiagBlocksLowerTriangular" | custom-call | tf_op jit(solution)/shard_map/triangular_solve/custom-call.2 | solution.py:392
  127.7 1.1 fusion.123
  129.6 26.1 %shard_map.100 = (bf16[8,72,128]{2,1,0:T(8,128)(2,1)}, bf16[4,72,1024]{2,1,0:T(8,128)(2,1)}, f32[36,36]{1,0:T(8,128)}, f32[36,36]{1,0:T(8,128)}, f32[2,36,36]{2,1,0:T(8,128)}) custom-call(bf16[72,1024]{1,0:T(8,128)(2,1)} %reshape.338.v_ref, f32[2,36,1024]{2,1,0:T(8,128)} %get-tuple-element.101.one_ref.cur_ref, f32[2,36,1024]{2,1,0:T(8,128)} %get-tuple-element.103.cur_ref, ...), custom_call_target="tpu_custom_call" | custom-call | tf_op jit(solution)/shard_map/pallas_call | solution.py:228
  155.7 1.6 fusion.20
  157.7 0.9 copy.56
  158.9 1.4 fusion.10
  161.4 14.8 %shard_map.101 = f32[72,1024]{1,0:T(8,128)} custom-call(f32[72,1024]{1,0:T(8,128)} %reshape.340.x_ref), custom_call_target="tpu_custom_call" | custom-call | tf_op jit(solution)/shard_map/pallas_call | solution.py:338
  176.2 1.0 reshape.341
  179.8 20.2 %shard_map.102 = f32[72,128]{1,0:T(8,128)} custom-call(f32[72,128]{1,0:T(8,128)} %bitcast.258), custom_call_target="tpu_custom_call" | custom-call | tf_op jit(solution)/shard_map/pallas_call | solution.py:95
  200.1 0.9 slice.97
  204.2 6.6 %cholesky.42 = f32[72,72]{1,0:T(8,128)S(1)} custom-call(f32[72,72]{1,0:T(8,128)S(1)} %fusion.64), custom_call_target="Cholesky" | custom-call | tf_op jit(solution)/shard_map/jit(cholesky)/cholesky | solution.py:509
  212.1 5.5 %custom-call.11 = f32[1,72,72]{1,2,0:T(8,128)S(1)} custom-call(f32[1,72,72]{2,1,0:T(8,128)S(1)} %fusion.53), custom_call_target="InvertDiagBlocksLowerTriangular" | custom-call | tf_op jit(solution)/shard_map/triangular_solve | solution.py:392
  217.8 0.8 fusion.78
  218.6 0.8 fusion.80
  223.0 0.9 copy.73
  (133 shorter events, 23.2 us)
Async XLA Ops:
  0.6 67.8 %copy-start = (bf16[1,4,2,64,1024]{4,3,2,1,0:T(8,128)(2,1)S(1)}, bf16[1,4,2,64,1024]{4,3,2,1,0:T(8,128)(2,1)}, u32[]{:S(2)}) copy-start(bf16[1,4,2,64,1024]{4,3,2,1,0:T(8,128)(2,1)} %param.22) | copy-start | bytes 3145732
  0.6 62.9 %copy-start.1 = (s32[1,8]{1,0:T(1,128)S(1)}, s32[1,8]{1,0:T(1,128)}, u32[]{:S(2)}) copy-start(s32[1,8]{1,0:T(1,128)} %param.24) | copy-start | bytes 100
  0.7 63.6 %copy-start.15 = (s32[1,4]{1,0:T(1,128)S(1)}, s32[1,4]{1,0:T(1,128)}, u32[]{:S(2)}) copy-start(s32[1,4]{1,0:T(1,128)} %param.25) | copy-start | bytes 52
  61.4 3.1 %copy-start.6 = (bf16[8,72,128]{2,1,0:T(8,128)(2,1)S(1)}, bf16[8,72,128]{2,1,0:T(8,128)(2,1)}, u32[]{:S(2)}) copy-start(bf16[8,72,128]{2,1,0:T(8,128)(2,1)} %get-tuple-element.17) | copy-start | bytes 442372
  64.8 20.5 %copy-start.2 = (f32[2,36,1024]{2,1,0:T(8,128)S(1)}, f32[2,36,1024]{2,1,0:T(8,128)}, u32[]{:S(2)}) copy-start(f32[2,36,1024]{2,1,0:T(8,128)} %get-tuple-element.101.one_ref.cur_ref) | copy-start | bytes 884740
  64.8 20.5 %copy-start.8 = (f32[1024]{0:T(1024)S(1)}, f32[1024]{0:T(1024)}, u32[]{:S(2)}) copy-start(f32[1024]{0:T(1024)} %param.20) | copy-start | bytes 12292
  64.8 21.0 %copy-start.9 = (f32[2,36,36]{2,1,0:T(8,128)S(1)}, f32[2,36,36]{2,1,0:T(8,128)}, u32[]{:S(2)}) copy-start(f32[2,36,36]{2,1,0:T(8,128)} %get-tuple-element.19) | copy-start | bytes 31108
  64.8 21.1 %copy-start.11 = (f32[36,36]{1,0:T(8,128)S(1)}, f32[36,36]{1,0:T(8,128)}, u32[]{:S(2)}) copy-start(f32[36,36]{1,0:T(8,128)} %get-tuple-element.20) | copy-start | bytes 15556
  68.8 86.9 %copy-start.5 = (bf16[1,4,2,64,1024]{4,3,2,1,0:T(8,128)(2,1)S(1)}, bf16[1,4,2,64,1024]{4,3,2,1,0:T(8,128)(2,1)}, u32[]{:S(2)}) copy-start(bf16[1,4,2,64,1024]{4,3,2,1,0:T(8,128)(2,1)} %param.23) | copy-start | bytes 3145732
  155.7 3.1 %copy-start.14 = (bf16[1,8,2,1024,128]{4,3,2,1,0:T(8,128)(2,1)S(1)}, bf16[1,8,2,1024,128]{4,3,2,1,0:T(8,128)(2,1)}, u32[]{:S(2)}) copy-start(bf16[1,8,2,1024,128]{4,3,2,1,0:T(8,128)(2,1)} %param.21) | copy-start | bytes 12582916
  158.8 18.4 %copy-start.4 = (f32[2,36,1024]{2,1,0:T(8,128)S(1)}, f32[2,36,1024]{2,1,0:T(8,128)}, u32[]{:S(2)}) copy-start(f32[2,36,1024]{2,1,0:T(8,128)} %get-tuple-element.103.cur_ref) | copy-start | bytes 884740
  158.8 19.4 %copy-start.3 = (f32[2,36,1024]{2,1,0:T(8,128)S(1)}, f32[2,36,1024]{2,1,0:T(8,128)}, u32[]{:S(2)}) copy-start(f32[2,36,1024]{2,1,0:T(8,128)} %get-tuple-element.101.one_ref.cur_ref) | copy-start | bytes 884740
  160.2 18.5 %copy-start.10 = (f32[2,36,36]{2,1,0:T(8,128)S(1)}, f32[2,36,36]{2,1,0:T(8,128)}, u32[]{:S(2)}) copy-start(f32[2,36,36]{2,1,0:T(8,128)} %get-tuple-element.25) | copy-start | bytes 31108
  160.3 18.7 %copy-start.13 = (f32[36,36]{1,0:T(8,128)S(1)}, f32[36,36]{1,0:T(8,128)}, u32[]{:S(2)}) copy-start(f32[36,36]{1,0:T(8,128)} %get-tuple-element.23) | copy-start | bytes 15556
  160.3 18.8 %copy-start.12 = (f32[36,36]{1,0:T(8,128)S(1)}, f32[36,36]{1,0:T(8,128)}, u32[]{:S(2)}) copy-start(f32[36,36]{1,0:T(8,128)} %get-tuple-element.24) | copy-start | bytes 15556
  160.3 59.7 %copy-start.7 = (f32[48,128]{1,0:T(8,128)S(1)}, f32[48,128]{1,0:T(8,128)}, u32[]{:S(2)}) copy-start(f32[48,128]{1,0:T(8,128)} %shard_map.98) | copy-start | bytes 73732

commit v13 on v12

--- a/solution.py
+++ b/solution.py
@@ -387,6 +387,11 @@
     return jnp.dot(left, right, precision=highest)
 
 
+def lower_solve(lower, vectors):
+    factor = jnp.broadcast_to(lower, (vectors.shape[0],) + lower.shape)
+    return lax.linalg.triangular_solve(factor, vectors, left_side=True, lower=True)
+
+
 def lower_inverse(lower):
     identity = jnp.eye(lower.shape[0], dtype=lower.dtype)
     return lax.linalg.triangular_solve(lower, identity, left_side=True, lower=True)
@@ -459,7 +464,7 @@
         return summed + diagonal[None, None, :] * vector, cross, self_gram, proj
 
     lower_first = jnp.linalg.cholesky(row_psum(ids, inner_products(incident, incident)))
-    basis_one = combine_rows(lower_inverse(lower_first), incident)
+    basis_one = lower_solve(lower_first, incident)
     image, _, self_one, harmonics_one = apply_operator(basis_one, basis_one)
     coupling_one, harmonics_one, self_one = row_psum(
         ids, inner_products(image, basis_one), harmonics_one, self_one
@@ -467,7 +472,7 @@
     rest = image - combine_rows(coupling_one, basis_one)
     gram_one = row_psum(ids, inner_products(rest, rest))
     lower_second = jnp.linalg.cholesky(gram_one)
-    basis_two = combine_rows(lower_inverse(lower_second), rest)
+    basis_two = lower_solve(lower_second, rest)
     image, cross, self_two, harmonics_two = apply_operator(basis_two, basis_one)
     coupling_onetwo, coupling_two, image_gram, cross, self_two, harmonics_two = row_psum(
         ids,

time: 228 us -> 231 us (1.013)
  other arithmetic: 29.5 us -> 35.1 us
    another operation x0 -> x5, other arithmetic: none -> 11.1 us  [lower_solve(): lax.linalg.triangular_solve(factor, vectors, left_side=True, lower=True)]
    another operation x6 -> x2, other arithmetic: 12.9 us -> 6.17 us  [lower_inverse(): lax.linalg.triangular_solve(lower, identity, left_side=True, lower=True)]
    another operation x0 -> x2, matrix products: none -> 3.43 us  [lower_solve(): lax.linalg.triangular_solve(factor, vectors, left_side=True, lower=True)]
    dot_general x5 -> x3, matrix products: 4.64 us -> 1.31 us  [combine_rows(): return jnp.einsum('st,ctn->csn', matrix, vectors, precision=highest)]
where the time goes in v13:
time: 231 us; the launch traced here: 227 us
  Pallas kernels  151 us (65%)
  other arithmetic  35.1 us (15%)
  matrix products  20.8 us (9%)
  local copies, waits for them, and re-layouts  19 us (8%)
    pallas_call x4, Pallas kernels, row_allreduce(): pl.pallas_call(partial(allreduce_kernel, inner, outer), out_shape=jax.Sha...  67.5 us
    pallas_call x2, Pallas kernels, gather_pieces(): pl.pallas_call(partial(gather_kernel, rows, cols, blocks, half), out_shap...  54 us
    pallas_call x2, Pallas kernels, col_reduce(): pl.pallas_call(partial(reduce_kernel, cols), out_shape=jax.ShapeDtypeStru...  29.5 us
    another operation x5, other arithmetic, lower_solve(): lax.linalg.triangular_solve(factor, vectors, left_side=True, lower=True)  11.1 us
    another operation x3, other arithmetic, body(): factor_inverse = lower_inverse(jnp.linalg.cholesky(normal))  7.26 us
    another operation x2, other arithmetic, lower_inverse(): lax.linalg.triangular_solve(lower, identity, left_side=True, lower=True)  6.17 us
    dot_general x2, matrix products, operator_terms(): jnp.einsum('caksf,kaef->cse', complex_lhs(near_vector, 1), near_blocks[0]...  5 us

profile of v13, /device:TPU:24, one launch (start us, length us, event | category | flops | bytes accessed | tf_op | source)
XLA Modules:
  0.0 227.3 jit_solution(8465697928344715115)
XLA Ops:
  0.7 1.7 convolution_bitcast_fusion.8
  3.0 17.3 %shard_map.95 = f32[16,128]{1,0:T(8,128)} custom-call(f32[16,128]{1,0:T(8,128)} %pad_bitcast_fusion.1.x_ref), custom_call_target="tpu_custom_call" | custom-call | tf_op jit(solution)/shard_map/pallas_call | solution.py:95
  20.4 0.8 reshape.325
  21.3 3.3 %cholesky.81 = f32[36,36]{1,0:T(8,128)S(1)} custom-call(f32[36,36]{1,0:T(8,128)S(1)} %fusion.74), custom_call_target="Cholesky" | custom-call | tf_op jit(solution)/shard_map/jit(cholesky)/cholesky | solution.py:466
  25.9 5.5 %custom-call.15 = f32[2,1,36,36]{2,3,1,0:T(8,128)S(1)} custom-call(f32[2,1,36,36]{3,2,1,0:T(8,128)S(1)} %select_bitcast_fusion.1), custom_call_target="InvertDiagBlocksLowerTriangular" | custom-call | tf_op jit(solution)/shard_map/triangular_solve/custom-call.2 | solution.py:392
  31.5 2.2 fusion.103
  34.4 1.8 copy.48.harm_ref
  36.2 27.9 %shard_map.96 = (bf16[8,72,128]{2,1,0:T(8,128)(2,1)}, bf16[4,72,1024]{2,1,0:T(8,128)(2,1)}, f32[36,36]{1,0:T(8,128)}, f32[36,36]{1,0:T(8,128)}, f32[2,36,36]{2,1,0:T(8,128)}) custom-call(bf16[72,1024]{1,0:T(8,128)(2,1)} %reshape.326.v_ref, f32[2,36,1024]{2,1,0:T(8,128)} %get-tuple-element.101.one_ref.cur_ref, ...), custom_call_target="tpu_custom_call" | custom-call | tf_op jit(solution)/shard_map/pallas_call | solution.py:228
  64.0 1.9 fusion.24
  67.4 3.6 %fusion.7 = f32[2,36,1024]{2,1,0:T(8,128)S(1)} fusion(bf16[1,2,8,36,128]{4,3,2,1,0:T(8,128)(2,1)S(1)} %get-tuple-element.93, bf16[1,2,8,36,128]{4,3,2,1,0:T(8,128)(2,1)S(1)} %get-tuple-element.92, bf16[1,8,2,1024,128]{4,3,2,1,0:T(8,128)(2,1)} %param.21), kind=kOutput, calls=%fused_computation.9 | convolution fusion | flops 302137344 | bytes 4784128 | tf_op jit(solution)/shard_map/caksf,kaef->cse/dot_general | solution.py:425
  72.1 14.7 %shard_map.97 = f32[72,1024]{1,0:T(8,128)} custom-call(f32[72,1024]{1,0:T(8,128)} %reshape.328.x_ref), custom_call_target="tpu_custom_call" | custom-call | tf_op jit(solution)/shard_map/pallas_call | solution.py:338
  86.8 1.0 reshape.329
  89.3 17.4 %shard_map.98 = f32[48,128]{1,0:T(8,128)} custom-call(f32[48,128]{1,0:T(8,128)} %bitcast.258), custom_call_target="tpu_custom_call" | custom-call | tf_op jit(solution)/shard_map/pallas_call | solution.py:95
  106.7 0.8 fusion.102
  109.1 12.6 %shard_map.99 = f32[16,128]{1,0:T(8,128)} custom-call(f32[16,128]{1,0:T(8,128)} %pad_bitcast_fusion.x_ref), custom_call_target="tpu_custom_call" | custom-call | tf_op jit(solution)/shard_map/pallas_call | solution.py:95
  121.7 0.8 reshape.339
  122.7 3.3 %cholesky.92 = f32[36,36]{1,0:T(8,128)S(1)} custom-call(f32[36,36]{1,0:T(8,128)S(1)} %copy.57), custom_call_target="Cholesky" | custom-call | tf_op jit(solution)/shard_map/jit(cholesky)/cholesky | solution.py:474
  127.4 5.5 %custom-call.16 = f32[2,1,36,36]{2,3,1,0:T(8,128)S(1)} custom-call(f32[2,1,36,36]{3,2,1,0:T(8,128)S(1)} %select_bitcast_fusion), custom_call_target="InvertDiagBlocksLowerTriangular" | custom-call | tf_op jit(solution)/shard_map/triangular_solve/custom-call.2 | solution.py:392
  132.9 1.2 fusion.104
  134.8 26.1 %shard_map.100 = (bf16[8,72,128]{2,1,0:T(8,128)(2,1)}, bf16[4,72,1024]{2,1,0:T(8,128)(2,1)}, f32[36,36]{1,0:T(8,128)}, f32[36,36]{1,0:T(8,128)}, f32[2,36,36]{2,1,0:T(8,128)}) custom-call(bf16[72,1024]{1,0:T(8,128)(2,1)} %reshape.340.v_ref, f32[2,36,1024]{2,1,0:T(8,128)} %get-tuple-element.101.one_ref.cur_ref, f32[2,36,1024]{2,1,0:T(8,128)} %get-tuple-element.103.cur_ref, ...), custom_call_target="tpu_custom_call" | custom-call | tf_op jit(solution)/shard_map/pallas_call | solution.py:228
  161.0 1.6 fusion.20
  163.0 0.9 copy.60
  164.1 1.4 fusion.10
  165.9 0.7 reshape.342.x_ref
  166.6 14.8 %shard_map.101 = f32[72,1024]{1,0:T(8,128)} custom-call(f32[72,1024]{1,0:T(8,128)} %reshape.342.x_ref), custom_call_target="tpu_custom_call" | custom-call | tf_op jit(solution)/shard_map/pallas_call | solution.py:338
  181.4 1.0 reshape.343
  185.0 20.2 %shard_map.102 = f32[72,128]{1,0:T(8,128)} custom-call(f32[72,128]{1,0:T(8,128)} %bitcast.255), custom_call_target="tpu_custom_call" | custom-call | tf_op jit(solution)/shard_map/pallas_call | solution.py:95
  205.3 0.9 slice.97
  208.8 6.6 %cholesky.42 = f32[72,72]{1,0:T(8,128)S(1)} custom-call(f32[72,72]{1,0:T(8,128)S(1)} %fusion.68), custom_call_target="Cholesky" | custom-call | tf_op jit(solution)/shard_map/jit(cholesky)/cholesky | solution.py:514
  216.7 5.5 %custom-call.11 = f32[1,72,72]{1,2,0:T(8,128)S(1)} custom-call(f32[1,72,72]{2,1,0:T(8,128)S(1)} %fusion.57), custom_call_target="InvertDiagBlocksLowerTriangular" | custom-call | tf_op jit(solution)/shard_map/triangular_solve | solution.py:397
  223.7 0.8 slice.198
  226.4 0.9 copy.77
  (134 shorter events, 21.0 us)
Async XLA Ops:
  0.6 70.4 %copy-start = (bf16[1,4,2,64,1024]{4,3,2,1,0:T(8,128)(2,1)S(1)}, bf16[1,4,2,64,1024]{4,3,2,1,0:T(8,128)(2,1)}, u32[]{:S(2)}) copy-start(bf16[1,4,2,64,1024]{4,3,2,1,0:T(8,128)(2,1)} %param.22) | copy-start | bytes 3145732
  0.6 65.5 %copy-start.1 = (s32[1,8]{1,0:T(1,128)S(1)}, s32[1,8]{1,0:T(1,128)}, u32[]{:S(2)}) copy-start(s32[1,8]{1,0:T(1,128)} %param.24) | copy-start | bytes 100
  0.7 66.2 %copy-start.15 = (s32[1,4]{1,0:T(1,128)S(1)}, s32[1,4]{1,0:T(1,128)}, u32[]{:S(2)}) copy-start(s32[1,4]{1,0:T(1,128)} %param.25) | copy-start | bytes 52
  64.0 3.1 %copy-start.6 = (bf16[8,72,128]{2,1,0:T(8,128)(2,1)S(1)}, bf16[8,72,128]{2,1,0:T(8,128)(2,1)}, u32[]{:S(2)}) copy-start(bf16[8,72,128]{2,1,0:T(8,128)(2,1)} %get-tuple-element.17) | copy-start | bytes 442372
  67.3 20.5 %copy-start.2 = (f32[2,36,1024]{2,1,0:T(8,128)S(1)}, f32[2,36,1024]{2,1,0:T(8,128)}, u32[]{:S(2)}) copy-start(f32[2,36,1024]{2,1,0:T(8,128)} %get-tuple-element.101.one_ref.cur_ref) | copy-start | bytes 884740
  67.4 20.5 %copy-start.8 = (f32[1024]{0:T(1024)S(1)}, f32[1024]{0:T(1024)}, u32[]{:S(2)}) copy-start(f32[1024]{0:T(1024)} %param.20) | copy-start | bytes 12292
  67.4 21.0 %copy-start.9 = (f32[2,36,36]{2,1,0:T(8,128)S(1)}, f32[2,36,36]{2,1,0:T(8,128)}, u32[]{:S(2)}) copy-start(f32[2,36,36]{2,1,0:T(8,128)} %get-tuple-element.19) | copy-start | bytes 31108
  67.4 21.1 %copy-start.11 = (f32[36,36]{1,0:T(8,128)S(1)}, f32[36,36]{1,0:T(8,128)}, u32[]{:S(2)}) copy-start(f32[36,36]{1,0:T(8,128)} %get-tuple-element.20) | copy-start | bytes 15556
  71.4 89.6 %copy-start.5 = (bf16[1,4,2,64,1024]{4,3,2,1,0:T(8,128)(2,1)S(1)}, bf16[1,4,2,64,1024]{4,3,2,1,0:T(8,128)(2,1)}, u32[]{:S(2)}) copy-start(bf16[1,4,2,64,1024]{4,3,2,1,0:T(8,128)(2,1)} %param.23) | copy-start | bytes 3145732
  160.9 3.1 %copy-start.14 = (bf16[1,8,2,1024,128]{4,3,2,1,0:T(8,128)(2,1)S(1)}, bf16[1,8,2,1024,128]{4,3,2,1,0:T(8,128)(2,1)}, u32[]{:S(2)}) copy-start(bf16[1,8,2,1024,128]{4,3,2,1,0:T(8,128)(2,1)} %param.21) | copy-start | bytes 12582916
  164.1 18.3 %copy-start.4 = (f32[2,36,1024]{2,1,0:T(8,128)S(1)}, f32[2,36,1024]{2,1,0:T(8,128)}, u32[]{:S(2)}) copy-start(f32[2,36,1024]{2,1,0:T(8,128)} %get-tuple-element.103.cur_ref) | copy-start | bytes 884740
  164.1 19.4 %copy-start.3 = (f32[2,36,1024]{2,1,0:T(8,128)S(1)}, f32[2,36,1024]{2,1,0:T(8,128)}, u32[]{:S(2)}) copy-start(f32[2,36,1024]{2,1,0:T(8,128)} %get-tuple-element.101.one_ref.cur_ref) | copy-start | bytes 884740
  165.5 18.5 %copy-start.10 = (f32[2,36,36]{2,1,0:T(8,128)S(1)}, f32[2,36,36]{2,1,0:T(8,128)}, u32[]{:S(2)}) copy-start(f32[2,36,36]{2,1,0:T(8,128)} %get-tuple-element.25) | copy-start | bytes 31108
  165.5 18.6 %copy-start.13 = (f32[36,36]{1,0:T(8,128)S(1)}, f32[36,36]{1,0:T(8,128)}, u32[]{:S(2)}) copy-start(f32[36,36]{1,0:T(8,128)} %get-tuple-element.23) | copy-start | bytes 15556
  165.5 18.7 %copy-start.12 = (f32[36,36]{1,0:T(8,128)S(1)}, f32[36,36]{1,0:T(8,128)}, u32[]{:S(2)}) copy-start(f32[36,36]{1,0:T(8,128)} %get-tuple-element.24) | copy-start | bytes 15556
  165.5 57.8 %copy-start.7 = (f32[48,128]{1,0:T(8,128)S(1)}, f32[48,128]{1,0:T(8,128)}, u32[]{:S(2)}) copy-start(f32[48,128]{1,0:T(8,128)} %shard_map.98) | copy-start | bytes 73732

commit v14 on v12

--- a/solution.py
+++ b/solution.py
@@ -201,8 +201,10 @@
     pltpu.make_async_copy(own, slices.at[0], first_recv.at[0]).start()
     cross_ref[...] = gram(one_ref[0], cur_ref[0]) + gram(one_ref[1], cur_ref[1])
     self_ref[...] = gram(cur_ref[0], cur_ref[0]) + gram(cur_ref[1], cur_ref[1])
-    proj_ref[0] = gram(harm_ref[0], cur_ref[0]) + gram(harm_ref[1], cur_ref[1])
-    proj_ref[1] = gram(harm_ref[0], cur_ref[1]) - gram(harm_ref[1], cur_ref[0])
+    harm_real = harm_ref[:, 0, :]
+    harm_imag = harm_ref[:, 1, :]
+    proj_ref[0] = gram(harm_real, cur_ref[0]) + gram(harm_imag, cur_ref[1])
+    proj_ref[1] = gram(harm_real, cur_ref[1]) - gram(harm_imag, cur_ref[0])
     lax.fori_loop(0, (cols - 1) * blocks, forward, 0)
     mine = []
     for n in range(blocks):
@@ -232,7 +234,7 @@
             jax.ShapeDtypeStruct((blocks, parts * fields, elements), vector.dtype),
             jax.ShapeDtypeStruct((fields, fields), jnp.float32),
             jax.ShapeDtypeStruct((fields, fields), jnp.float32),
-            jax.ShapeDtypeStruct((2, harmonics.shape[1], fields), jnp.float32),
+            jax.ShapeDtypeStruct((2, harmonics.shape[0], fields), jnp.float32),
         ),
         in_specs=[pl.BlockSpec(memory_space=pltpu.VMEM)] * 4,
         out_specs=tuple(pl.BlockSpec(memory_space=pltpu.VMEM) for _ in range(5)),
@@ -450,7 +452,7 @@
     def apply_operator(vector, basis_one):
         rounded = vector.astype(jnp.bfloat16)
         near_pieces, far_pieces, cross, self_gram, proj = gather_pieces(
-            rounded, basis_one, vector, harmonics, blocks, half_band, width, 16 + len(ids)
+            rounded, basis_one, vector, jnp.transpose(harmonics, (1, 0, 2)), blocks, half_band, width, 16 + len(ids)
         )
         ids.append(None)
         total = operator_terms(near_pieces, far_pieces)

time: 228 us -> 226 us (level)
  no operation moved by 1% of the time
where the time goes in v14:
time: 226 us; the launch traced here: 223 us
  Pallas kernels  151 us (67%)
  other arithmetic  29.5 us (13%)
  matrix products  23 us (10%)
  local copies, waits for them, and re-layouts  17.2 us (8%)
    pallas_call x4, Pallas kernels, row_allreduce(): pl.pallas_call(partial(allreduce_kernel, inner, outer), out_shape=jax.Sha...  67.9 us
    pallas_call x2, Pallas kernels, gather_pieces(): pl.pallas_call(partial(gather_kernel, rows, cols, blocks, half), out_shap...  54 us
    pallas_call x2, Pallas kernels, col_reduce(): pl.pallas_call(partial(reduce_kernel, cols), out_shape=jax.ShapeDtypeStru...  29.4 us
    another operation x6, other arithmetic, lower_inverse(): lax.linalg.triangular_solve(lower, identity, left_side=True, lower=True)  12.9 us
    another operation x3, other arithmetic, body(): factor_inverse = lower_inverse(jnp.linalg.cholesky(normal))  7.26 us
    dot_general x2, matrix products, operator_terms(): jnp.einsum('caksf,kaef->cse', complex_lhs(near_vector, 1), near_blocks[0]...  5 us
    dot_general x5, matrix products, combine_rows(): return jnp.einsum('st,ctn->csn', matrix, vectors, precision=highest)  4.64 us

profile of v14, /device:TPU:24, one launch (start us, length us, event | category | flops | bytes accessed | tf_op | source)
XLA Modules:
  0.0 222.6 jit_solution(11511362109231817773)
XLA Ops:
  0.7 1.7 convolution_bitcast_fusion.12
  3.0 17.3 %shard_map.95 = f32[16,128]{1,0:T(8,128)} custom-call(f32[16,128]{1,0:T(8,128)} %pad_bitcast_fusion.1.x_ref), custom_call_target="tpu_custom_call" | custom-call | tf_op jit(solution)/shard_map/pallas_call | solution.py:95
  20.4 0.8 reshape.323
  21.3 3.3 %cholesky.81 = f32[36,36]{1,0:T(8,128)S(1)} custom-call(f32[36,36]{1,0:T(8,128)S(1)} %fusion.74), custom_call_target="Cholesky" | custom-call | tf_op jit(solution)/shard_map/jit(cholesky)/cholesky | solution.py:463
  25.9 2.8 %custom-call.15 = f32[1,36,36]{1,2,0:T(8,128)S(1)} custom-call(f32[1,36,36]{2,1,0:T(8,128)S(1)} %select_bitcast_fusion.1), custom_call_target="InvertDiagBlocksLowerTriangular" | custom-call | tf_op jit(solution)/shard_map/triangular_solve/custom-call.2 | solution.py:394
  28.9 2.2 fusion.122
  31.8 27.9 %shard_map.96 = (bf16[8,72,128]{2,1,0:T(8,128)(2,1)}, bf16[4,72,1024]{2,1,0:T(8,128)(2,1)}, f32[36,36]{1,0:T(8,128)}, f32[36,36]{1,0:T(8,128)}, f32[2,36,36]{2,1,0:T(8,128)}) custom-call(bf16[72,1024]{1,0:T(8,128)(2,1)} %reshape.324.v_ref, f32[2,36,1024]{2,1,0:T(8,128)} %get-tuple-element.101.one_ref.cur_ref, ...), custom_call_target="tpu_custom_call" | custom-call | tf_op jit(solution)/shard_map/pallas_call | solution.py:230
  59.7 1.9 fusion.24
  63.1 3.6 %fusion.7 = f32[2,36,1024]{2,1,0:T(8,128)S(1)} fusion(bf16[1,2,8,36,128]{4,3,2,1,0:T(8,128)(2,1)S(1)} %get-tuple-element.93, bf16[1,2,8,36,128]{4,3,2,1,0:T(8,128)(2,1)S(1)} %get-tuple-element.92, bf16[1,8,2,1024,128]{4,3,2,1,0:T(8,128)(2,1)} %param.21), kind=kOutput, calls=%fused_computation.9 | convolution fusion | flops 302137344 | bytes 4784128 | tf_op jit(solution)/shard_map/caksf,kaef->cse/dot_general | solution.py:422
  67.8 14.6 %shard_map.97 = f32[72,1024]{1,0:T(8,128)} custom-call(f32[72,1024]{1,0:T(8,128)} %reshape.326.x_ref), custom_call_target="tpu_custom_call" | custom-call | tf_op jit(solution)/shard_map/pallas_call | solution.py:340
  82.4 1.0 reshape.327
  84.9 17.4 %shard_map.98 = f32[48,128]{1,0:T(8,128)} custom-call(f32[48,128]{1,0:T(8,128)} %bitcast.264), custom_call_target="tpu_custom_call" | custom-call | tf_op jit(solution)/shard_map/pallas_call | solution.py:95
  102.3 0.8 fusion.121
  104.7 12.6 %shard_map.99 = f32[16,128]{1,0:T(8,128)} custom-call(f32[16,128]{1,0:T(8,128)} %pad_bitcast_fusion.x_ref), custom_call_target="tpu_custom_call" | custom-call | tf_op jit(solution)/shard_map/pallas_call | solution.py:95
  117.3 0.8 reshape.337
  118.3 3.3 %cholesky.92 = f32[36,36]{1,0:T(8,128)S(1)} custom-call(f32[36,36]{1,0:T(8,128)S(1)} %copy.51), custom_call_target="Cholesky" | custom-call | tf_op jit(solution)/shard_map/jit(cholesky)/cholesky | solution.py:471
  122.9 2.8 %custom-call.16 = f32[1,36,36]{1,2,0:T(8,128)S(1)} custom-call(f32[1,36,36]{2,1,0:T(8,128)S(1)} %select_bitcast_fusion), custom_call_target="InvertDiagBlocksLowerTriangular" | custom-call | tf_op jit(solution)/shard_map/triangular_solve/custom-call.2 | solution.py:394
  125.9 1.1 fusion.123
  127.8 26.1 %shard_map.100 = (bf16[8,72,128]{2,1,0:T(8,128)(2,1)}, bf16[4,72,1024]{2,1,0:T(8,128)(2,1)}, f32[36,36]{1,0:T(8,128)}, f32[36,36]{1,0:T(8,128)}, f32[2,36,36]{2,1,0:T(8,128)}) custom-call(bf16[72,1024]{1,0:T(8,128)(2,1)} %reshape.338.v_ref, f32[2,36,1024]{2,1,0:T(8,128)} %get-tuple-element.101.one_ref.cur_ref, f32[2,36,1024]{2,1,0:T(8,128)} %get-tuple-element.103.cur_ref, ...), custom_call_target="tpu_custom_call" | custom-call | tf_op jit(solution)/shard_map/pallas_call | solution.py:230
  153.9 1.6 fusion.20
  155.9 0.9 copy.52
  157.1 1.4 fusion.10
  159.6 14.8 %shard_map.101 = f32[72,1024]{1,0:T(8,128)} custom-call(f32[72,1024]{1,0:T(8,128)} %reshape.340.x_ref), custom_call_target="tpu_custom_call" | custom-call | tf_op jit(solution)/shard_map/pallas_call | solution.py:340
  174.4 1.0 reshape.341
  178.0 20.6 %shard_map.102 = f32[72,128]{1,0:T(8,128)} custom-call(f32[72,128]{1,0:T(8,128)} %bitcast.261), custom_call_target="tpu_custom_call" | custom-call | tf_op jit(solution)/shard_map/pallas_call | solution.py:95
  198.7 0.9 slice.97
  202.8 6.6 %cholesky.42 = f32[72,72]{1,0:T(8,128)S(1)} custom-call(f32[72,72]{1,0:T(8,128)S(1)} %fusion.64), custom_call_target="Cholesky" | custom-call | tf_op jit(solution)/shard_map/jit(cholesky)/cholesky | solution.py:511
  210.7 5.5 %custom-call.11 = f32[1,72,72]{1,2,0:T(8,128)S(1)} custom-call(f32[1,72,72]{2,1,0:T(8,128)S(1)} %fusion.53), custom_call_target="InvertDiagBlocksLowerTriangular" | custom-call | tf_op jit(solution)/shard_map/triangular_solve | solution.py:394
  216.4 0.8 fusion.78
  217.3 0.8 fusion.80
  219.0 0.8 slice.198
  221.6 0.9 copy.69
  (132 shorter events, 22.5 us)
Async XLA Ops:
  0.6 66.1 %copy-start = (bf16[1,4,2,64,1024]{4,3,2,1,0:T(8,128)(2,1)S(1)}, bf16[1,4,2,64,1024]{4,3,2,1,0:T(8,128)(2,1)}, u32[]{:S(2)}) copy-start(bf16[1,4,2,64,1024]{4,3,2,1,0:T(8,128)(2,1)} %param.22) | copy-start | bytes 3145732
  0.6 61.2 %copy-start.1 = (s32[1,8]{1,0:T(1,128)S(1)}, s32[1,8]{1,0:T(1,128)}, u32[]{:S(2)}) copy-start(s32[1,8]{1,0:T(1,128)} %param.24) | copy-start | bytes 100
  0.7 61.9 %copy-start.15 = (s32[1,4]{1,0:T(1,128)S(1)}, s32[1,4]{1,0:T(1,128)}, u32[]{:S(2)}) copy-start(s32[1,4]{1,0:T(1,128)} %param.25) | copy-start | bytes 52
  59.7 3.1 %copy-start.6 = (bf16[8,72,128]{2,1,0:T(8,128)(2,1)S(1)}, bf16[8,72,128]{2,1,0:T(8,128)(2,1)}, u32[]{:S(2)}) copy-start(bf16[8,72,128]{2,1,0:T(8,128)(2,1)} %get-tuple-element.17) | copy-start | bytes 442372
  63.0 20.4 %copy-start.2 = (f32[2,36,1024]{2,1,0:T(8,128)S(1)}, f32[2,36,1024]{2,1,0:T(8,128)}, u32[]{:S(2)}) copy-start(f32[2,36,1024]{2,1,0:T(8,128)} %get-tuple-element.101.one_ref.cur_ref) | copy-start | bytes 884740
  63.0 20.4 %copy-start.8 = (f32[1024]{0:T(1024)S(1)}, f32[1024]{0:T(1024)}, u32[]{:S(2)}) copy-start(f32[1024]{0:T(1024)} %param.20) | copy-start | bytes 12292
  63.1 20.9 %copy-start.9 = (f32[2,36,36]{2,1,0:T(8,128)S(1)}, f32[2,36,36]{2,1,0:T(8,128)}, u32[]{:S(2)}) copy-start(f32[2,36,36]{2,1,0:T(8,128)} %get-tuple-element.19) | copy-start | bytes 31108
  63.1 21.0 %copy-start.11 = (f32[36,36]{1,0:T(8,128)S(1)}, f32[36,36]{1,0:T(8,128)}, u32[]{:S(2)}) copy-start(f32[36,36]{1,0:T(8,128)} %get-tuple-element.20) | copy-start | bytes 15556
  67.0 86.9 %copy-start.5 = (bf16[1,4,2,64,1024]{4,3,2,1,0:T(8,128)(2,1)S(1)}, bf16[1,4,2,64,1024]{4,3,2,1,0:T(8,128)(2,1)}, u32[]{:S(2)}) copy-start(bf16[1,4,2,64,1024]{4,3,2,1,0:T(8,128)(2,1)} %param.23) | copy-start | bytes 3145732
  153.9 3.1 %copy-start.14 = (bf16[1,8,2,1024,128]{4,3,2,1,0:T(8,128)(2,1)S(1)}, bf16[1,8,2,1024,128]{4,3,2,1,0:T(8,128)(2,1)}, u32[]{:S(2)}) copy-start(bf16[1,8,2,1024,128]{4,3,2,1,0:T(8,128)(2,1)} %param.21) | copy-start | bytes 12582916
  157.0 18.3 %copy-start.4 = (f32[2,36,1024]{2,1,0:T(8,128)S(1)}, f32[2,36,1024]{2,1,0:T(8,128)}, u32[]{:S(2)}) copy-start(f32[2,36,1024]{2,1,0:T(8,128)} %get-tuple-element.103.cur_ref) | copy-start | bytes 884740
  157.1 19.4 %copy-start.3 = (f32[2,36,1024]{2,1,0:T(8,128)S(1)}, f32[2,36,1024]{2,1,0:T(8,128)}, u32[]{:S(2)}) copy-start(f32[2,36,1024]{2,1,0:T(8,128)} %get-tuple-element.101.one_ref.cur_ref) | copy-start | bytes 884740
  158.5 18.5 %copy-start.10 = (f32[2,36,36]{2,1,0:T(8,128)S(1)}, f32[2,36,36]{2,1,0:T(8,128)}, u32[]{:S(2)}) copy-start(f32[2,36,36]{2,1,0:T(8,128)} %get-tuple-element.25) | copy-start | bytes 31108
  158.5 18.6 %copy-start.13 = (f32[36,36]{1,0:T(8,128)S(1)}, f32[36,36]{1,0:T(8,128)}, u32[]{:S(2)}) copy-start(f32[36,36]{1,0:T(8,128)} %get-tuple-element.23) | copy-start | bytes 15556
  158.5 18.7 %copy-start.12 = (f32[36,36]{1,0:T(8,128)S(1)}, f32[36,36]{1,0:T(8,128)}, u32[]{:S(2)}) copy-start(f32[36,36]{1,0:T(8,128)} %get-tuple-element.24) | copy-start | bytes 15556
  158.5 60.1 %copy-start.7 = (f32[48,128]{1,0:T(8,128)S(1)}, f32[48,128]{1,0:T(8,128)}, u32[]{:S(2)}) copy-start(f32[48,128]{1,0:T(8,128)} %shard_map.98) | copy-start | bytes 73732

commit v15 on v14

--- a/solution.py
+++ b/solution.py
@@ -355,6 +355,23 @@
     return summed.reshape(partial_sum.shape)
 
 
+def combine_kernel(first_ref, second_ref, one_ref, two_ref, o_ref):
+    for part in range(one_ref.shape[0]):
+        o_ref[:, part, :] = jnp.dot(
+            first_ref[...], one_ref[part], precision=highest, preferred_element_type=jnp.float32
+        ) + jnp.dot(second_ref[...], two_ref[part], precision=highest, preferred_element_type=jnp.float32)
+
+
+def final_combine(first_weights, second_weights, basis_one, basis_two):
+    parts, fields, elements = basis_one.shape
+    return pl.pallas_call(
+        combine_kernel,
+        out_shape=jax.ShapeDtypeStruct((fields, parts, elements), jnp.float32),
+        in_specs=[pl.BlockSpec(memory_space=pltpu.VMEM)] * 4,
+        out_specs=pl.BlockSpec(memory_space=pltpu.VMEM),
+    )(first_weights, second_weights, basis_one, basis_two)
+
+
 def row_psum(ids, *arrays):
     flat = [a.reshape(-1) for a in arrays]
     sizes = [f.shape[0] for f in flat]
@@ -512,7 +529,7 @@
     weights = matmul(factor_inverse.T, matmul(factor_inverse, target.T)).T
     first_weights = weights[:, :fields]
     second_weights = weights[:, fields:]
-    solution = combine_rows(first_weights, basis_one) + combine_rows(second_weights, basis_two)
+    solution = final_combine(first_weights, second_weights, basis_one, basis_two).transpose(1, 0, 2)
     coefficients = jnp.einsum(
         "cmt,st->cms", harmonics_one, first_weights, precision=highest
     ) + jnp.einsum("cmt,st->cms", harmonics_two, second_weights, precision=highest)

time: 226 us -> 227 us (level)
  Pallas kernels: 151 us -> 154 us
    pallas_call x0 -> x1, Pallas kernels: none -> 2.5 us  [final_combine(): pl.pallas_call(combine_kernel, out_shape=jax.ShapeDtypeStruct((fields, pa...]
    dot_general x5 -> x3, matrix products: 4.64 us -> 3.78 us  [combine_rows(): return jnp.einsum('st,ctn->csn', matrix, vectors, precision=highest)]
where the time goes in v15:
time: 227 us; the launch traced here: 224 us
  Pallas kernels  154 us (68%)
  other arithmetic  29.6 us (13%)
  matrix products  22.3 us (10%)
  local copies, waits for them, and re-layouts  16.9 us (7%)
    pallas_call x4, Pallas kernels, row_allreduce(): pl.pallas_call(partial(allreduce_kernel, inner, outer), out_shape=jax.Sha...  68 us
    pallas_call x2, Pallas kernels, gather_pieces(): pl.pallas_call(partial(gather_kernel, rows, cols, blocks, half), out_shap...  54 us
    pallas_call x2, Pallas kernels, col_reduce(): pl.pallas_call(partial(reduce_kernel, cols), out_shape=jax.ShapeDtypeStru...  29.4 us
    another operation x6, other arithmetic, lower_inverse(): lax.linalg.triangular_solve(lower, identity, left_side=True, lower=True)  13 us
    another operation x3, other arithmetic, body(): factor_inverse = lower_inverse(jnp.linalg.cholesky(normal))  7.26 us
    dot_general x2, matrix products, operator_terms(): jnp.einsum('caksf,kaef->cse', complex_lhs(near_vector, 1), near_blocks[0]...  5 us

profile of v15, /device:TPU:24, one launch (start us, length us, event | category | flops | bytes accessed | tf_op | source)
XLA Modules:
  0.0 224.2 jit_solution(2873971868587238414)
XLA Ops:
  0.7 1.7 convolution_bitcast_fusion.12
  3.0 17.3 %shard_map.95 = f32[16,128]{1,0:T(8,128)} custom-call(f32[16,128]{1,0:T(8,128)} %pad_bitcast_fusion.1.x_ref), custom_call_target="tpu_custom_call" | custom-call | tf_op jit(solution)/shard_map/pallas_call | solution.py:95
  20.4 0.8 reshape.323
  21.3 3.3 %cholesky.81 = f32[36,36]{1,0:T(8,128)S(1)} custom-call(f32[36,36]{1,0:T(8,128)S(1)} %fusion.76), custom_call_target="Cholesky" | custom-call | tf_op jit(solution)/shard_map/jit(cholesky)/cholesky | solution.py:480
  25.9 2.8 %custom-call.15 = f32[1,36,36]{1,2,0:T(8,128)S(1)} custom-call(f32[1,36,36]{2,1,0:T(8,128)S(1)} %select_bitcast_fusion.1), custom_call_target="InvertDiagBlocksLowerTriangular" | custom-call | tf_op jit(solution)/shard_map/triangular_solve/custom-call.2 | solution.py:411
  28.9 2.2 fusion.125
  31.8 27.9 %shard_map.96 = (bf16[8,72,128]{2,1,0:T(8,128)(2,1)}, bf16[4,72,1024]{2,1,0:T(8,128)(2,1)}, f32[36,36]{1,0:T(8,128)}, f32[36,36]{1,0:T(8,128)}, f32[2,36,36]{2,1,0:T(8,128)}) custom-call(bf16[72,1024]{1,0:T(8,128)(2,1)} %reshape.324.v_ref, f32[2,36,1024]{2,1,0:T(8,128)} %get-tuple-element.103.one_ref.cur_ref, ...), custom_call_target="tpu_custom_call" | custom-call | tf_op jit(solution)/shard_map/pallas_call | solution.py:230
  59.7 1.9 fusion.23
  63.0 3.6 %fusion.6 = f32[2,36,1024]{2,1,0:T(8,128)S(1)} fusion(bf16[1,2,8,36,128]{4,3,2,1,0:T(8,128)(2,1)S(1)} %get-tuple-element.93, bf16[1,2,8,36,128]{4,3,2,1,0:T(8,128)(2,1)S(1)} %get-tuple-element.92, bf16[1,8,2,1024,128]{4,3,2,1,0:T(8,128)(2,1)} %param.21), kind=kOutput, calls=%fused_computation.7 | convolution fusion | flops 302137344 | bytes 4784128 | tf_op jit(solution)/shard_map/caksf,kaef->cse/dot_general | solution.py:439
  67.8 14.6 %shard_map.97 = f32[72,1024]{1,0:T(8,128)} custom-call(f32[72,1024]{1,0:T(8,128)} %reshape.326.x_ref), custom_call_target="tpu_custom_call" | custom-call | tf_op jit(solution)/shard_map/pallas_call | solution.py:340
  82.4 1.0 reshape.327
  84.9 17.4 %shard_map.98 = f32[48,128]{1,0:T(8,128)} custom-call(f32[48,128]{1,0:T(8,128)} %bitcast.260), custom_call_target="tpu_custom_call" | custom-call | tf_op jit(solution)/shard_map/pallas_call | solution.py:95
  102.3 0.8 fusion.123
  104.7 12.6 %shard_map.99 = f32[16,128]{1,0:T(8,128)} custom-call(f32[16,128]{1,0:T(8,128)} %pad_bitcast_fusion.x_ref), custom_call_target="tpu_custom_call" | custom-call | tf_op jit(solution)/shard_map/pallas_call | solution.py:95
  117.3 0.8 reshape.337
  118.3 3.3 %cholesky.92 = f32[36,36]{1,0:T(8,128)S(1)} custom-call(f32[36,36]{1,0:T(8,128)S(1)} %copy.50), custom_call_target="Cholesky" | custom-call | tf_op jit(solution)/shard_map/jit(cholesky)/cholesky | solution.py:488
  123.1 2.8 %custom-call.16 = f32[1,36,36]{1,2,0:T(8,128)S(1)} custom-call(f32[1,36,36]{2,1,0:T(8,128)S(1)} %select_bitcast_fusion), custom_call_target="InvertDiagBlocksLowerTriangular" | custom-call | tf_op jit(solution)/shard_map/triangular_solve/custom-call.2 | solution.py:411
  126.1 1.2 fusion.126
  127.9 26.1 %shard_map.100 = (bf16[8,72,128]{2,1,0:T(8,128)(2,1)}, bf16[4,72,1024]{2,1,0:T(8,128)(2,1)}, f32[36,36]{1,0:T(8,128)}, f32[36,36]{1,0:T(8,128)}, f32[2,36,36]{2,1,0:T(8,128)}) custom-call(bf16[72,1024]{1,0:T(8,128)(2,1)} %reshape.338.v_ref, f32[2,36,1024]{2,1,0:T(8,128)} %get-tuple-element.103.one_ref.cur_ref, ...), custom_call_target="tpu_custom_call" | custom-call | tf_op jit(solution)/shard_map/pallas_call | solution.py:230
  154.1 1.7 fusion.19
  156.1 0.9 copy.51
  157.2 1.4 fusion.9
  159.8 14.8 %shard_map.101 = f32[72,1024]{1,0:T(8,128)} custom-call(f32[72,1024]{1,0:T(8,128)} %reshape.340.x_ref), custom_call_target="tpu_custom_call" | custom-call | tf_op jit(solution)/shard_map/pallas_call | solution.py:340
  174.5 1.0 reshape.341
  178.2 20.7 %shard_map.102 = f32[72,128]{1,0:T(8,128)} custom-call(f32[72,128]{1,0:T(8,128)} %bitcast.257), custom_call_target="tpu_custom_call" | custom-call | tf_op jit(solution)/shard_map/pallas_call | solution.py:95
  198.9 0.9 slice.97
  200.1 0.9 convolution_add_fusion.3
  203.0 6.6 %cholesky.42 = f32[72,72]{1,0:T(8,128)S(1)} custom-call(f32[72,72]{1,0:T(8,128)S(1)} %fusion.63), custom_call_target="Cholesky" | custom-call | tf_op jit(solution)/shard_map/jit(cholesky)/cholesky | solution.py:528
  211.0 5.5 %custom-call.11 = f32[1,72,72]{1,2,0:T(8,128)S(1)} custom-call(f32[1,72,72]{2,1,0:T(8,128)S(1)} %fusion.52), custom_call_target="InvertDiagBlocksLowerTriangular" | custom-call | tf_op jit(solution)/shard_map/triangular_solve | solution.py:411
  216.7 0.8 fusion.78
  219.2 0.8 slice.198
  221.7 2.5 %shard_map.103 = f32[36,2,1024]{2,1,0:T(2,128)} custom-call(f32[36,36]{1,0:T(8,128)} %get-tuple-element.101.first_ref, f32[36,36]{1,0:T(8,128)} %get-tuple-element.100.second_ref, f32[2,36,1024]{2,1,0:T(8,128)} %get-tuple-element.103.one_ref.cur_ref, f32[2,36,1024]{2,1,0:T(8,128)} %get-tuple-element.105.cur_ref.two_ref), custom_call_target="tpu_custom_call" | custom-call | tf_op jit(solution)/shard_map/pallas_call | solution.py:367
  (131 shorter events, 22.4 us)
Async XLA Ops:
  0.6 66.0 %copy-start = (bf16[1,4,2,64,1024]{4,3,2,1,0:T(8,128)(2,1)S(1)}, bf16[1,4,2,64,1024]{4,3,2,1,0:T(8,128)(2,1)}, u32[]{:S(2)}) copy-start(bf16[1,4,2,64,1024]{4,3,2,1,0:T(8,128)(2,1)} %param.22) | copy-start | bytes 3145732
  0.6 61.2 %copy-start.1 = (s32[1,8]{1,0:T(1,128)S(1)}, s32[1,8]{1,0:T(1,128)}, u32[]{:S(2)}) copy-start(s32[1,8]{1,0:T(1,128)} %param.24) | copy-start | bytes 100
  0.7 61.8 %copy-start.15 = (s32[1,4]{1,0:T(1,128)S(1)}, s32[1,4]{1,0:T(1,128)}, u32[]{:S(2)}) copy-start(s32[1,4]{1,0:T(1,128)} %param.25) | copy-start | bytes 52
  59.7 3.1 %copy-start.6 = (bf16[8,72,128]{2,1,0:T(8,128)(2,1)S(1)}, bf16[8,72,128]{2,1,0:T(8,128)(2,1)}, u32[]{:S(2)}) copy-start(bf16[8,72,128]{2,1,0:T(8,128)(2,1)} %get-tuple-element.17) | copy-start | bytes 442372
  63.0 20.4 %copy-start.2 = (f32[2,36,1024]{2,1,0:T(8,128)S(1)}, f32[2,36,1024]{2,1,0:T(8,128)}, u32[]{:S(2)}) copy-start(f32[2,36,1024]{2,1,0:T(8,128)} %get-tuple-element.103.one_ref.cur_ref) | copy-start | bytes 884740
  63.0 20.4 %copy-start.8 = (f32[1024]{0:T(1024)S(1)}, f32[1024]{0:T(1024)}, u32[]{:S(2)}) copy-start(f32[1024]{0:T(1024)} %param.20) | copy-start | bytes 12292
  63.0 21.0 %copy-start.9 = (f32[2,36,36]{2,1,0:T(8,128)S(1)}, f32[2,36,36]{2,1,0:T(8,128)}, u32[]{:S(2)}) copy-start(f32[2,36,36]{2,1,0:T(8,128)} %get-tuple-element.19) | copy-start | bytes 31108
  63.0 21.1 %copy-start.11 = (f32[36,36]{1,0:T(8,128)S(1)}, f32[36,36]{1,0:T(8,128)}, u32[]{:S(2)}) copy-start(f32[36,36]{1,0:T(8,128)} %get-tuple-element.20) | copy-start | bytes 15556
  67.0 87.0 %copy-start.5 = (bf16[1,4,2,64,1024]{4,3,2,1,0:T(8,128)(2,1)S(1)}, bf16[1,4,2,64,1024]{4,3,2,1,0:T(8,128)(2,1)}, u32[]{:S(2)}) copy-start(bf16[1,4,2,64,1024]{4,3,2,1,0:T(8,128)(2,1)} %param.23) | copy-start | bytes 3145732
  154.0 3.2 %copy-start.14 = (bf16[1,8,2,1024,128]{4,3,2,1,0:T(8,128)(2,1)S(1)}, bf16[1,8,2,1024,128]{4,3,2,1,0:T(8,128)(2,1)}, u32[]{:S(2)}) copy-start(bf16[1,8,2,1024,128]{4,3,2,1,0:T(8,128)(2,1)} %param.21) | copy-start | bytes 12582916
  157.2 18.3 %copy-start.4 = (f32[2,36,1024]{2,1,0:T(8,128)S(1)}, f32[2,36,1024]{2,1,0:T(8,128)}, u32[]{:S(2)}) copy-start(f32[2,36,1024]{2,1,0:T(8,128)} %get-tuple-element.105.cur_ref.two_ref) | copy-start | bytes 884740
  157.2 19.4 %copy-start.3 = (f32[2,36,1024]{2,1,0:T(8,128)S(1)}, f32[2,36,1024]{2,1,0:T(8,128)}, u32[]{:S(2)}) copy-start(f32[2,36,1024]{2,1,0:T(8,128)} %get-tuple-element.103.one_ref.cur_ref) | copy-start | bytes 884740
  158.6 18.5 %copy-start.10 = (f32[2,36,36]{2,1,0:T(8,128)S(1)}, f32[2,36,36]{2,1,0:T(8,128)}, u32[]{:S(2)}) copy-start(f32[2,36,36]{2,1,0:T(8,128)} %get-tuple-element.25) | copy-start | bytes 31108
  158.6 18.6 %copy-start.13 = (f32[36,36]{1,0:T(8,128)S(1)}, f32[36,36]{1,0:T(8,128)}, u32[]{:S(2)}) copy-start(f32[36,36]{1,0:T(8,128)} %get-tuple-element.23) | copy-start | bytes 15556
  158.6 18.7 %copy-start.12 = (f32[36,36]{1,0:T(8,128)S(1)}, f32[36,36]{1,0:T(8,128)}, u32[]{:S(2)}) copy-start(f32[36,36]{1,0:T(8,128)} %get-tuple-element.24) | copy-start | bytes 15556
  158.6 60.2 %copy-start.7 = (f32[48,128]{1,0:T(8,128)S(1)}, f32[48,128]{1,0:T(8,128)}, u32[]{:S(2)}) copy-start(f32[48,128]{1,0:T(8,128)} %shard_map.98) | copy-start | bytes 73732

commit v16 on v14

--- a/solution.py
+++ b/solution.py
@@ -356,6 +356,13 @@
 
 
 def row_psum(ids, *arrays):
+    if len(arrays) == 1 and arrays[0].ndim == 2 and arrays[0].shape[1] <= 128:
+        matrix = arrays[0]
+        rows, columns = matrix.shape
+        padded = jnp.pad(matrix, ((0, -rows % 8), (0, 128 - columns)))
+        summed = row_allreduce(padded, len(ids))
+        ids.append(None)
+        return summed[:rows, :columns]
     flat = [a.reshape(-1) for a in arrays]
     sizes = [f.shape[0] for f in flat]
     total = sum(sizes)

time: 226 us -> 230 us (1.018)
  Pallas kernels: 151 us -> 155 us
    pallas_call x4, Pallas kernels: 67.9 us -> 71.6 us  [row_allreduce(): pl.pallas_call(partial(allreduce_kernel, inner, outer), out_shape=jax.Sha...]
where the time goes in v16:
time: 230 us; the launch traced here: 227 us
  Pallas kernels  155 us (67%)
  other arithmetic  30.8 us (13%)
  matrix products  22.9 us (10%)
  local copies, waits for them, and re-layouts  16.9 us (7%)
    pallas_call x4, Pallas kernels, row_allreduce(): pl.pallas_call(partial(allreduce_kernel, inner, outer), out_shape=jax.Sha...  71.6 us
    pallas_call x2, Pallas kernels, gather_pieces(): pl.pallas_call(partial(gather_kernel, rows, cols, blocks, half), out_shap...  54.4 us
    pallas_call x2, Pallas kernels, col_reduce(): pl.pallas_call(partial(reduce_kernel, cols), out_shape=jax.ShapeDtypeStru...  29 us
    another operation x6, other arithmetic, lower_inverse(): lax.linalg.triangular_solve(lower, identity, left_side=True, lower=True)  12.8 us
    another operation x3, other arithmetic, body(): factor_inverse = lower_inverse(jnp.linalg.cholesky(normal))  7.26 us
    dot_general x2, matrix products, operator_terms(): jnp.einsum('caksf,kaef->cse', complex_lhs(near_vector, 1), near_blocks[0]...  5 us
    dot_general x5, matrix products, combine_rows(): return jnp.einsum('st,ctn->csn', matrix, vectors, precision=highest)  4.66 us

profile of v16, /device:TPU:24, one launch (start us, length us, event | category | flops | bytes accessed | tf_op | source)
XLA Modules:
  0.0 227.1 jit_solution(1593184001651590917)
XLA Ops:
  0.7 1.7 convolution_bitcast_fusion.12
  2.9 19.0 %shard_map.95 = f32[40,128]{1,0:T(8,128)} custom-call(f32[40,128]{1,0:T(8,128)} %pad.8.x_ref), custom_call_target="tpu_custom_call" | custom-call | tf_op jit(solution)/shard_map/pallas_call | solution.py:95
  22.0 0.8 copy.102
  23.6 3.3 %cholesky.81 = f32[36,36]{1,0:T(8,128)S(1)} custom-call(f32[36,36]{1,0:T(8,128)S(1)} %fusion.74), custom_call_target="Cholesky" | custom-call | tf_op jit(solution)/shard_map/jit(cholesky)/cholesky | solution.py:470
  28.1 2.8 %custom-call.15 = f32[1,36,36]{1,2,0:T(8,128)S(1)} custom-call(f32[1,36,36]{2,1,0:T(8,128)S(1)} %select_bitcast_fusion.1), custom_call_target="InvertDiagBlocksLowerTriangular" | custom-call | tf_op jit(solution)/shard_map/triangular_solve/custom-call.2 | solution.py:401
  31.1 2.2 fusion.122
  34.0 28.3 %shard_map.96 = (bf16[8,72,128]{2,1,0:T(8,128)(2,1)}, bf16[4,72,1024]{2,1,0:T(8,128)(2,1)}, f32[36,36]{1,0:T(8,128)}, f32[36,36]{1,0:T(8,128)}, f32[2,36,36]{2,1,0:T(8,128)}) custom-call(bf16[72,1024]{1,0:T(8,128)(2,1)} %reshape.296.v_ref, f32[2,36,1024]{2,1,0:T(8,128)} %get-tuple-element.101.one_ref.cur_ref, ...), custom_call_target="tpu_custom_call" | custom-call | tf_op jit(solution)/shard_map/pallas_call | solution.py:230
  62.4 1.9 fusion.24
  65.7 3.6 %fusion.7 = f32[2,36,1024]{2,1,0:T(8,128)S(1)} fusion(bf16[1,2,8,36,128]{4,3,2,1,0:T(8,128)(2,1)S(1)} %get-tuple-element.93, bf16[1,2,8,36,128]{4,3,2,1,0:T(8,128)(2,1)S(1)} %get-tuple-element.92, bf16[1,8,2,1024,128]{4,3,2,1,0:T(8,128)(2,1)} %param.21), kind=kOutput, calls=%fused_computation.9 | convolution fusion | flops 302137344 | bytes 4784128 | tf_op jit(solution)/shard_map/caksf,kaef->cse/dot_general | solution.py:429
  69.7 0.7 reshape.298.x_ref
  70.4 14.5 %shard_map.97 = f32[72,1024]{1,0:T(8,128)} custom-call(f32[72,1024]{1,0:T(8,128)} %reshape.298.x_ref), custom_call_target="tpu_custom_call" | custom-call | tf_op jit(solution)/shard_map/pallas_call | solution.py:340
  84.9 1.0 reshape.299
  87.4 17.7 %shard_map.98 = f32[48,128]{1,0:T(8,128)} custom-call(f32[48,128]{1,0:T(8,128)} %bitcast.260), custom_call_target="tpu_custom_call" | custom-call | tf_op jit(solution)/shard_map/pallas_call | solution.py:95
  105.1 0.8 fusion.121
  107.4 13.6 %shard_map.99 = f32[40,128]{1,0:T(8,128)} custom-call(f32[40,128]{1,0:T(8,128)} %pad.9.x_ref), custom_call_target="tpu_custom_call" | custom-call | tf_op jit(solution)/shard_map/pallas_call | solution.py:95
  121.0 0.8 copy.52
  122.7 3.3 %cholesky.92 = f32[36,36]{1,0:T(8,128)S(1)} custom-call(f32[36,36]{1,0:T(8,128)S(1)} %copy.53), custom_call_target="Cholesky" | custom-call | tf_op jit(solution)/shard_map/jit(cholesky)/cholesky | solution.py:478
  127.2 2.8 %custom-call.16 = f32[1,36,36]{1,2,0:T(8,128)S(1)} custom-call(f32[1,36,36]{2,1,0:T(8,128)S(1)} %select_bitcast_fusion), custom_call_target="InvertDiagBlocksLowerTriangular" | custom-call | tf_op jit(solution)/shard_map/triangular_solve/custom-call.2 | solution.py:401
  130.3 1.2 fusion.123
  132.1 26.1 %shard_map.100 = (bf16[8,72,128]{2,1,0:T(8,128)(2,1)}, bf16[4,72,1024]{2,1,0:T(8,128)(2,1)}, f32[36,36]{1,0:T(8,128)}, f32[36,36]{1,0:T(8,128)}, f32[2,36,36]{2,1,0:T(8,128)}) custom-call(bf16[72,1024]{1,0:T(8,128)(2,1)} %reshape.306.v_ref, f32[2,36,1024]{2,1,0:T(8,128)} %get-tuple-element.101.one_ref.cur_ref, f32[2,36,1024]{2,1,0:T(8,128)} %get-tuple-element.103.cur_ref, ...), custom_call_target="tpu_custom_call" | custom-call | tf_op jit(solution)/shard_map/pallas_call | solution.py:230
  158.2 1.6 fusion.20
  160.2 0.9 copy.54
  161.3 1.4 fusion.10
  163.1 0.7 reshape.308.x_ref
  163.9 14.5 %shard_map.101 = f32[72,1024]{1,0:T(8,128)} custom-call(f32[72,1024]{1,0:T(8,128)} %reshape.308.x_ref), custom_call_target="tpu_custom_call" | custom-call | tf_op jit(solution)/shard_map/pallas_call | solution.py:340
  178.4 1.0 reshape.309
  182.0 21.2 %shard_map.102 = f32[72,128]{1,0:T(8,128)} custom-call(f32[72,128]{1,0:T(8,128)} %bitcast.257), custom_call_target="tpu_custom_call" | custom-call | tf_op jit(solution)/shard_map/pallas_call | solution.py:95
  203.3 0.9 slice.97
  207.4 6.6 %cholesky.42 = f32[72,72]{1,0:T(8,128)S(1)} custom-call(f32[72,72]{1,0:T(8,128)S(1)} %fusion.64), custom_call_target="Cholesky" | custom-call | tf_op jit(solution)/shard_map/jit(cholesky)/cholesky | solution.py:518
  215.3 5.5 %custom-call.11 = f32[1,72,72]{1,2,0:T(8,128)S(1)} custom-call(f32[1,72,72]{2,1,0:T(8,128)S(1)} %fusion.53), custom_call_target="InvertDiagBlocksLowerTriangular" | custom-call | tf_op jit(solution)/shard_map/triangular_solve | solution.py:401
  223.4 0.8 slice.196
  226.1 0.9 copy.71
  (130 shorter events, 23.4 us)
Async XLA Ops:
  0.6 68.7 %copy-start = (bf16[1,4,2,64,1024]{4,3,2,1,0:T(8,128)(2,1)S(1)}, bf16[1,4,2,64,1024]{4,3,2,1,0:T(8,128)(2,1)}, u32[]{:S(2)}) copy-start(bf16[1,4,2,64,1024]{4,3,2,1,0:T(8,128)(2,1)} %param.22) | copy-start | bytes 3145732
  0.6 63.8 %copy-start.1 = (s32[1,8]{1,0:T(1,128)S(1)}, s32[1,8]{1,0:T(1,128)}, u32[]{:S(2)}) copy-start(s32[1,8]{1,0:T(1,128)} %param.24) | copy-start | bytes 100
  0.7 64.5 %copy-start.16 = (s32[1,4]{1,0:T(1,128)S(1)}, s32[1,4]{1,0:T(1,128)}, u32[]{:S(2)}) copy-start(s32[1,4]{1,0:T(1,128)} %param.25) | copy-start | bytes 52
  62.3 3.1 %copy-start.7 = (bf16[8,72,128]{2,1,0:T(8,128)(2,1)S(1)}, bf16[8,72,128]{2,1,0:T(8,128)(2,1)}, u32[]{:S(2)}) copy-start(bf16[8,72,128]{2,1,0:T(8,128)(2,1)} %get-tuple-element.17) | copy-start | bytes 442372
  65.7 20.3 %copy-start.2 = (f32[2,36,1024]{2,1,0:T(8,128)S(1)}, f32[2,36,1024]{2,1,0:T(8,128)}, u32[]{:S(2)}) copy-start(f32[2,36,1024]{2,1,0:T(8,128)} %get-tuple-element.101.one_ref.cur_ref) | copy-start | bytes 884740
  65.7 20.3 %copy-start.9 = (f32[1024]{0:T(1024)S(1)}, f32[1024]{0:T(1024)}, u32[]{:S(2)}) copy-start(f32[1024]{0:T(1024)} %param.20) | copy-start | bytes 12292
  65.7 20.8 %copy-start.10 = (f32[2,36,36]{2,1,0:T(8,128)S(1)}, f32[2,36,36]{2,1,0:T(8,128)}, u32[]{:S(2)}) copy-start(f32[2,36,36]{2,1,0:T(8,128)} %get-tuple-element.19) | copy-start | bytes 31108
  65.7 20.9 %copy-start.12 = (f32[36,36]{1,0:T(8,128)S(1)}, f32[36,36]{1,0:T(8,128)}, u32[]{:S(2)}) copy-start(f32[36,36]{1,0:T(8,128)} %get-tuple-element.20) | copy-start | bytes 15556
  69.7 88.5 %copy-start.5 = (bf16[1,4,2,64,1024]{4,3,2,1,0:T(8,128)(2,1)S(1)}, bf16[1,4,2,64,1024]{4,3,2,1,0:T(8,128)(2,1)}, u32[]{:S(2)}) copy-start(bf16[1,4,2,64,1024]{4,3,2,1,0:T(8,128)(2,1)} %param.23) | copy-start | bytes 3145732
  158.2 3.1 %copy-start.15 = (bf16[1,8,2,1024,128]{4,3,2,1,0:T(8,128)(2,1)S(1)}, bf16[1,8,2,1024,128]{4,3,2,1,0:T(8,128)(2,1)}, u32[]{:S(2)}) copy-start(bf16[1,8,2,1024,128]{4,3,2,1,0:T(8,128)(2,1)} %param.21) | copy-start | bytes 12582916
  161.3 18.1 %copy-start.4 = (f32[2,36,1024]{2,1,0:T(8,128)S(1)}, f32[2,36,1024]{2,1,0:T(8,128)}, u32[]{:S(2)}) copy-start(f32[2,36,1024]{2,1,0:T(8,128)} %get-tuple-element.103.cur_ref) | copy-start | bytes 884740
  161.3 19.1 %copy-start.3 = (f32[2,36,1024]{2,1,0:T(8,128)S(1)}, f32[2,36,1024]{2,1,0:T(8,128)}, u32[]{:S(2)}) copy-start(f32[2,36,1024]{2,1,0:T(8,128)} %get-tuple-element.101.one_ref.cur_ref) | copy-start | bytes 884740
  162.7 18.3 %copy-start.11 = (f32[2,36,36]{2,1,0:T(8,128)S(1)}, f32[2,36,36]{2,1,0:T(8,128)}, u32[]{:S(2)}) copy-start(f32[2,36,36]{2,1,0:T(8,128)} %get-tuple-element.25) | copy-start | bytes 31108
  162.7 18.4 %copy-start.14 = (f32[36,36]{1,0:T(8,128)S(1)}, f32[36,36]{1,0:T(8,128)}, u32[]{:S(2)}) copy-start(f32[36,36]{1,0:T(8,128)} %get-tuple-element.23) | copy-start | bytes 15556
  162.7 18.5 %copy-start.13 = (f32[36,36]{1,0:T(8,128)S(1)}, f32[36,36]{1,0:T(8,128)}, u32[]{:S(2)}) copy-start(f32[36,36]{1,0:T(8,128)} %get-tuple-element.24) | copy-start | bytes 15556
  162.8 42.5 %copy-start.6 = (f32[40,128]{1,0:T(8,128)S(1)}, f32[40,128]{1,0:T(8,128)}, u32[]{:S(2)}) copy-start(f32[40,128]{1,0:T(8,128)} %shard_map.99) | copy-start | bytes 61444
  162.8 60.3 %copy-start.8 = (f32[48,128]{1,0:T(8,128)S(1)}, f32[48,128]{1,0:T(8,128)}, u32[]{:S(2)}) copy-start(f32[48,128]{1,0:T(8,128)} %shard_map.98) | copy-start | bytes 73732

commit v17 on v14

--- a/solution.py
+++ b/solution.py
@@ -460,7 +460,7 @@
         ids.append(None)
         return summed + diagonal[None, None, :] * vector, cross, self_gram, proj
 
-    lower_first = jnp.linalg.cholesky(row_psum(ids, inner_products(incident, incident)))
+    lower_first = lax.linalg.cholesky(row_psum(ids, inner_products(incident, incident)), symmetrize_input=False)
     basis_one = combine_rows(lower_inverse(lower_first), incident)
     image, _, self_one, harmonics_one = apply_operator(basis_one, basis_one)
     coupling_one, harmonics_one, self_one = row_psum(
@@ -468,7 +468,7 @@
     )
     rest = image - combine_rows(coupling_one, basis_one)
     gram_one = row_psum(ids, inner_products(rest, rest))
-    lower_second = jnp.linalg.cholesky(gram_one)
+    lower_second = lax.linalg.cholesky(gram_one, symmetrize_input=False)
     basis_two = combine_rows(lower_inverse(lower_second), rest)
     image, cross, self_two, harmonics_two = apply_operator(basis_two, basis_one)
     coupling_onetwo, coupling_two, image_gram, cross, self_two, harmonics_two = row_psum(
@@ -508,7 +508,7 @@
     target = jnp.concatenate(
         [matmul(lower_first, coupling_one.T), matmul(lower_first, coupling_onetwo.T)], axis=1
     )
-    factor_inverse = lower_inverse(jnp.linalg.cholesky(normal))
+    factor_inverse = lower_inverse(lax.linalg.cholesky(normal, symmetrize_input=False))
     weights = matmul(factor_inverse.T, matmul(factor_inverse, target.T)).T
     first_weights = weights[:, :fields]
     second_weights = weights[:, fields:]

time: 226 us -> 226 us (level)
  no operation moved by 1% of the time
where the time goes in v17:
time: 226 us; the launch traced here: 222 us
  Pallas kernels  151 us (67%)
  other arithmetic  29.3 us (13%)
  matrix products  23 us (10%)
  local copies, waits for them, and re-layouts  16.8 us (7%)
    pallas_call x4, Pallas kernels, row_allreduce(): pl.pallas_call(partial(allreduce_kernel, inner, outer), out_shape=jax.Sha...  67.9 us
    pallas_call x2, Pallas kernels, gather_pieces(): pl.pallas_call(partial(gather_kernel, rows, cols, blocks, half), out_shap...  54.1 us
    pallas_call x2, Pallas kernels, col_reduce(): pl.pallas_call(partial(reduce_kernel, cols), out_shape=jax.ShapeDtypeStru...  29.3 us
    another operation x6, other arithmetic, lower_inverse(): lax.linalg.triangular_solve(lower, identity, left_side=True, lower=True)  12.9 us
    another operation x3, other arithmetic, body(): lax.linalg.cholesky(normal, symmetrize_input=False)  7.25 us
    dot_general x2, matrix products, operator_terms(): jnp.einsum('caksf,kaef->cse', complex_lhs(near_vector, 1), near_blocks[0]...  5 us
    dot_general x5, matrix products, combine_rows(): return jnp.einsum('st,ctn->csn', matrix, vectors, precision=highest)  4.64 us

profile of v17, /device:TPU:24, one launch (start us, length us, event | category | flops | bytes accessed | tf_op | source)
XLA Modules:
  0.0 221.9 jit_solution(5094866778084185393)
XLA Ops:
  0.7 1.7 convolution_bitcast_fusion.12
  3.0 17.3 %shard_map.95 = f32[16,128]{1,0:T(8,128)} custom-call(f32[16,128]{1,0:T(8,128)} %pad_bitcast_fusion.1.x_ref), custom_call_target="tpu_custom_call" | custom-call | tf_op jit(solution)/shard_map/pallas_call | solution.py:95
  20.4 0.8 reshape.321
  21.2 3.3 %custom-call.16 = f32[36,36]{1,0:T(8,128)S(1)} custom-call(f32[36,36]{1,0:T(8,128)S(1)} %reshape.321), custom_call_target="Cholesky" | custom-call | tf_op jit(solution)/shard_map/cholesky/custom-call.1 | solution.py:463
  25.8 2.8 %custom-call.17 = f32[1,36,36]{1,2,0:T(8,128)S(1)} custom-call(f32[1,36,36]{2,1,0:T(8,128)S(1)} %select_bitcast_fusion.1), custom_call_target="InvertDiagBlocksLowerTriangular" | custom-call | tf_op jit(solution)/shard_map/triangular_solve/custom-call.2 | solution.py:394
  28.8 2.2 fusion.119
  31.7 27.9 %shard_map.96 = (bf16[8,72,128]{2,1,0:T(8,128)(2,1)}, bf16[4,72,1024]{2,1,0:T(8,128)(2,1)}, f32[36,36]{1,0:T(8,128)}, f32[36,36]{1,0:T(8,128)}, f32[2,36,36]{2,1,0:T(8,128)}) custom-call(bf16[72,1024]{1,0:T(8,128)(2,1)} %reshape.322.v_ref, f32[2,36,1024]{2,1,0:T(8,128)} %get-tuple-element.100.one_ref.cur_ref, ...), custom_call_target="tpu_custom_call" | custom-call | tf_op jit(solution)/shard_map/pallas_call | solution.py:230
  59.6 1.9 fusion.24
  63.0 3.6 %fusion.7 = f32[2,36,1024]{2,1,0:T(8,128)S(1)} fusion(bf16[1,2,8,36,128]{4,3,2,1,0:T(8,128)(2,1)S(1)} %get-tuple-element.92, bf16[1,2,8,36,128]{4,3,2,1,0:T(8,128)(2,1)S(1)} %get-tuple-element.91, bf16[1,8,2,1024,128]{4,3,2,1,0:T(8,128)(2,1)} %param.21), kind=kOutput, calls=%fused_computation.9 | convolution fusion | flops 302137344 | bytes 4784128 | tf_op jit(solution)/shard_map/caksf,kaef->cse/dot_general | solution.py:422
  67.7 14.6 %shard_map.97 = f32[72,1024]{1,0:T(8,128)} custom-call(f32[72,1024]{1,0:T(8,128)} %reshape.324.x_ref), custom_call_target="tpu_custom_call" | custom-call | tf_op jit(solution)/shard_map/pallas_call | solution.py:340
  82.3 1.0 reshape.325
  84.8 17.5 %shard_map.98 = f32[48,128]{1,0:T(8,128)} custom-call(f32[48,128]{1,0:T(8,128)} %bitcast.251), custom_call_target="tpu_custom_call" | custom-call | tf_op jit(solution)/shard_map/pallas_call | solution.py:95
  102.2 0.8 fusion.118
  104.7 12.5 %shard_map.99 = f32[16,128]{1,0:T(8,128)} custom-call(f32[16,128]{1,0:T(8,128)} %pad_bitcast_fusion.x_ref), custom_call_target="tpu_custom_call" | custom-call | tf_op jit(solution)/shard_map/pallas_call | solution.py:95
  117.2 0.8 reshape.335
  118.0 3.3 %custom-call.18 = f32[36,36]{1,0:T(8,128)S(1)} custom-call(f32[36,36]{1,0:T(8,128)S(1)} %reshape.335), custom_call_target="Cholesky" | custom-call | tf_op jit(solution)/shard_map/cholesky/custom-call.1 | solution.py:471
  122.6 2.8 %custom-call.19 = f32[1,36,36]{1,2,0:T(8,128)S(1)} custom-call(f32[1,36,36]{2,1,0:T(8,128)S(1)} %select_bitcast_fusion), custom_call_target="InvertDiagBlocksLowerTriangular" | custom-call | tf_op jit(solution)/shard_map/triangular_solve/custom-call.2 | solution.py:394
  125.6 1.1 fusion.120
  127.4 26.2 %shard_map.100 = (bf16[8,72,128]{2,1,0:T(8,128)(2,1)}, bf16[4,72,1024]{2,1,0:T(8,128)(2,1)}, f32[36,36]{1,0:T(8,128)}, f32[36,36]{1,0:T(8,128)}, f32[2,36,36]{2,1,0:T(8,128)}) custom-call(bf16[72,1024]{1,0:T(8,128)(2,1)} %reshape.336.v_ref, f32[2,36,1024]{2,1,0:T(8,128)} %get-tuple-element.100.one_ref.cur_ref, f32[2,36,1024]{2,1,0:T(8,128)} %get-tuple-element.102.cur_ref, ...), custom_call_target="tpu_custom_call" | custom-call | tf_op jit(solution)/shard_map/pallas_call | solution.py:230
  153.7 1.6 fusion.20
  155.7 0.9 copy.47
  156.8 1.4 fusion.10
  159.3 14.7 %shard_map.101 = f32[72,1024]{1,0:T(8,128)} custom-call(f32[72,1024]{1,0:T(8,128)} %reshape.338.x_ref), custom_call_target="tpu_custom_call" | custom-call | tf_op jit(solution)/shard_map/pallas_call | solution.py:340
  174.1 1.0 reshape.339
  177.7 20.6 %shard_map.102 = f32[72,128]{1,0:T(8,128)} custom-call(f32[72,128]{1,0:T(8,128)} %bitcast.248), custom_call_target="tpu_custom_call" | custom-call | tf_op jit(solution)/shard_map/pallas_call | solution.py:95
  198.3 0.9 slice.93
  202.1 6.6 %cholesky.19 = f32[72,72]{1,0:T(8,128)S(1)} custom-call(f32[72,72]{1,0:T(8,128)S(1)} %maximum_maximum_fusion), custom_call_target="Cholesky" | custom-call | tf_op jit(solution)/shard_map/cholesky | solution.py:511
  210.0 5.5 %custom-call.11 = f32[1,72,72]{1,2,0:T(8,128)S(1)} custom-call(f32[1,72,72]{2,1,0:T(8,128)S(1)} %fusion.53), custom_call_target="InvertDiagBlocksLowerTriangular" | custom-call | tf_op jit(solution)/shard_map/triangular_solve | solution.py:394
  215.8 0.8 fusion.75
  216.6 0.8 fusion.77
  218.3 0.8 slice.194
  221.0 0.9 copy.60
  (125 shorter events, 21.9 us)
Async XLA Ops:
  0.6 66.0 %copy-start = (bf16[1,4,2,64,1024]{4,3,2,1,0:T(8,128)(2,1)S(1)}, bf16[1,4,2,64,1024]{4,3,2,1,0:T(8,128)(2,1)}, u32[]{:S(2)}) copy-start(bf16[1,4,2,64,1024]{4,3,2,1,0:T(8,128)(2,1)} %param.22) | copy-start | bytes 3145732
  0.6 61.1 %copy-start.1 = (s32[1,8]{1,0:T(1,128)S(1)}, s32[1,8]{1,0:T(1,128)}, u32[]{:S(2)}) copy-start(s32[1,8]{1,0:T(1,128)} %param.24) | copy-start | bytes 100
  0.7 61.7 %copy-start.15 = (s32[1,4]{1,0:T(1,128)S(1)}, s32[1,4]{1,0:T(1,128)}, u32[]{:S(2)}) copy-start(s32[1,4]{1,0:T(1,128)} %param.25) | copy-start | bytes 52
  59.6 3.1 %copy-start.6 = (bf16[8,72,128]{2,1,0:T(8,128)(2,1)S(1)}, bf16[8,72,128]{2,1,0:T(8,128)(2,1)}, u32[]{:S(2)}) copy-start(bf16[8,72,128]{2,1,0:T(8,128)(2,1)} %get-tuple-element.17) | copy-start | bytes 442372
  62.9 20.4 %copy-start.2 = (f32[2,36,1024]{2,1,0:T(8,128)S(1)}, f32[2,36,1024]{2,1,0:T(8,128)}, u32[]{:S(2)}) copy-start(f32[2,36,1024]{2,1,0:T(8,128)} %get-tuple-element.100.one_ref.cur_ref) | copy-start | bytes 884740
  62.9 20.4 %copy-start.8 = (f32[1024]{0:T(1024)S(1)}, f32[1024]{0:T(1024)}, u32[]{:S(2)}) copy-start(f32[1024]{0:T(1024)} %param.20) | copy-start | bytes 12292
  62.9 20.9 %copy-start.9 = (f32[2,36,36]{2,1,0:T(8,128)S(1)}, f32[2,36,36]{2,1,0:T(8,128)}, u32[]{:S(2)}) copy-start(f32[2,36,36]{2,1,0:T(8,128)} %get-tuple-element.19) | copy-start | bytes 31108
  63.0 21.0 %copy-start.11 = (f32[36,36]{1,0:T(8,128)S(1)}, f32[36,36]{1,0:T(8,128)}, u32[]{:S(2)}) copy-start(f32[36,36]{1,0:T(8,128)} %get-tuple-element.20) | copy-start | bytes 15556
  66.6 87.1 %copy-start.5 = (bf16[1,4,2,64,1024]{4,3,2,1,0:T(8,128)(2,1)S(1)}, bf16[1,4,2,64,1024]{4,3,2,1,0:T(8,128)(2,1)}, u32[]{:S(2)}) copy-start(bf16[1,4,2,64,1024]{4,3,2,1,0:T(8,128)(2,1)} %param.23) | copy-start | bytes 3145732
  153.6 3.1 %copy-start.14 = (bf16[1,8,2,1024,128]{4,3,2,1,0:T(8,128)(2,1)S(1)}, bf16[1,8,2,1024,128]{4,3,2,1,0:T(8,128)(2,1)}, u32[]{:S(2)}) copy-start(bf16[1,8,2,1024,128]{4,3,2,1,0:T(8,128)(2,1)} %param.21) | copy-start | bytes 12582916
  156.8 18.3 %copy-start.4 = (f32[2,36,1024]{2,1,0:T(8,128)S(1)}, f32[2,36,1024]{2,1,0:T(8,128)}, u32[]{:S(2)}) copy-start(f32[2,36,1024]{2,1,0:T(8,128)} %get-tuple-element.102.cur_ref) | copy-start | bytes 884740
  156.8 19.3 %copy-start.3 = (f32[2,36,1024]{2,1,0:T(8,128)S(1)}, f32[2,36,1024]{2,1,0:T(8,128)}, u32[]{:S(2)}) copy-start(f32[2,36,1024]{2,1,0:T(8,128)} %get-tuple-element.100.one_ref.cur_ref) | copy-start | bytes 884740
  158.2 18.5 %copy-start.10 = (f32[2,36,36]{2,1,0:T(8,128)S(1)}, f32[2,36,36]{2,1,0:T(8,128)}, u32[]{:S(2)}) copy-start(f32[2,36,36]{2,1,0:T(8,128)} %get-tuple-element.25) | copy-start | bytes 31108
  158.2 18.6 %copy-start.13 = (f32[36,36]{1,0:T(8,128)S(1)}, f32[36,36]{1,0:T(8,128)}, u32[]{:S(2)}) copy-start(f32[36,36]{1,0:T(8,128)} %get-tuple-element.23) | copy-start | bytes 15556
  158.2 18.7 %copy-start.12 = (f32[36,36]{1,0:T(8,128)S(1)}, f32[36,36]{1,0:T(8,128)}, u32[]{:S(2)}) copy-start(f32[36,36]{1,0:T(8,128)} %get-tuple-element.24) | copy-start | bytes 15556
  158.2 59.7 %copy-start.7 = (f32[48,128]{1,0:T(8,128)S(1)}, f32[48,128]{1,0:T(8,128)}, u32[]{:S(2)}) copy-start(f32[48,128]{1,0:T(8,128)} %shard_map.98) | copy-start | bytes 73732

commit v18 on v17

--- a/solution.py
+++ b/solution.py
@@ -514,8 +514,11 @@
     second_weights = weights[:, fields:]
     solution = combine_rows(first_weights, basis_one) + combine_rows(second_weights, basis_two)
     coefficients = jnp.einsum(
-        "cmt,st->cms", harmonics_one, first_weights, precision=highest
-    ) + jnp.einsum("cmt,st->cms", harmonics_two, second_weights, precision=highest)
+        "cmt,st->cms",
+        jnp.concatenate([harmonics_one, harmonics_two], axis=2),
+        weights,
+        precision=highest,
+    )
     return (solution, coefficients)
 
 

time: 226 us -> 225 us (level)
  no operation moved by 1% of the time
where the time goes in v18:
time: 225 us; the launch traced here: 222 us
  Pallas kernels  151 us (67%)
  other arithmetic  29.3 us (13%)
  matrix products  22.8 us (10%)
  local copies, waits for them, and re-layouts  16.8 us (7%)
    pallas_call x4, Pallas kernels, row_allreduce(): pl.pallas_call(partial(allreduce_kernel, inner, outer), out_shape=jax.Sha...  67.9 us
    pallas_call x2, Pallas kernels, gather_pieces(): pl.pallas_call(partial(gather_kernel, rows, cols, blocks, half), out_shap...  54.1 us
    pallas_call x2, Pallas kernels, col_reduce(): pl.pallas_call(partial(reduce_kernel, cols), out_shape=jax.ShapeDtypeStru...  29.3 us
    another operation x6, other arithmetic, lower_inverse(): lax.linalg.triangular_solve(lower, identity, left_side=True, lower=True)  12.9 us
    another operation x3, other arithmetic, body(): lax.linalg.cholesky(normal, symmetrize_input=False)  7.25 us
    dot_general x2, matrix products, operator_terms(): jnp.einsum('caksf,kaef->cse', complex_lhs(near_vector, 1), near_blocks[0]...  5 us
    dot_general x5, matrix products, combine_rows(): return jnp.einsum('st,ctn->csn', matrix, vectors, precision=highest)  4.64 us

profile of v18, /device:TPU:24, one launch (start us, length us, event | category | flops | bytes accessed | tf_op | source)
XLA Modules:
  0.0 221.8 jit_solution(9063187636889901330)
XLA Ops:
  0.7 1.7 convolution_bitcast_fusion.12
  3.0 17.3 %shard_map.95 = f32[16,128]{1,0:T(8,128)} custom-call(f32[16,128]{1,0:T(8,128)} %pad_bitcast_fusion.1.x_ref), custom_call_target="tpu_custom_call" | custom-call | tf_op jit(solution)/shard_map/pallas_call | solution.py:95
  20.4 0.8 reshape.321
  21.2 3.3 %custom-call.16 = f32[36,36]{1,0:T(8,128)S(1)} custom-call(f32[36,36]{1,0:T(8,128)S(1)} %reshape.321), custom_call_target="Cholesky" | custom-call | tf_op jit(solution)/shard_map/cholesky/custom-call.1 | solution.py:463
  25.8 2.8 %custom-call.17 = f32[1,36,36]{1,2,0:T(8,128)S(1)} custom-call(f32[1,36,36]{2,1,0:T(8,128)S(1)} %select_bitcast_fusion.1), custom_call_target="InvertDiagBlocksLowerTriangular" | custom-call | tf_op jit(solution)/shard_map/triangular_solve/custom-call.2 | solution.py:394
  28.8 2.2 fusion.124
  31.7 27.9 %shard_map.96 = (bf16[8,72,128]{2,1,0:T(8,128)(2,1)}, bf16[4,72,1024]{2,1,0:T(8,128)(2,1)}, f32[36,36]{1,0:T(8,128)}, f32[36,36]{1,0:T(8,128)}, f32[2,36,36]{2,1,0:T(8,128)}) custom-call(bf16[72,1024]{1,0:T(8,128)(2,1)} %reshape.322.v_ref, f32[2,36,1024]{2,1,0:T(8,128)} %get-tuple-element.100.one_ref.cur_ref, ...), custom_call_target="tpu_custom_call" | custom-call | tf_op jit(solution)/shard_map/pallas_call | solution.py:230
  59.6 1.9 fusion.24
  63.0 3.6 %fusion.7 = f32[2,36,1024]{2,1,0:T(8,128)S(1)} fusion(bf16[1,2,8,36,128]{4,3,2,1,0:T(8,128)(2,1)S(1)} %get-tuple-element.92, bf16[1,2,8,36,128]{4,3,2,1,0:T(8,128)(2,1)S(1)} %get-tuple-element.91, bf16[1,8,2,1024,128]{4,3,2,1,0:T(8,128)(2,1)} %param.21), kind=kOutput, calls=%fused_computation.9 | convolution fusion | flops 302137344 | bytes 4784128 | tf_op jit(solution)/shard_map/caksf,kaef->cse/dot_general | solution.py:422
  67.7 14.6 %shard_map.97 = f32[72,1024]{1,0:T(8,128)} custom-call(f32[72,1024]{1,0:T(8,128)} %reshape.324.x_ref), custom_call_target="tpu_custom_call" | custom-call | tf_op jit(solution)/shard_map/pallas_call | solution.py:340
  82.3 1.0 reshape.325
  84.8 17.5 %shard_map.98 = f32[48,128]{1,0:T(8,128)} custom-call(f32[48,128]{1,0:T(8,128)} %bitcast.253), custom_call_target="tpu_custom_call" | custom-call | tf_op jit(solution)/shard_map/pallas_call | solution.py:95
  102.2 0.8 fusion.123
  104.7 12.5 %shard_map.99 = f32[16,128]{1,0:T(8,128)} custom-call(f32[16,128]{1,0:T(8,128)} %pad_bitcast_fusion.x_ref), custom_call_target="tpu_custom_call" | custom-call | tf_op jit(solution)/shard_map/pallas_call | solution.py:95
  117.2 0.8 reshape.335
  118.0 3.3 %custom-call.18 = f32[36,36]{1,0:T(8,128)S(1)} custom-call(f32[36,36]{1,0:T(8,128)S(1)} %reshape.335), custom_call_target="Cholesky" | custom-call | tf_op jit(solution)/shard_map/cholesky/custom-call.1 | solution.py:471
  122.6 2.8 %custom-call.19 = f32[1,36,36]{1,2,0:T(8,128)S(1)} custom-call(f32[1,36,36]{2,1,0:T(8,128)S(1)} %select_bitcast_fusion), custom_call_target="InvertDiagBlocksLowerTriangular" | custom-call | tf_op jit(solution)/shard_map/triangular_solve/custom-call.2 | solution.py:394
  125.6 1.1 fusion.125
  127.4 26.2 %shard_map.100 = (bf16[8,72,128]{2,1,0:T(8,128)(2,1)}, bf16[4,72,1024]{2,1,0:T(8,128)(2,1)}, f32[36,36]{1,0:T(8,128)}, f32[36,36]{1,0:T(8,128)}, f32[2,36,36]{2,1,0:T(8,128)}) custom-call(bf16[72,1024]{1,0:T(8,128)(2,1)} %reshape.336.v_ref, f32[2,36,1024]{2,1,0:T(8,128)} %get-tuple-element.100.one_ref.cur_ref, f32[2,36,1024]{2,1,0:T(8,128)} %get-tuple-element.102.cur_ref, ...), custom_call_target="tpu_custom_call" | custom-call | tf_op jit(solution)/shard_map/pallas_call | solution.py:230
  153.7 1.6 fusion.20
  155.7 0.9 copy.47
  156.8 1.4 fusion.10
  159.3 14.7 %shard_map.101 = f32[72,1024]{1,0:T(8,128)} custom-call(f32[72,1024]{1,0:T(8,128)} %reshape.338.x_ref), custom_call_target="tpu_custom_call" | custom-call | tf_op jit(solution)/shard_map/pallas_call | solution.py:340
  174.1 1.0 reshape.339
  177.7 20.6 %shard_map.102 = f32[72,128]{1,0:T(8,128)} custom-call(f32[72,128]{1,0:T(8,128)} %bitcast.250), custom_call_target="tpu_custom_call" | custom-call | tf_op jit(solution)/shard_map/pallas_call | solution.py:95
  198.3 0.9 slice.93
  202.1 6.6 %cholesky.19 = f32[72,72]{1,0:T(8,128)S(1)} custom-call(f32[72,72]{1,0:T(8,128)S(1)} %maximum_maximum_fusion), custom_call_target="Cholesky" | custom-call | tf_op jit(solution)/shard_map/cholesky | solution.py:511
  210.0 5.5 %custom-call.11 = f32[1,72,72]{1,2,0:T(8,128)S(1)} custom-call(f32[1,72,72]{2,1,0:T(8,128)S(1)} %fusion.57), custom_call_target="InvertDiagBlocksLowerTriangular" | custom-call | tf_op jit(solution)/shard_map/triangular_solve | solution.py:394
  215.8 0.8 fusion.79
  216.6 0.8 fusion.81
  217.9 0.8 slice.194
  220.8 0.9 copy.60
  (124 shorter events, 21.7 us)
Async XLA Ops:
  0.6 66.0 %copy-start = (bf16[1,4,2,64,1024]{4,3,2,1,0:T(8,128)(2,1)S(1)}, bf16[1,4,2,64,1024]{4,3,2,1,0:T(8,128)(2,1)}, u32[]{:S(2)}) copy-start(bf16[1,4,2,64,1024]{4,3,2,1,0:T(8,128)(2,1)} %param.22) | copy-start | bytes 3145732
  0.6 61.1 %copy-start.1 = (s32[1,8]{1,0:T(1,128)S(1)}, s32[1,8]{1,0:T(1,128)}, u32[]{:S(2)}) copy-start(s32[1,8]{1,0:T(1,128)} %param.24) | copy-start | bytes 100
  0.7 61.7 %copy-start.15 = (s32[1,4]{1,0:T(1,128)S(1)}, s32[1,4]{1,0:T(1,128)}, u32[]{:S(2)}) copy-start(s32[1,4]{1,0:T(1,128)} %param.25) | copy-start | bytes 52
  59.6 3.1 %copy-start.6 = (bf16[8,72,128]{2,1,0:T(8,128)(2,1)S(1)}, bf16[8,72,128]{2,1,0:T(8,128)(2,1)}, u32[]{:S(2)}) copy-start(bf16[8,72,128]{2,1,0:T(8,128)(2,1)} %get-tuple-element.17) | copy-start | bytes 442372
  62.9 20.4 %copy-start.2 = (f32[2,36,1024]{2,1,0:T(8,128)S(1)}, f32[2,36,1024]{2,1,0:T(8,128)}, u32[]{:S(2)}) copy-start(f32[2,36,1024]{2,1,0:T(8,128)} %get-tuple-element.100.one_ref.cur_ref) | copy-start | bytes 884740
  62.9 20.4 %copy-start.8 = (f32[1024]{0:T(1024)S(1)}, f32[1024]{0:T(1024)}, u32[]{:S(2)}) copy-start(f32[1024]{0:T(1024)} %param.20) | copy-start | bytes 12292
  62.9 20.9 %copy-start.9 = (f32[2,36,36]{2,1,0:T(8,128)S(1)}, f32[2,36,36]{2,1,0:T(8,128)}, u32[]{:S(2)}) copy-start(f32[2,36,36]{2,1,0:T(8,128)} %get-tuple-element.19) | copy-start | bytes 31108
  63.0 21.0 %copy-start.11 = (f32[36,36]{1,0:T(8,128)S(1)}, f32[36,36]{1,0:T(8,128)}, u32[]{:S(2)}) copy-start(f32[36,36]{1,0:T(8,128)} %get-tuple-element.20) | copy-start | bytes 15556
  66.6 87.1 %copy-start.5 = (bf16[1,4,2,64,1024]{4,3,2,1,0:T(8,128)(2,1)S(1)}, bf16[1,4,2,64,1024]{4,3,2,1,0:T(8,128)(2,1)}, u32[]{:S(2)}) copy-start(bf16[1,4,2,64,1024]{4,3,2,1,0:T(8,128)(2,1)} %param.23) | copy-start | bytes 3145732
  153.6 3.1 %copy-start.14 = (bf16[1,8,2,1024,128]{4,3,2,1,0:T(8,128)(2,1)S(1)}, bf16[1,8,2,1024,128]{4,3,2,1,0:T(8,128)(2,1)}, u32[]{:S(2)}) copy-start(bf16[1,8,2,1024,128]{4,3,2,1,0:T(8,128)(2,1)} %param.21) | copy-start | bytes 12582916
  156.8 18.3 %copy-start.4 = (f32[2,36,1024]{2,1,0:T(8,128)S(1)}, f32[2,36,1024]{2,1,0:T(8,128)}, u32[]{:S(2)}) copy-start(f32[2,36,1024]{2,1,0:T(8,128)} %get-tuple-element.102.cur_ref) | copy-start | bytes 884740
  156.8 19.3 %copy-start.3 = (f32[2,36,1024]{2,1,0:T(8,128)S(1)}, f32[2,36,1024]{2,1,0:T(8,128)}, u32[]{:S(2)}) copy-start(f32[2,36,1024]{2,1,0:T(8,128)} %get-tuple-element.100.one_ref.cur_ref) | copy-start | bytes 884740
  158.2 18.5 %copy-start.10 = (f32[2,36,36]{2,1,0:T(8,128)S(1)}, f32[2,36,36]{2,1,0:T(8,128)}, u32[]{:S(2)}) copy-start(f32[2,36,36]{2,1,0:T(8,128)} %get-tuple-element.25) | copy-start | bytes 31108
  158.2 18.6 %copy-start.13 = (f32[36,36]{1,0:T(8,128)S(1)}, f32[36,36]{1,0:T(8,128)}, u32[]{:S(2)}) copy-start(f32[36,36]{1,0:T(8,128)} %get-tuple-element.23) | copy-start | bytes 15556
  158.2 18.7 %copy-start.12 = (f32[36,36]{1,0:T(8,128)S(1)}, f32[36,36]{1,0:T(8,128)}, u32[]{:S(2)}) copy-start(f32[36,36]{1,0:T(8,128)} %get-tuple-element.24) | copy-start | bytes 15556
  158.2 60.6 %copy-start.7 = (f32[48,128]{1,0:T(8,128)S(1)}, f32[48,128]{1,0:T(8,128)}, u32[]{:S(2)}) copy-start(f32[48,128]{1,0:T(8,128)} %shard_map.98) | copy-start | bytes 73732
